TPU v7x, 32 devices: a whole 2x2x4 slice. The times are simulated.
32 devices in a mesh: dp: 4 (over z), seq: 4 (over x, core), fsdp: 2 (over y).
Axes of the slice: x: 2, y: 2, z: 4, core: 2. Of those that a mesh axis runs over, the one named last changes fastest.
Arguments:
- tokens: bfloat16 [4, 2560, 1024], P('dp', ('seq', 'fsdp')), may hold values from -6 to 6
- cotangent: bfloat16 [4, 2560, 1024], P('dp', ('seq', 'fsdp')), may hold values from -6 to 6
- lengths: int32 [4], P('dp'), may hold values from 640 to 2560, as said below
- order: int32 [16], replicated, may hold values from 0 to 15, each once
- routes: int32 [4, 2560, 8], P('dp', ('seq', 'fsdp')), may hold values from 0 to 15, all different within a row; in each aligned block of 320 rows (0 to 319, 320 to 639, ..., all dimensions but the last counted through in order) at most 256 rows name the same one
- norm1: bfloat16 [1024], P('fsdp'), may hold values from 0.5 to 1.5
- query_key_value_weight: bfloat16 [1024, 2048], P('fsdp'), may hold values from -0.25 to 0.25
- w_out: bfloat16 [1024, 1024], P('fsdp'), may hold values from -1.1953125 to 1.1953125
- norm2: bfloat16 [1024], P('fsdp'), may hold values from 0.5 to 1.5
- router: bfloat16 [1024, 16], P('fsdp'), may hold values from -0.09375 to 0.09375
- w_gate: bfloat16 [16, 1024, 512], P('fsdp'), may hold values from -0.1875 to 0.1875
- w_up: bfloat16 [16, 1024, 512], P('fsdp'), may hold values from -0.1875 to 0.1875
- w_down: bfloat16 [16, 512, 1024], P('fsdp'), may hold values from -1 to 1
Outputs:
- layer_out: bfloat16 [4, 2560, 1024], P('dp', ('seq', 'fsdp'))
- d_tokens: float32 [4, 2560, 1024], P('dp', ('seq', 'fsdp'))
- grad_norm1: float32 [1024], P('fsdp')
- grad_w_qkv: float32 [1024, 2048], P('fsdp')
- grad_w_out: float32 [1024, 1024], P('fsdp')
- grad_norm2: float32 [1024], P('fsdp')
- grad_router: float32 [1024, 16], P('fsdp')
- grad_w_gate: float32 [16, 1024, 512], P('fsdp')
- grad_w_up: float32 [16, 1024, 512], P('fsdp')
- grad_w_down: float32 [16, 512, 1024], P('fsdp')
Inputs may be any that keep to these rules, and one draw needn't show every extreme that they name: `lengths`: one slot has exactly 2560 valid tokens and another exactly 640. `routes`: each token names 8 different experts; in each aligned block of 320 rows (the rows of one device) no expert is named by more than 256 rows, a bound that some block reaches. `order`: each span index appears once.
All inputs are finite; a program needn't handle non-finite values.
Results may differ from a plain program's by a relative error of at most 0.023.
Values may be sent and summed in bfloat16 or wider, within the bound.
A program may use at most 384 MiB of HBM per device.

v0:
```python
import math

import jax
import jax.numpy as jnp
from jax import lax
from jax.sharding import PartitionSpec as P

QUERY_HEADS = 16
KEY_VALUE_HEADS = 8
HEAD_WIDTH = 64
CAP = 256


epsilon = 1e-06
rope_base = 10000.0


def rope_tables(positions, head_size):
    half_size = head_size // 2
    freqs = jnp.exp(
        jnp.arange(half_size, dtype=jnp.float32) * (-2.0 * math.log(rope_base) / head_size)
    )
    angles = positions.astype(jnp.float32)[:, None] * freqs[None, :]
    angles = jnp.concatenate([angles, angles], axis=1)
    return (jnp.cos(angles), jnp.sin(angles))


def rotate(value_rows):
    half_size = value_rows.shape[-1] // 2
    return jnp.concatenate([-value_rows[..., half_size:], value_rows[..., :half_size]], axis=-1)


def rotate_back(value_rows):
    half_size = value_rows.shape[-1] // 2
    return jnp.concatenate([value_rows[..., half_size:], -value_rows[..., :half_size]], axis=-1)


def apply_rope(value_rows, cosine_table, sine_values):
    return value_rows * cosine_table[:, None, :] + rotate(value_rows) * sine_values[:, None, :]


def undo_rope(grads, cosine_table, sine_values):
    return grads * cosine_table[:, None, :] + rotate_back(grads * sine_values[:, None, :])


def rms_forward(inputs, gain):
    factor = lax.rsqrt(jnp.mean(inputs * inputs, axis=-1, keepdims=True) + epsilon)
    normed = inputs * factor
    return (normed, factor, normed * gain)


def rms_backward(upstream, normed, factor, gain):
    d_normed = upstream * gain
    d_gain = jnp.sum(upstream * normed, axis=0)
    d_inputs = factor * (d_normed - normed * jnp.mean(d_normed * normed, axis=-1, keepdims=True))
    return (d_inputs, d_gain)


def outer_sum(left_side, right_side):
    return lax.dot_general(
        left_side, right_side, (((0,), (0,)), ((), ())), preferred_element_type=jnp.float32
    )


def times_transpose(left_side, right_side):
    return lax.dot_general(
        left_side, right_side, (((1,), (1,)), ((), ())), preferred_element_type=jnp.float32
    )


def slot_tables(chosen, block_rows, capacity):
    row_count, expert_count = chosen.shape
    block_count = row_count // block_rows
    ranks = jnp.cumsum(chosen.reshape(block_count, block_rows, expert_count), axis=1).reshape(
        row_count, expert_count
    )
    row_ids = jnp.arange(row_count, dtype=jnp.int32)
    block_base = row_ids // block_rows * capacity
    width = block_count * capacity
    slots = jnp.where(chosen > 0, block_base[:, None] + ranks.astype(jnp.int32) - 1, width)
    expert_ids = jnp.broadcast_to(
        jnp.arange(expert_count, dtype=jnp.int32)[None, :], (row_count, expert_count)
    )
    row_grid = jnp.broadcast_to(row_ids[:, None], (row_count, expert_count))
    index_table = (
        jnp.zeros((expert_count, width), jnp.int32).at[expert_ids, slots].set(row_grid, mode="drop")
    )
    live_table = (
        jnp.zeros((expert_count, width), jnp.float32).at[expert_ids, slots].set(1.0, mode="drop")
    )
    return (index_table, live_table)


def expert_pass(
    inputs, gate_cols, upstream, gate_weights, up_weights, down_weights, index_table, live_table
):
    row_count = inputs.shape[0]
    zero_rows = jnp.zeros((row_count, down_weights.shape[2]), jnp.float32)

    def expert_step(carry, expert_item):
        total, d_inputs = carry
        weight_gate, weight_up, weight_down, column, row_index, live = expert_item
        picked = jnp.take(inputs, row_index, axis=0)
        picked_up = jnp.take(upstream, row_index, axis=0)
        weight_col = (jnp.take(column, row_index, axis=0).astype(jnp.float32) * live)[:, None]
        gate_pre = jnp.dot(picked, weight_gate, preferred_element_type=jnp.float32)
        up_pre = jnp.dot(picked, weight_up, preferred_element_type=jnp.float32)
        sigmoid = jax.nn.sigmoid(gate_pre)
        activated = (gate_pre * sigmoid * up_pre).astype(jnp.bfloat16)
        expert_out = jnp.dot(activated, weight_down, preferred_element_type=jnp.float32)
        total = total.at[row_index].add(weight_col * expert_out)
        column_grad = live * jnp.sum(expert_out * picked_up.astype(jnp.float32), axis=1)
        d_column = jnp.zeros((row_count,), jnp.float32).at[row_index].add(column_grad)
        d_expert = (weight_col * picked_up.astype(jnp.float32)).astype(jnp.bfloat16)
        d_down = outer_sum(activated, d_expert)
        d_act = times_transpose(d_expert, weight_down)
        d_gate = (d_act * up_pre * sigmoid * (1.0 + gate_pre * (1.0 - sigmoid))).astype(
            jnp.bfloat16
        )
        d_up = (d_act * gate_pre * sigmoid).astype(jnp.bfloat16)
        d_picked = times_transpose(d_gate, weight_gate) + times_transpose(d_up, weight_up)
        d_inputs = d_inputs.at[row_index].add(d_picked)
        return (
            (total, d_inputs),
            (d_column, outer_sum(picked, d_gate), outer_sum(picked, d_up), d_down),
        )

    (total, d_inputs), (d_columns, grad_gate, grad_up, grad_down) = lax.scan(
        expert_step,
        (zero_rows, zero_rows),
        (gate_weights, up_weights, down_weights, gate_cols.T, index_table, live_table),
    )
    return (total, d_inputs, d_columns.T, grad_gate, grad_up, grad_down)


def local(
    tokens,
    cotangent,
    lengths,
    order,
    routes,
    norm1,
    query_key_value_weight,
    w_out,
    norm2,
    router,
    w_gate,
    w_up,
    w_down,
):
    seq_devices = lax.axis_size("seq")
    fsdp_devices = lax.axis_size("fsdp")
    seq_index = lax.axis_index("seq")
    fsdp_index = lax.axis_index("fsdp")
    token_rows = tokens.shape[1]
    half_rows = token_rows // 2
    seq_limit = lengths[0]
    span_table = order.reshape(seq_devices, fsdp_devices, 2)

    def span_positions(span_ids):
        return (
            span_ids[:, None] * half_rows + jnp.arange(half_rows, dtype=jnp.int32)[None, :]
        ).reshape(-1)

    own_spans = lax.dynamic_index_in_dim(
        lax.dynamic_index_in_dim(span_table, seq_index, 0, keepdims=False),
        fsdp_index,
        0,
        keepdims=False,
    )
    own_pos = span_positions(own_spans)
    query_pos = span_positions(
        lax.dynamic_index_in_dim(span_table, fsdp_index, 1, keepdims=False).reshape(-1)
    )
    key_pos = span_positions(jnp.transpose(span_table, (1, 0, 2)).reshape(-1))
    key_valid = key_pos < seq_limit
    valid_rows = (own_pos < seq_limit).astype(jnp.float32)[:, None]
    gain_one, qkv_full, out_full, gain_two, route_full = (
        lax.all_gather(norm1, "fsdp", axis=0, tiled=True),
        lax.all_gather(query_key_value_weight, "fsdp", axis=0, tiled=True),
        lax.all_gather(w_out, "fsdp", axis=0, tiled=True),
        lax.all_gather(norm2, "fsdp", axis=0, tiled=True),
        lax.all_gather(router, "fsdp", axis=0, tiled=True),
    )
    gain_one = gain_one.astype(jnp.float32)
    gain_two = gain_two.astype(jnp.float32)
    inputs = tokens[0].astype(jnp.float32)
    normed_one, factor_one, scaled_one = rms_forward(inputs, gain_one)
    hidden_one = scaled_one.astype(jnp.bfloat16)
    projected_rows = jnp.dot(hidden_one, qkv_full, preferred_element_type=jnp.float32)
    query_width = QUERY_HEADS * HEAD_WIDTH
    key_value_width = KEY_VALUE_HEADS * HEAD_WIDTH
    cosine_table, sine_values = rope_tables(own_pos, HEAD_WIDTH)
    queries = apply_rope(
        projected_rows[:, :query_width].reshape(token_rows, QUERY_HEADS, HEAD_WIDTH),
        cosine_table,
        sine_values,
    )
    queries = queries.astype(jnp.bfloat16).reshape(token_rows, query_width)
    keys_rot = apply_rope(
        projected_rows[:, query_width : query_width + key_value_width].reshape(
            token_rows, KEY_VALUE_HEADS, HEAD_WIDTH
        ),
        cosine_table,
        sine_values,
    )
    keys_rot = keys_rot.astype(jnp.bfloat16).reshape(token_rows, key_value_width)
    value_rows = projected_rows[:, query_width + key_value_width :].astype(jnp.bfloat16)
    head_queries, head_keys, head_values = (
        lax.all_to_all(queries, "seq", split_axis=1, concat_axis=0, tiled=True),
        lax.all_to_all(keys_rot, "seq", split_axis=1, concat_axis=0, tiled=True),
        lax.all_to_all(value_rows, "seq", split_axis=1, concat_axis=0, tiled=True),
    )
    all_keys, all_values = (
        lax.all_gather(head_keys, "fsdp", axis=0, tiled=True),
        lax.all_gather(head_values, "fsdp", axis=0, tiled=True),
    )
    local_heads = head_queries.shape[1] // HEAD_WIDTH
    local_kv = head_keys.shape[1] // HEAD_WIDTH
    group_size = local_heads // local_kv
    query_rows = head_queries.shape[0]
    block_rows = math.gcd(query_rows, max(1, 512 // local_heads))
    blocks = query_rows // block_rows
    key_heads = all_keys.reshape(-1, local_kv, HEAD_WIDTH)
    value_heads = all_values.reshape(-1, local_kv, HEAD_WIDTH)
    score_scale = HEAD_WIDTH ** (-0.5)

    def block_scores(query_block, positions):
        raw_scores = (
            jnp.einsum("qgjd,kgd->gjqk", query_block, key_heads, preferred_element_type=jnp.float32)
            * score_scale
        )
        allowed = key_valid[None, :] & (key_pos[None, :] <= positions[:, None])
        return jnp.where(allowed[None, None], raw_scores, -1e30)

    query_blocks = head_queries.reshape(blocks, block_rows, local_kv, group_size, HEAD_WIDTH)
    pos_blocks = query_pos.reshape(blocks, block_rows)

    def forward_block(block_item):
        query_block, positions = block_item
        scores = block_scores(query_block, positions)
        top_score = jnp.max(scores, axis=-1, keepdims=True)
        raised = jnp.exp(scores - top_score)
        totals = jnp.sum(raised, axis=-1, keepdims=True)
        softmax_low = (raised / totals).astype(jnp.bfloat16)
        attended = jnp.einsum(
            "gjqk,kgd->qgjd", softmax_low, value_heads, preferred_element_type=jnp.float32
        )
        return (attended.astype(jnp.bfloat16), top_score[..., 0] + jnp.log(totals[..., 0]))

    attended, log_totals = lax.map(forward_block, (query_blocks, pos_blocks))
    head_out = attended.reshape(query_rows, local_heads * HEAD_WIDTH)
    token_out = lax.all_to_all(head_out, "seq", split_axis=0, concat_axis=1, tiled=True)
    middle = inputs + jnp.dot(token_out, out_full, preferred_element_type=jnp.float32)
    normed_two, factor_two, scaled_two = rms_forward(middle, gain_two)
    hidden_two = scaled_two.astype(jnp.bfloat16)
    logits = jnp.dot(hidden_two, route_full, preferred_element_type=jnp.float32)
    expert_total = route_full.shape[1]
    chosen = jnp.sum(
        (routes[0][:, :, None] == jnp.arange(expert_total, dtype=jnp.int32)[None, None, :]).astype(
            jnp.float32
        ),
        axis=1,
    )
    picked_max = jnp.max(jnp.where(chosen > 0, logits, -1e30), axis=-1, keepdims=True)
    raised_gates = jnp.where(chosen > 0, jnp.exp(logits - picked_max), 0.0)
    gates = raised_gates / jnp.sum(raised_gates, axis=-1, keepdims=True)
    gates_low = gates.astype(jnp.bfloat16)
    masked_cot = cotangent[0].astype(jnp.float32) * valid_rows
    branch_grad = masked_cot.astype(jnp.bfloat16)
    gate_full, up_full, down_full = (
        lax.all_gather(w_gate, "fsdp", axis=0, tiled=True),
        lax.all_gather(w_up, "fsdp", axis=0, tiled=True),
        lax.all_gather(w_down, "fsdp", axis=0, tiled=True),
    )
    index_table, live_table = slot_tables(chosen, token_rows, CAP)
    moe_out, d_hidden, d_gates, grad_gate, grad_up, grad_down = expert_pass(
        hidden_two, gates_low, branch_grad, gate_full, up_full, down_full, index_table, live_table
    )
    grad_gate, grad_up, grad_down = (
        lax.psum_scatter(
            grad_gate.astype(jnp.bfloat16), "fsdp", scatter_dimension=0, tiled=True
        ).astype(jnp.float32),
        lax.psum_scatter(
            grad_up.astype(jnp.bfloat16), "fsdp", scatter_dimension=0, tiled=True
        ).astype(jnp.float32),
        lax.psum_scatter(
            grad_down.astype(jnp.bfloat16), "fsdp", scatter_dimension=0, tiled=True
        ).astype(jnp.float32),
    )
    d_logits = (gates * (d_gates - jnp.sum(gates * d_gates, axis=-1, keepdims=True))).astype(
        jnp.bfloat16
    )
    grad_router = outer_sum(hidden_two, d_logits)
    d_hidden = d_hidden + times_transpose(d_logits, route_full)
    d_middle, grad_gain_two = rms_backward(d_hidden, normed_two, factor_two, gain_two)
    d_middle = d_middle + masked_cot
    d_attn = d_middle.astype(jnp.bfloat16)
    grad_out = outer_sum(token_out, d_attn)
    d_token_out = times_transpose(d_attn, out_full).astype(jnp.bfloat16)
    d_head_out = lax.all_to_all(d_token_out, "seq", split_axis=1, concat_axis=0, tiled=True)
    d_blocks = d_head_out.reshape(blocks, block_rows, local_kv, group_size, HEAD_WIDTH)

    def backward_block(carry, block_item):
        d_keys, d_values = carry
        query_block, positions, log_total, d_block = block_item
        scores = block_scores(query_block, positions)
        weights_now = jnp.exp(scores - log_total[..., None])
        d_weights = jnp.einsum(
            "qgjd,kgd->gjqk", d_block, value_heads, preferred_element_type=jnp.float32
        )
        inner = jnp.sum(weights_now * d_weights, axis=-1, keepdims=True)
        d_scores = (weights_now * (d_weights - inner)).astype(jnp.bfloat16)
        d_query = (
            jnp.einsum("gjqk,kgd->qgjd", d_scores, key_heads, preferred_element_type=jnp.float32)
            * score_scale
        )
        d_keys = (
            d_keys
            + jnp.einsum(
                "gjqk,qgjd->kgd", d_scores, query_block, preferred_element_type=jnp.float32
            )
            * score_scale
        )
        d_values = d_values + jnp.einsum(
            "gjqk,qgjd->kgd",
            weights_now.astype(jnp.bfloat16),
            d_block,
            preferred_element_type=jnp.float32,
        )
        return ((d_keys, d_values), d_query.astype(jnp.bfloat16))

    zero_heads = jnp.zeros(key_heads.shape, jnp.float32)
    (d_keys, d_values), d_queries = lax.scan(
        backward_block, (zero_heads, zero_heads), (query_blocks, pos_blocks, log_totals, d_blocks)
    )
    key_count = key_heads.shape[0]
    own_dk, own_dv = (
        lax.psum_scatter(
            d_keys.reshape(key_count, local_kv * HEAD_WIDTH).astype(jnp.bfloat16),
            "fsdp",
            scatter_dimension=0,
            tiled=True,
        ).astype(jnp.float32),
        lax.psum_scatter(
            d_values.reshape(key_count, local_kv * HEAD_WIDTH).astype(jnp.bfloat16),
            "fsdp",
            scatter_dimension=0,
            tiled=True,
        ).astype(jnp.float32),
    )
    back_queries, keys_backward, back_values = (
        lax.all_to_all(
            d_queries.reshape(query_rows, local_heads * HEAD_WIDTH),
            "seq",
            split_axis=0,
            concat_axis=1,
            tiled=True,
        ),
        lax.all_to_all(own_dk.astype(jnp.bfloat16), "seq", split_axis=0, concat_axis=1, tiled=True),
        lax.all_to_all(own_dv.astype(jnp.bfloat16), "seq", split_axis=0, concat_axis=1, tiled=True),
    )
    d_projected = jnp.concatenate(
        [
            undo_rope(
                back_queries.astype(jnp.float32).reshape(token_rows, QUERY_HEADS, HEAD_WIDTH),
                cosine_table,
                sine_values,
            ).reshape(token_rows, query_width),
            undo_rope(
                keys_backward.astype(jnp.float32).reshape(token_rows, KEY_VALUE_HEADS, HEAD_WIDTH),
                cosine_table,
                sine_values,
            ).reshape(token_rows, key_value_width),
            back_values.astype(jnp.float32),
        ],
        axis=1,
    ).astype(jnp.bfloat16)
    grad_qkv = outer_sum(hidden_one, d_projected)
    d_hidden_one = times_transpose(d_projected, qkv_full)
    d_inputs, grad_gain_one = rms_backward(d_hidden_one, normed_one, factor_one, gain_one)
    d_inputs = d_inputs + d_middle
    shard_gain_one, shard_qkv, shard_out, shard_gain_two, shard_router = (
        lax.psum_scatter(
            grad_gain_one.astype(jnp.bfloat16), "fsdp", scatter_dimension=0, tiled=True
        ).astype(jnp.float32),
        lax.psum_scatter(
            grad_qkv.astype(jnp.bfloat16), "fsdp", scatter_dimension=0, tiled=True
        ).astype(jnp.float32),
        lax.psum_scatter(
            grad_out.astype(jnp.bfloat16), "fsdp", scatter_dimension=0, tiled=True
        ).astype(jnp.float32),
        lax.psum_scatter(
            grad_gain_two.astype(jnp.bfloat16), "fsdp", scatter_dimension=0, tiled=True
        ).astype(jnp.float32),
        lax.psum_scatter(
            grad_router.astype(jnp.bfloat16), "fsdp", scatter_dimension=0, tiled=True
        ).astype(jnp.float32),
    )
    summed = (
        lax.psum(shard_gain_one.astype(jnp.bfloat16), ("dp", "seq")).astype(jnp.float32),
        lax.psum(shard_qkv.astype(jnp.bfloat16), ("dp", "seq")).astype(jnp.float32),
        lax.psum(shard_out.astype(jnp.bfloat16), ("dp", "seq")).astype(jnp.float32),
        lax.psum(shard_gain_two.astype(jnp.bfloat16), ("dp", "seq")).astype(jnp.float32),
        lax.psum(shard_router.astype(jnp.bfloat16), ("dp", "seq")).astype(jnp.float32),
        lax.psum(grad_gate.astype(jnp.bfloat16), ("dp", "seq")).astype(jnp.float32),
        lax.psum(grad_up.astype(jnp.bfloat16), ("dp", "seq")).astype(jnp.float32),
        lax.psum(grad_down.astype(jnp.bfloat16), ("dp", "seq")).astype(jnp.float32),
    )
    layer_out = (middle + moe_out).astype(jnp.bfloat16)
    return (
        layer_out[None],
        d_inputs[None],
        summed[0],
        summed[1],
        summed[2],
        summed[3],
        summed[4],
        summed[5],
        summed[6],
        summed[7],
    )


def solution(mesh):
    placed = (
        P("dp", ("seq", "fsdp"), None),
        P("dp", ("seq", "fsdp"), None),
        P("dp"),
        P(),
        P("dp", ("seq", "fsdp"), None),
        P("fsdp"),
        P("fsdp", None),
        P("fsdp", None),
        P("fsdp"),
        P("fsdp", None),
        P("fsdp", None, None),
        P("fsdp", None, None),
        P("fsdp", None, None),
    )
    return jax.shard_map(
        local,
        mesh=mesh,
        in_specs=placed,
        out_specs=(
            P("dp", ("seq", "fsdp"), None),
            P("dp", ("seq", "fsdp"), None),
            P("fsdp"),
            P("fsdp", None),
            P("fsdp", None),
            P("fsdp"),
            P("fsdp", None),
            P("fsdp", None, None),
            P("fsdp", None, None),
            P("fsdp", None, None),
        ),
        check_vma=False,
    )
```

profile of v0, /device:TPU:0, one launch (start us, length us, event | category | flops | bytes accessed | tf_op | source)
XLA Modules:
  0.0 2822.2 jit_solution(3685858512837801337)
XLA Ops:
  20.5 48.5 %all-gather.8.cloned.1.call-done = bf16[1024,2048]{1,0:T(8,128)(2,1)} async-done(((bf16[512,2048]{1,0:T(8,128)(2,1)}), bf16[1024,2048]{1,0:T(8,128)(2,1)}) %all-gather.8.cloned.1.call-update) | async-done | bytes 4194320 | tf_op jit(solution)/shard_map/all_gather | solution.py:180
  112.7 9.8 all_gather.32
  122.8 17.8 all_gather.33
  143.2 50.6 %while.52 = (s32[]{:T(128)}, bf16[10,128,2,2,64]{1,4,3,2,0:T(8,128)(2,1)S(1)}, f32[10,2,2,128]{3,2,1,0:T(2,128)}, s32[10,128]{1,0:T(8,128)S(1)}, bf16[10,128,2,2...) while((s32[]{:T(128)}, ...), condition=%wide.region_4.5_spmd.clone.clone, body=%wide.region_1.4_spmd.clone.clone.sunk | while | flops 346725376 | bytes 17895668 | solution.py:251
  218.3 19.3 scatter_custom_fusion.3
  237.6 19.4 scatter_custom_fusion.4
  257.1 54.4 %all-gather.12.cloned.1.call-done = bf16[16,1024,512]{2,1,0:T(8,128)(2,1)} async-done(((bf16[8,1024,512]{2,1,0:T(8,128)(2,1)}), bf16[16,1024,512]{2,1,0:T(8,128)(2,1)}) %all-gather.12.cloned.1.call-update) | async-done | bytes 16777232 | tf_op jit(solution)/shard_map/all_gather | solution.py:272
  311.6 200.3 %all-gather.14.cloned.1.call-done = bf16[16,1024,512]{2,1,0:T(8,128)(2,1)} async-done(((bf16[8,1024,512]{2,1,0:T(8,128)(2,1)}), bf16[16,1024,512]{2,1,0:T(8,128)(2,1)}) %all-gather.14.cloned.1.call-update) | async-done | bytes 16777232 | tf_op jit(solution)/shard_map/all_gather | solution.py:273
  511.9 200.3 %all-gather.16.cloned.1.call-done = bf16[16,512,1024]{2,1,0:T(8,128)(2,1)} async-done(((bf16[8,512,1024]{2,1,0:T(8,128)(2,1)}), bf16[16,512,1024]{2,1,0:T(8,128)(2,1)}) %all-gather.16.cloned.1.call-update) | async-done | bytes 16777232 | tf_op jit(solution)/shard_map/all_gather | solution.py:274
  713.5 637.5 %while.51 = (s32[]{:T(128)}, f32[320,1024]{1,0:T(8,128)}, f32[320,1024]{1,0:T(8,128)S(1)}, f32[16,320]{1,0:T(8,128)}, bf16[16,1024,512]{2,1,0:T(8,128)(2,1)}, /*...) while((s32[]{:T(128)}, f32[320,1024]{1,0:T(8,128)}, ...), condition=%wide.region_18.20_spmd, body=%wide.region_13.19_spmd.sunk | while | flops 2423265280 | bytes 39193552 | solution.py:128
  743.9 5.8 scatter_custom_fusion.16
  1362.5 10.1 all-to-all-done.4
  1376.8 187.4 %while.53 = (s32[]{:T(128)}, f32[2560,2,64]{0,2,1:T(8,128)}, f32[2560,2,64]{0,2,1:T(8,128)}, bf16[10,128,2,2,64]{1,4,3,2,0:T(8,128)(2,1)}, bf16[10,128,2,2,64]{1...) while((s32[]{:T(128)}, f32[2560,2,64]{0,2,1:T(8,128)}, ...), condition=%wide.region_23.25_spmd.clone.clone.clone, body=%wide.region_21.24_spmd.clone.clone.clone.sunk | while | flops 853023744 | bytes 97386936 | solution.py:334
  1576.4 13.7 all_to_all.128
  1620.1 6.2 convolution_convert_fusion
  1634.7 57.3 %reduce-scatter.13.cloned.1.call-done = bf16[512,2048]{1,0:T(8,128)(2,1)} async-done(((bf16[1024,2048]{1,0:T(8,128)(2,1)}), bf16[512,2048]{1,0:T(8,128)(2,1)}) %reduce-scatter.13.cloned.1.call-update) | async-done | bytes 2097168 | tf_op jit(solution)/shard_map/reduce_scatter | solution.py:387
  1692.0 191.9 %reduce-scatter.19.cloned.1.call-done = bf16[8,1024,512]{2,1,0:T(8,128)(2,1)} async-done(((bf16[16,1024,512]{2,1,0:T(8,128)(2,1)}), bf16[8,1024,512]{2,1,0:T(8,128)(2,1)}) %reduce-scatter.19.cloned.1.call-update) | async-done | bytes 8388624 | tf_op jit(solution)/shard_map/reduce_scatter | solution.py:281
  1883.9 192.1 %reduce-scatter.21.cloned.1.call-done = bf16[8,1024,512]{2,1,0:T(8,128)(2,1)} async-done(((bf16[16,1024,512]{2,1,0:T(8,128)(2,1)}), bf16[8,1024,512]{2,1,0:T(8,128)(2,1)}) %reduce-scatter.21.cloned.1.call-update) | async-done | bytes 8388624 | tf_op jit(solution)/shard_map/reduce_scatter | solution.py:284
  2076.1 191.9 %reduce-scatter.23.cloned.1.call-done = bf16[8,512,1024]{2,1,0:T(8,128)(2,1)} async-done(((bf16[16,512,1024]{2,1,0:T(8,128)(2,1)}), bf16[8,512,1024]{2,1,0:T(8,128)(2,1)}) %reduce-scatter.23.cloned.1.call-update) | async-done | bytes 8388624 | tf_op jit(solution)/shard_map/reduce_scatter | solution.py:287
  2280.6 63.9 %all-reduce.3 = (bf16[512]{0:T(512)(128)(2,1)S(1)}, bf16[512]{0:T(512)(128)(2,1)S(1)}, bf16[512,16]{0,1:T(8,128)(2,1)S(1)}) all-reduce(bf16[512]{0:T(512)(128)(2,1)S(1)} %dynamic-slice.3, bf16[512]{0:T(512)(128)(2,1)S(1)} %dynamic-slice.5, ...), channel_id=1, replica_groups=mesh['dp'=4,'seq'=4,'fsdp'=2] {'dp','seq'}, use_global_device_ids=true, to_apply=%region_29.31 | all-reduce | flops 9216 | bytes 36864 | tf_op jit(solution)/shard_map/psum | solution.py:401
  2347.7 427.8 %all-reduce.8.cloned.1.call-done = (bf16[512,2048]{1,0:T(8,128)(2,1)}, bf16[512,1024]{1,0:T(8,128)(2,1)}, bf16[8,1024,512]{2,1,0:T(8,128)(2,1)}, bf16[8,1024,512]{2,1,0:T(8,128)(2,1)}, bf16[8,512,1024]{2,1,0:T(8,128)(2,1)}) async-done(((bf16[512,2048]{1,0:T(8,128)(2,1)}, bf16[512,1024]{1,0:T(8,128)(2,1)}, bf16[8,1024,512]{2,1,0:T(8,128)(2,1)}, bf16[8,1024,512]{2,1,0:T(8,128)(2,1)}, ...) | async-done | bytes 28311568 | tf_op jit(solution)/shard_map/psum | solution.py:402
  2775.5 11.9 convert_element_type.301
  2787.3 11.9 convert_element_type.303
  2799.2 11.9 convert_element_type.305
  (1339 shorter events, 1035.8 us)
Async XLA Ops:
  7.2 61.9 %all-gather.8.cloned.1.call-start = ((), (), s32[]{:S(2)}) async-start(), calls=%async_computation.16 | async-start | bytes 6291456 | tf_op jit(solution)/shard_map/all_gather | solution.py:180
  7.9 205.7 %all-gather.10.cloned.1.call-start = ((), (), s32[]{:S(2)}) async-start(), calls=%async_computation.17 | async-start | bytes 3145728 | tf_op jit(solution)/shard_map/all_gather | solution.py:181
  8.7 302.9 %all-gather.12.cloned.1.call-start = ((), (), s32[]{:S(2)}) async-start(), calls=%async_computation.18 | async-start | bytes 25165824 | tf_op jit(solution)/shard_map/all_gather | solution.py:272
  9.4 502.5 %all-gather.14.cloned.1.call-start = ((), (), s32[]{:S(2)}) async-start(), calls=%async_computation.19 | async-start | bytes 25165824 | tf_op jit(solution)/shard_map/all_gather | solution.py:273
  10.0 702.1 %all-gather.16.cloned.1.call-start = ((), (), s32[]{:S(2)}) async-start(), calls=%async_computation.20 | async-start | bytes 25165824 | tf_op jit(solution)/shard_map/all_gather | solution.py:274
  79.7 12.9 all-to-all-start.1
  92.6 10.2 all-to-all-start.2
  103.5 37.4 %all-to-all-start = ((bf16[320,4,256]{2,0,1:T(8,128)(2,1)}), bf16[320,4,256]{2,0,1:T(8,128)(2,1)S(1)}, u32[]{:S(2)}, u32[]{:S(2)}) async-start(bf16[320,4,256]{2,0,1:T(8,128)(2,1)} %bitcast.299), calls=%async_computation | async-start | bytes 1310720 | tf_op jit(solution)/shard_map/all_to_all | solution.py:210
  199.7 13.9 all-to-all-start.3
  217.9 494.3 %copy-start.34 = (f32[320,16]{0,1:T(8,128)}, f32[320,16]{0,1:T(8,128)S(1)}, u32[]{:S(2)}) copy-start(f32[320,16]{0,1:T(8,128)S(1)} %get-tuple-element.614) | copy-start | bytes 61444
  217.9 494.3 %copy-start.39 = (pred[320,16]{0,1:T(8,128)(4,1)}, pred[320,16]{0,1:T(8,128)(4,1)S(1)}, u32[]{:S(2)}) copy-start(pred[320,16]{0,1:T(8,128)(4,1)S(1)} %get-tuple-element.590) | copy-start | bytes 15364
  217.9 495.7 %copy-start.43 = (f32[320]{0:T(512)}, f32[320]{0:T(512)S(1)}, u32[]{:S(2)}) copy-start(f32[320]{0:T(512)S(1)} %get-tuple-element.589) | copy-start | bytes 3844
  1359.0 13.7 all-to-all-start.4
  1362.5 232.7 %reduce-scatter.9.cloned.1.call-start = ((), (), s32[]{:S(2)}) async-start(), calls=%async_computation.21 | async-start | bytes 983040 | tf_op jit(solution)/shard_map/reduce_scatter | solution.py:339
  1566.4 38.3 %reduce-scatter.11.cloned.1.call-start = ((), (), s32[]{:S(2)}) async-start(), calls=%async_computation.22 | async-start | bytes 983040 | tf_op jit(solution)/shard_map/reduce_scatter | solution.py:345
  1568.9 65.9 %reduce-scatter.15.cloned.1.call-start = ((), (), s32[]{:S(2)}) async-start(), calls=%async_computation.24 | async-start | bytes 3145728 | tf_op jit(solution)/shard_map/reduce_scatter | solution.py:390
  1597.1 10.9 all-to-all-start.6
  1608.0 10.9 all-to-all-start.7
  1612.1 80.0 %reduce-scatter.13.cloned.1.call-start = ((), (), s32[]{:S(2)}) async-start(), calls=%async_computation.23 | async-start | bytes 6291456 | tf_op jit(solution)/shard_map/reduce_scatter | solution.py:387
  1626.3 257.6 %reduce-scatter.19.cloned.1.call-start = ((), (), s32[]{:S(2)}) async-start(), calls=%async_computation.26 | async-start | bytes 25165824 | tf_op jit(solution)/shard_map/reduce_scatter | solution.py:281
  1626.9 449.1 %reduce-scatter.21.cloned.1.call-start = ((), (), s32[]{:S(2)}) async-start(), calls=%async_computation.27 | async-start | bytes 25165824 | tf_op jit(solution)/shard_map/reduce_scatter | solution.py:284
  1627.6 640.3 %reduce-scatter.23.cloned.1.call-start = ((), (), s32[]{:S(2)}) async-start(), calls=%async_computation.28 | async-start | bytes 25165824 | tf_op jit(solution)/shard_map/reduce_scatter | solution.py:287
  1628.2 652.4 %reduce-scatter.17.cloned.1.call-start = ((), (), s32[]{:S(2)}) async-start(), calls=%async_computation.25 | async-start | bytes 49152 | tf_op jit(solution)/shard_map/reduce_scatter | solution.py:396
  1629.1 1146.4 %all-reduce.8.cloned.1.call-start = ((), (), s32[]{:S(2)}) async-start(), calls=%async_computation.29 | async-start | bytes 56623104 | tf_op jit(solution)/shard_map/psum | solution.py:402
  (262 other events, 2037.5 us)
Sparse Core Ops, SparseCore 0:
  9.6 59.4 all-gather.7
  70.6 33.1 all-gather.9
  105.3 206.2 all-gather.11
  313.0 198.8 all-gather.13
  513.2 198.8 all-gather.15
  1566.6 15.0 reduce-scatter.8
  1584.0 15.9 reduce-scatter.10
  1602.8 31.8 reduce-scatter.14
  1637.7 54.2 reduce-scatter.12
  1694.7 189.1 reduce-scatter.18
  1886.9 189.1 reduce-scatter.20
  2078.8 189.1 reduce-scatter.22
  2270.8 9.8 reduce-scatter.16
  2286.5 488.8 all-reduce.7
where the time goes:
time: 2840 us; the launch traced here: 2820 us
  waiting for transfers between devices  1600 us (56%)
  matrix products  499 us (18%)
  other arithmetic  301 us (11%)
  local copies, waits for them, and re-layouts  252 us (9%)
  blocking collectives  124 us (4%)
    psum x1, waiting for transfers between devices, local(): lax.psum(shard_qkv.astype(jnp.bfloat16), ('dp', 'seq')).astype(jnp.float32)  428 us
    all_gather x1, waiting for transfers between devices, local(): lax.all_gather(w_up, 'fsdp', axis=0, tiled=True)  200 us
    all_gather x1, waiting for transfers between devices, local(): lax.all_gather(w_down, 'fsdp', axis=0, tiled=True)  200 us
    reduce_scatter x1, waiting for transfers between devices, local(): lax.psum_scatter(grad_up.astype(jnp.bfloat16), 'fsdp', scatter_dimension=...  192 us
    reduce_scatter x1, waiting for transfers between devices, local(): lax.psum_scatter(grad_down.astype(jnp.bfloat16), 'fsdp', scatter_dimensio...  192 us
    reduce_scatter x1, waiting for transfers between devices, local(): lax.psum_scatter(grad_gate.astype(jnp.bfloat16), 'fsdp', scatter_dimensio...  192 us
    dot_general x51, matrix products, times_transpose(): lax.dot_general(left_side, right_side, (((1,), (1,)), ((), ())), preferre...  116 us
    scatter-add x16, other arithmetic, expert_step(): total = total.at[row_index].add(weight_col * expert_out)  92.7 us
  transfers between devices with their start and end apart: 21, of which 16 were waited for; matrix products, arithmetic and copies ran while one was open for 6% of the time, Pallas kernels for 0%

commit v1 on v0

v1 whole, which is shorter than its diff:
```python
import functools
import math

import jax
import jax.numpy as jnp
from jax import lax
from jax.experimental import pallas as pl
from jax.experimental.pallas import tpu as pltpu
from jax.sharding import PartitionSpec as P

QUERY_HEADS = 16
KEY_VALUE_HEADS = 8
HEAD_WIDTH = 64
TOPK = 8

EPS = 1e-06
ROPE_BASE = 10000.0
LOG2E = math.log2(math.e)
NEG = -1e30
BF = jnp.bfloat16
F32 = jnp.float32
VMEM_LIMIT = 60 * 1024 * 1024

NT_DIMS = (((1,), (1,)), ((), ()))
TN_DIMS = (((0,), (0,)), ((), ()))


def mm(a, b):
    return jnp.dot(a, b, preferred_element_type=F32)


def mm_nt(a, b):
    return lax.dot_general(a, b, NT_DIMS, preferred_element_type=F32)


def mm_tn(a, b):
    return lax.dot_general(a, b, TN_DIMS, preferred_element_type=F32)


def params(**kw):
    return pltpu.CompilerParams(vmem_limit_bytes=VMEM_LIMIT, **kw)


def whole(shape):
    return pl.BlockSpec(shape, lambda *_: (0,) * len(shape))


def rms_parts(x):
    factor = lax.rsqrt(jnp.mean(x * x, axis=-1, keepdims=True) + EPS)
    return x * factor, factor


def qkv_kernel(tok_ref, gain_ref, w_ref, cos_ref, sin_ref, h_ref, q_ref, kv_ref):
    normed, _ = rms_parts(tok_ref[...].astype(F32))
    h = (normed * gain_ref[...]).astype(BF)
    h_ref[...] = h
    proj = mm(h, w_ref[...])
    cos, sin = cos_ref[...], sin_ref[...]
    low_half = lax.broadcasted_iota(jnp.int32, cos.shape, 1) % HEAD_WIDTH < HEAD_WIDTH // 2
    half = HEAD_WIDTH // 2
    for t in range(3):
        w = proj[:, t * 128 : (t + 1) * 128]
        rot = jnp.where(low_half, -pltpu.roll(w, 128 - half, 1), pltpu.roll(w, half, 1))
        out = (w * cos + rot * sin).astype(BF)
        if t < 2:
            q_ref[:, t * 128 : (t + 1) * 128] = out
        else:
            kv_ref[:, :128] = out
    kv_ref[:, 128:] = proj[:, 384:].astype(BF)


def project(tok, gain, w, cos, sin, tile):
    rows, width = tok.shape
    return pl.pallas_call(
        qkv_kernel,
        grid=(rows // tile,),
        in_specs=[
            pl.BlockSpec((tile, width), lambda i: (i, 0)),
            whole((1, width)),
            whole(w.shape),
            pl.BlockSpec((tile, 128), lambda i: (i, 0)),
            pl.BlockSpec((tile, 128), lambda i: (i, 0)),
        ],
        out_specs=[
            pl.BlockSpec((tile, width), lambda i: (i, 0)),
            pl.BlockSpec((tile, 256), lambda i: (i, 0)),
            pl.BlockSpec((tile, 256), lambda i: (i, 0)),
        ],
        out_shape=[
            jax.ShapeDtypeStruct((rows, width), BF),
            jax.ShapeDtypeStruct((rows, 256), BF),
            jax.ShapeDtypeStruct((rows, 256), BF),
        ],
        compiler_params=params(),
        name="project",
    )(tok, gain, w, cos, sin)


def project_back_kernel(
    tok_ref, h_ref, dq_ref, dkv_ref, w_ref, cos_ref, sin_ref, dh_ref, gw_ref, gn_ref, acc
):
    step = pl.program_id(0)

    @pl.when(step == 0)
    def _():
        acc[...] = jnp.zeros_like(acc)
        gn_ref[...] = jnp.zeros_like(gn_ref)

    cos, sin = cos_ref[...], sin_ref[...]
    half = HEAD_WIDTH // 2
    low_half = lax.broadcasted_iota(jnp.int32, cos.shape, 1) % HEAD_WIDTH < half
    parts = []
    for t in range(3):
        w = dq_ref[:, t * 128 : (t + 1) * 128] if t < 2 else dkv_ref[:, :128]
        w = w.astype(F32)
        y = w * sin
        rot = jnp.where(low_half, pltpu.roll(y, 128 - half, 1), -pltpu.roll(y, half, 1))
        parts.append((w * cos + rot).astype(BF))
    parts.append(dkv_ref[:, 128:].astype(BF))
    dproj = jnp.concatenate(parts, axis=1)
    acc[...] += mm_tn(h_ref[...], dproj)
    dh = mm_nt(dproj, w_ref[...])
    dh_ref[...] = dh.astype(BF)
    normed, _ = rms_parts(tok_ref[...].astype(F32))
    gn_ref[...] += jnp.sum((dh * normed).reshape(-1, 8, dh.shape[1]), axis=0)

    @pl.when(step == pl.num_programs(0) - 1)
    def _():
        gw_ref[...] = acc[...].astype(BF)


def project_back(tok, h, dq, dkv, w, cos, sin, tile):
    rows, width = tok.shape
    row = lambda n: pl.BlockSpec((tile, n), lambda i: (i, 0))
    return pl.pallas_call(
        project_back_kernel,
        grid=(rows // tile,),
        in_specs=[row(width), row(width), row(256), row(256), whole(w.shape), row(128), row(128)],
        out_specs=[row(width), whole(w.shape), whole((8, width))],
        out_shape=[
            jax.ShapeDtypeStruct((rows, width), BF),
            jax.ShapeDtypeStruct(w.shape, BF),
            jax.ShapeDtypeStruct((8, width), F32),
        ],
        scratch_shapes=[pltpu.VMEM(w.shape, F32)],
        compiler_params=params(),
        name="project_back",
    )(tok, h, dq, dkv, w, cos, sin)


def stack_heads(a, b):
    low = lax.broadcasted_iota(jnp.int32, a.shape, 1) < HEAD_WIDTH
    zero = jnp.zeros_like(a)
    return jnp.concatenate(
        [jnp.where(low, a, zero), jnp.where(low, b, zero), jnp.where(low, zero, a), jnp.where(low, zero, b)],
        axis=0,
    )


def unstack_heads(x):
    n = x.shape[0] // 4
    low = lax.broadcasted_iota(jnp.int32, (n, 128), 1) < HEAD_WIDTH
    return (
        jnp.where(low, x[:n], x[2 * n : 3 * n]),
        jnp.where(low, x[n : 2 * n], x[3 * n :]),
    )


def block_counts(span_id, limit, span, kb):
    first = span_id * span
    seen = (first + span - 1) // kb + 1
    blocks = jnp.minimum(seen, (limit + kb - 1) // kb)
    full = jnp.minimum(first + 1, limit) // kb
    return jnp.minimum(full, blocks), blocks


def sort_spans(ktab_ref, src, dst, lanes, span, count):
    @pl.loop(0, count)
    def _(j):
        to = pl.multiple_of(ktab_ref[j] * span, span)
        dst[pl.ds(to, span), :] = src[pl.ds(pl.multiple_of(j * span, span), span), lanes]


def attend_kernel(
    qtab_ref, ktab_ref, len_ref, q_ref, kv_ref, o_ref, lse_ref, ks, vs, *, span, kb
):
    step = pl.program_id(0)
    count = ks.shape[0] // span

    @pl.when(step == 0)
    def _():
        sort_spans(ktab_ref, kv_ref, ks, slice(0, 128), span, count)
        sort_spans(ktab_ref, kv_ref, vs, slice(128, 256), span, count)

    q = stack_heads(q_ref[:, :128], q_ref[:, 128:])
    rows = 4 * span
    limit = len_ref[0]
    span_id = qtab_ref[step]
    full, blocks = block_counts(span_id, limit, span, kb)
    qpos = span_id * span + lax.broadcasted_iota(jnp.int32, (rows, kb), 0) % span
    col = lax.broadcasted_iota(jnp.int32, (rows, kb), 1)
    last = jnp.minimum(qpos, limit - 1)

    def body(masked, i, carry):
        top, total, acc = carry
        at = pl.multiple_of(i * kb, kb)
        s = mm_nt(q, ks[pl.ds(at, kb), :]) * (HEAD_WIDTH**-0.5 * LOG2E)
        if masked:
            s = jnp.where(col + i * kb <= last, s, NEG)
        new = jnp.maximum(top, jnp.max(s, axis=1, keepdims=True))
        fade = jnp.exp2(top - new)
        p = jnp.exp2(s - new)
        total = total * fade + jnp.sum(p, axis=1, keepdims=True)
        acc = acc * fade + mm(p.astype(BF), vs[pl.ds(at, kb), :])
        return new, total, acc

    carry = (
        jnp.full((rows, 1), NEG, F32),
        jnp.zeros((rows, 1), F32),
        jnp.zeros((rows, 128), F32),
    )
    carry = lax.fori_loop(0, full, functools.partial(body, False), carry)
    top, total, acc = lax.fori_loop(full, blocks, functools.partial(body, True), carry)
    a, b = unstack_heads(acc / total)
    o_ref[:, :128] = a
    o_ref[:, 128:] = b
    lse = jnp.broadcast_to(top + jnp.log2(total), (rows, 128))
    lse_ref[0] = jnp.transpose(lse)[:8]


def attend(qtab, ktab, limit, q, kv, span, kb):
    steps, keys = q.shape[0] // span, kv.shape[0]
    return pl.pallas_call(
        functools.partial(attend_kernel, span=span, kb=kb),
        grid_spec=pltpu.PrefetchScalarGridSpec(
            num_scalar_prefetch=3,
            grid=(steps,),
            in_specs=[pl.BlockSpec((span, 256), lambda i, *_: (i, 0)), whole(kv.shape)],
            out_specs=[
                pl.BlockSpec((span, 256), lambda i, *_: (i, 0)),
                pl.BlockSpec((1, 8, 4 * span), lambda i, *_: (i, 0, 0)),
            ],
            scratch_shapes=[pltpu.VMEM((keys, 128), BF), pltpu.VMEM((keys, 128), BF)],
        ),
        out_shape=[
            jax.ShapeDtypeStruct((q.shape[0], 256), F32),
            jax.ShapeDtypeStruct((steps, 8, 4 * span), F32),
        ],
        compiler_params=params(),
        name="attend",
    )(qtab, ktab, limit, q, kv)


def attend_back_kernel(
    qtab_ref, ktab_ref, len_ref, q_ref, kv_ref, do_ref, o_ref, lse_ref, dq_ref, dkv_ref,
    ks, vs, dk, dv, *, span, kb,
):
    step = pl.program_id(0)
    count = ks.shape[0] // span
    scale = HEAD_WIDTH**-0.5

    @pl.when(step == 0)
    def _():
        sort_spans(ktab_ref, kv_ref, ks, slice(0, 128), span, count)
        sort_spans(ktab_ref, kv_ref, vs, slice(128, 256), span, count)
        dk[...] = jnp.zeros_like(dk)
        dv[...] = jnp.zeros_like(dv)

    q = stack_heads(q_ref[:, :128], q_ref[:, 128:])
    do = stack_heads(do_ref[:, :128], do_ref[:, 128:])
    rows = 4 * span
    inner = do.astype(F32) * stack_heads(o_ref[:, :128], o_ref[:, 128:])
    delta = jnp.sum(jnp.transpose(inner), axis=0, keepdims=True)
    lse = lse_ref[0, :1]
    limit = len_ref[0]
    span_id = qtab_ref[step]
    full, blocks = block_counts(span_id, limit, span, kb)
    blocks = jnp.where(span_id * span < limit, blocks, 0)
    full = jnp.minimum(full, blocks)
    qpos = span_id * span + lax.broadcasted_iota(jnp.int32, (kb, rows), 1) % span
    key = lax.broadcasted_iota(jnp.int32, (kb, rows), 0)
    last = jnp.minimum(qpos, limit - 1)

    def body(masked, i, dq):
        at = pl.ds(pl.multiple_of(i * kb, kb), kb)
        k, v = ks[at, :], vs[at, :]
        s = mm_nt(k, q) * (scale * LOG2E)
        p = jnp.exp2(s - lse)
        if masked:
            p = jnp.where(key + i * kb <= last, p, 0.0)
        dp = mm_nt(v, do)
        ds = (p * (dp - delta)).astype(BF)
        dk[at, :] += mm(ds, q)
        dv[at, :] += mm(p.astype(BF), do)
        return dq + mm_tn(ds, k)

    dq = jnp.zeros((rows, 128), F32)
    dq = lax.fori_loop(0, full, functools.partial(body, False), dq)
    dq = lax.fori_loop(full, blocks, functools.partial(body, True), dq)
    a, b = unstack_heads(dq * scale)
    dq_ref[:, :128] = a.astype(BF)
    dq_ref[:, 128:] = b.astype(BF)

    @pl.when(step == pl.num_programs(0) - 1)
    def _():
        @pl.loop(0, count)
        def _(j):
            at = pl.ds(pl.multiple_of(ktab_ref[j] * span, span), span)
            to = pl.ds(pl.multiple_of(j * span, span), span)
            dkv_ref[to, :128] = (dk[at, :] * scale).astype(BF)
            dkv_ref[to, 128:] = dv[at, :].astype(BF)


def attend_back(qtab, ktab, limit, q, kv, do, o, lse, span, kb):
    steps, keys = q.shape[0] // span, kv.shape[0]
    row = pl.BlockSpec((span, 256), lambda i, *_: (i, 0))
    return pl.pallas_call(
        functools.partial(attend_back_kernel, span=span, kb=kb),
        grid_spec=pltpu.PrefetchScalarGridSpec(
            num_scalar_prefetch=3,
            grid=(steps,),
            in_specs=[
                row, whole(kv.shape), row, row,
                pl.BlockSpec((1, 8, 4 * span), lambda i, *_: (i, 0, 0)),
            ],
            out_specs=[row, whole(kv.shape)],
            scratch_shapes=[
                pltpu.VMEM((keys, 128), BF), pltpu.VMEM((keys, 128), BF),
                pltpu.VMEM((keys, 128), F32), pltpu.VMEM((keys, 128), F32),
            ],
        ),
        out_shape=[
            jax.ShapeDtypeStruct((q.shape[0], 256), BF),
            jax.ShapeDtypeStruct(kv.shape, BF),
        ],
        compiler_params=params(),
        name="attend_back",
    )(qtab, ktab, limit, q, kv, do, o, lse)


def experts_kernel(
    base_ref, h_ref, c_ref, wg_ref, wu_ref, wd_ref, moe_ref, dh_ref, gg_ref, gu_ref, gd_ref,
    moe, dh, dgates, s_act, s_gate, s_up, *, tile,
):
    step = pl.program_id(0)
    width = c_ref.shape[1]
    expert = base_ref[1] + step
    wg, wu, wd = wg_ref[0], wu_ref[0], wd_ref[0]

    @pl.when(step == 0)
    def _():
        moe[...] = jnp.zeros_like(moe)
        dh[...] = jnp.zeros_like(dh)
        dgates[...] = jnp.zeros_like(dgates)

    @pl.loop(0, moe.shape[0] // tile)
    def _(t):
        at = pl.ds(pl.multiple_of(t * tile, tile), tile)
        h, c = h_ref[at, :width], c_ref[at, :]
        lane = lax.broadcasted_iota(jnp.int32, (tile, 128), 1)
        mine = lane == expert
        gate = jnp.sum(
            jnp.where(mine, h_ref[at, width:].astype(F32), 0.0), axis=1, keepdims=True
        )
        g, u, z = mm(h, wg), mm(h, wu), mm_nt(c, wd)
        sig = jax.nn.sigmoid(g)
        silu = g * sig
        act = silu * u
        dgates[at, :] += jnp.where(mine, jnp.sum(act * z, axis=1, keepdims=True), 0.0)
        act = (act * gate).astype(BF)
        dact = z * gate
        dgate = (dact * u * sig * (1.0 + g * (1.0 - sig))).astype(BF)
        dup = (dact * silu).astype(BF)
        s_act[at, :] = act
        s_gate[at, :] = dgate
        s_up[at, :] = dup
        moe[at, :] += mm(act, wd)
        dh[at, :] += mm_nt(dgate, wg) + mm_nt(dup, wu)

    for i in range(4):
        n = width // 4
        gg_ref[0, i * n : (i + 1) * n, :] = mm_tn(h_ref[:, i * n : (i + 1) * n], s_gate[...]).astype(BF)
        gu_ref[0, i * n : (i + 1) * n, :] = mm_tn(h_ref[:, i * n : (i + 1) * n], s_up[...]).astype(BF)
    for i in range(2):
        n = wd.shape[0] // 2
        gd_ref[0, i * n : (i + 1) * n, :] = mm_tn(s_act[:, i * n : (i + 1) * n], c_ref[...]).astype(BF)

    @pl.when(step == pl.num_programs(0) - 1)
    def _():
        moe_ref[...] = moe[...].astype(BF)
        dh_ref[:, :width] = dh[...].astype(BF)
        dh_ref[:, width:] = dgates[...].astype(BF)


def experts(base, count, h, c, wg, wu, wd, tile):
    rows, width = c.shape
    ff = wg.shape[2]
    pick = lambda shape: pl.BlockSpec((1,) + shape, lambda e, s: (s[0] + e, 0, 0))
    put = lambda shape: pl.BlockSpec((1,) + shape, lambda e, s: (e, 0, 0))
    return pl.pallas_call(
        functools.partial(experts_kernel, tile=tile),
        grid_spec=pltpu.PrefetchScalarGridSpec(
            num_scalar_prefetch=1,
            grid=(count,),
            in_specs=[
                whole(h.shape), whole(c.shape),
                pick((width, ff)), pick((width, ff)), pick((ff, width)),
            ],
            out_specs=[
                whole(c.shape), whole(h.shape),
                put((width, ff)), put((width, ff)), put((ff, width)),
            ],
            scratch_shapes=[
                pltpu.VMEM((rows, width), F32), pltpu.VMEM((rows, width), F32),
                pltpu.VMEM((rows, 128), F32),
                pltpu.VMEM((rows, ff), BF), pltpu.VMEM((rows, ff), BF), pltpu.VMEM((rows, ff), BF),
            ],
        ),
        out_shape=[
            jax.ShapeDtypeStruct(c.shape, BF),
            jax.ShapeDtypeStruct(h.shape, BF),
            jax.ShapeDtypeStruct((count, width, ff), BF),
            jax.ShapeDtypeStruct((count, width, ff), BF),
            jax.ShapeDtypeStruct((count, ff, width), BF),
        ],
        compiler_params=params(),
        name="experts",
    )(base, h, c, wg, wu, wd)


def flip_core(x):
    return lax.ppermute(x, "seq", [(0, 1), (1, 0), (2, 3), (3, 2)])


def flip_x(x):
    return lax.ppermute(x, "seq", [(0, 2), (2, 0), (1, 3), (3, 1)])


def flip_both(x):
    return lax.ppermute(x, "seq", [(0, 3), (3, 0), (1, 2), (2, 1)])


def gather_seq(x):
    own = jnp.stack([x, flip_core(x)])
    far = flip_x(x)
    return jnp.concatenate([own, far[None], flip_core(far)[None]])


def swap_seq(blocks):
    return [blocks[0], flip_core(blocks[1]), flip_x(blocks[2]), flip_both(blocks[3])]


def gather_fsdp(x, axis=0):
    if lax.axis_size("fsdp") == 2:
        return jnp.concatenate([x, lax.ppermute(x, "fsdp", [(0, 1), (1, 0)])], axis=axis)
    return lax.all_gather(x, "fsdp", axis=axis, tiled=True)


def scatter_fsdp(x):
    if lax.axis_size("fsdp") == 2:
        n = x.shape[0] // 2
        other = lax.ppermute(x[n:], "fsdp", [(0, 1), (1, 0)])
        return x[:n].astype(F32) + other.astype(F32)
    return lax.psum_scatter(x, "fsdp", scatter_dimension=0, tiled=True).astype(F32)


def gather_rows(x):
    return lax.all_gather(x, "fsdp", axis=0, tiled=True)


def local(
    tokens, cotangent, lengths, order, routes, norm1, query_key_value_weight, w_out, norm2, router,
    w_gate, w_up, w_down,
):
    groups = lax.axis_size("seq")
    shards = lax.axis_size("fsdp")
    slots = lax.axis_size("dp")
    assert groups == 4
    seq, fsdp = lax.axis_index("seq"), lax.axis_index("fsdp")
    core = seq % 2
    rows, width = tokens.shape[1:]
    span = rows // 2
    x = tokens[0]
    limit = lengths[:1]
    n_experts = router.shape[1]
    owned = w_gate.shape[0]
    count = owned // 2

    table = order.reshape(groups, shards, 2)
    relative = jnp.arange(groups, dtype=jnp.int32) ^ seq
    table = jnp.take(table, relative, axis=0)
    qtab = jnp.take(table, fsdp, axis=1).reshape(-1)
    if shards == 2:
        held = jnp.stack([fsdp, 1 - fsdp])
    else:
        held = jnp.arange(shards)
    ktab = jnp.transpose(jnp.take(table, held, axis=1), (1, 0, 2)).reshape(-1)
    qpos = (qtab[:, None] * span + jnp.arange(span, dtype=jnp.int32)[None, :]).reshape(-1)
    half = HEAD_WIDTH // 2
    freqs = jnp.exp(jnp.arange(half, dtype=F32) * (-2.0 * math.log(ROPE_BASE) / HEAD_WIDTH))
    angles = qpos.astype(F32)[:, None] * freqs[None, :]
    cos = jnp.tile(jnp.cos(angles), (1, 4))
    sin = jnp.tile(jnp.sin(angles), (1, 4))

    heads = QUERY_HEADS // groups
    qw, kw = heads * HEAD_WIDTH, KEY_VALUE_HEADS // groups * HEAD_WIDTH
    w3 = query_key_value_weight
    wq = lax.dynamic_slice_in_dim(w3, seq * qw, qw, 1).reshape(-1, 2, 2, HEAD_WIDTH)
    wq = jnp.swapaxes(wq, 1, 2).reshape(-1, qw)
    wk = lax.dynamic_slice_in_dim(w3, QUERY_HEADS * HEAD_WIDTH + seq * kw, kw, 1)
    wv = lax.dynamic_slice_in_dim(w3, (QUERY_HEADS + KEY_VALUE_HEADS) * HEAD_WIDTH + seq * kw, kw, 1)
    wcols = gather_rows(jnp.concatenate([wq, wk, wv], axis=1))
    small = jnp.concatenate([norm1[:, None], norm2[:, None], router], axis=1)
    small = gather_rows(small)
    gain_one = small[:, 0].astype(F32)
    gain_two = small[:, 1].astype(F32)
    route_full = small[:, 2:]
    out_full = gather_rows(w_out)

    tok = gather_seq(x).reshape(groups * rows, width)
    hidden_one, q, kv_own = project(tok, gain_one[None], wcols, cos, sin, rows)
    kv = gather_fsdp(kv_own)
    kb = 4 * span
    attended, lse = attend(qtab, ktab, limit, q, kv, span, kb)
    sent = attended.astype(BF).reshape(groups, rows, qw)
    got = jnp.stack(swap_seq([sent[m] for m in range(groups)]))
    got = jnp.take(got, relative, axis=0).reshape(groups, rows, 2, 2, HEAD_WIDTH)
    token_out = jnp.transpose(got, (1, 0, 3, 2, 4)).reshape(rows, groups * qw)

    own_valid = (qpos[:rows] < limit[0])[:, None]
    inputs = x.astype(F32)
    middle = inputs + mm(token_out, out_full)
    normed_two, factor_two = rms_parts(middle)
    hidden_two = (normed_two * gain_two).astype(BF)
    logits = mm(hidden_two, route_full)
    chosen = jnp.any(
        routes[0][:, :, None] == jnp.arange(n_experts, dtype=jnp.int32)[None, None, :], axis=1
    )
    top = jnp.max(jnp.where(chosen, logits, NEG), axis=-1, keepdims=True)
    raised = jnp.where(chosen, jnp.exp(logits - top), 0.0)
    gates = raised / jnp.sum(raised, axis=-1, keepdims=True)
    masked_cot = jnp.where(own_valid, cotangent[0], jnp.zeros_like(cotangent[0]))

    def share(v):
        near = gather_fsdp(v)
        return jnp.concatenate([near, flip_core(near)])

    cot_all = share(masked_cot)
    extended = jnp.concatenate(
        [hidden_two, gates.astype(BF), jnp.zeros((rows, 128 - n_experts), BF)], axis=1
    )
    hid_all = share(extended)
    base = jnp.stack([core * count, fsdp * owned + core * count]).astype(jnp.int32)
    part = rows * 4
    moe_parts, dh_parts, weight_grads = [], [], None
    for i in range(hid_all.shape[0] // part):
        got = experts(
            base, count, hid_all[i * part : (i + 1) * part], cot_all[i * part : (i + 1) * part],
            w_gate, w_up, w_down, rows,
        )
        moe_parts.append(got[0])
        dh_parts.append(got[1])
        if weight_grads is None:
            weight_grads = list(got[2:])
        else:
            weight_grads = [a.astype(F32) + b.astype(F32) for a, b in zip(weight_grads, got[2:])]
            weight_grads = [a.astype(BF) for a in weight_grads]

    def give_back(parts):
        v = jnp.concatenate(parts) if len(parts) > 1 else parts[0]
        n = v.shape[0] // 2
        near = v[:n].astype(F32) + flip_core(v[n:]).astype(F32)
        return scatter_fsdp(near.astype(BF))

    d_ext = give_back(dh_parts)
    d_gates = d_ext[:, width : width + n_experts]
    d_logits = (gates * (d_gates - jnp.sum(gates * d_gates, axis=-1, keepdims=True))).astype(BF)
    grad_router = mm_tn(hidden_two, d_logits)
    d_hidden = d_ext[:, :width] + mm_nt(d_logits, route_full)
    grad_norm2 = jnp.sum(d_hidden * normed_two, axis=0)
    d_n = d_hidden * gain_two
    d_middle = masked_cot.astype(F32) + factor_two * (
        d_n - normed_two * jnp.mean(d_n * normed_two, axis=-1, keepdims=True)
    )
    d_attn = d_middle.astype(BF)
    grad_out = mm_tn(token_out, d_attn).astype(BF)
    d_token_out = mm_nt(d_attn, out_full).astype(BF)
    d_heads = d_token_out.reshape(rows, groups, 2, 2, HEAD_WIDTH)
    d_heads = jnp.transpose(d_heads, (1, 0, 3, 2, 4)).reshape(groups, rows, qw)
    d_heads = jnp.take(d_heads, relative, axis=0)
    d_heads = jnp.concatenate(swap_seq([d_heads[m] for m in range(groups)]))
    dq, dkv = attend_back(qtab, ktab, limit, q, kv, d_heads, attended, lse, span, kb)
    dkv = scatter_fsdp(dkv)
    dh_one, grad_cols, grad_norm1 = project_back(
        tok, hidden_one, dq, dkv, wcols, cos, sin, rows
    )
    dh_one = dh_one.reshape(groups, rows, width)
    near = dh_one[0::2].astype(F32) + flip_core(dh_one[1::2]).astype(F32)
    d_hidden_one = near[0] + flip_x(near[1].astype(BF)).astype(F32)
    normed_one, factor_one = rms_parts(inputs)
    d_n = d_hidden_one * gain_one
    d_inputs = d_middle + factor_one * (
        d_n - normed_one * jnp.mean(d_n * normed_one, axis=-1, keepdims=True)
    )

    every = ("dp", "seq")
    fold = [[d * groups + 2 * i + c for d in range(slots) for i in range(groups // 2)] for c in range(2)]

    def reduce_experts(g):
        part = lax.psum_scatter(
            g, every, scatter_dimension=1, tiled=True, axis_index_groups=fold
        )
        full = lax.all_gather(part, every, axis=0)
        n, r, m = part.shape
        full = full.reshape(slots, groups // 2, 2, n, r, m)
        full = jnp.transpose(full, (2, 3, 0, 1, 4, 5))
        return full.reshape(2 * n, slots * groups // 2 * r, m).astype(F32)

    grad_gate, grad_up, grad_down = [reduce_experts(g) for g in weight_grads]
    shard_out = lax.psum(
        lax.psum_scatter(grad_out, "fsdp", scatter_dimension=0, tiled=True), every
    ).astype(F32)
    shard_cols = lax.psum(
        lax.psum_scatter(grad_cols, "fsdp", scatter_dimension=0, tiled=True), "dp"
    )
    cols = lax.all_gather(shard_cols, "seq", axis=0)
    gq = cols[:, :, :qw].reshape(groups, -1, 2, 2, HEAD_WIDTH)
    gq = jnp.transpose(gq, (1, 0, 3, 2, 4)).reshape(-1, groups * qw)
    gk = jnp.transpose(cols[:, :, qw : qw + kw], (1, 0, 2)).reshape(-1, groups * kw)
    gv = jnp.transpose(cols[:, :, qw + kw :], (1, 0, 2)).reshape(-1, groups * kw)
    shard_qkv = jnp.concatenate([gq, gk, gv], axis=1).astype(F32)
    tiny = jnp.concatenate(
        [jnp.sum(grad_norm1, axis=0)[:, None], grad_norm2[:, None], grad_router], axis=1
    )
    tiny = lax.psum(lax.psum_scatter(tiny, "fsdp", scatter_dimension=0, tiled=True), every)
    layer_out = (middle + give_back(moe_parts)).astype(BF)
    return (
        layer_out[None], d_inputs[None], tiny[:, 0], shard_qkv, shard_out, tiny[:, 1], tiny[:, 2:],
        grad_gate, grad_up, grad_down,
    )


def solution(mesh):
    placed = (
        P("dp", ("seq", "fsdp"), None),
        P("dp", ("seq", "fsdp"), None),
        P("dp"),
        P(),
        P("dp", ("seq", "fsdp"), None),
        P("fsdp"),
        P("fsdp", None),
        P("fsdp", None),
        P("fsdp"),
        P("fsdp", None),
        P("fsdp", None, None),
        P("fsdp", None, None),
        P("fsdp", None, None),
    )
    return jax.shard_map(
        local,
        mesh=mesh,
        in_specs=placed,
        out_specs=(
            P("dp", ("seq", "fsdp"), None),
            P("dp", ("seq", "fsdp"), None),
            P("fsdp"),
            P("fsdp", None),
            P("fsdp", None),
            P("fsdp"),
            P("fsdp", None),
            P("fsdp", None, None),
            P("fsdp", None, None),
            P("fsdp", None, None),
        ),
        check_vma=False,
    )
```

time: 2840 us -> 1130 us (0.40)
  waiting for transfers between devices: 1600 us -> 733 us
  matrix products: 499 us -> 8.25 us
  other arithmetic: 301 us -> 70.5 us
  local copies, waits for them, and re-layouts: 252 us -> 68.8 us
  Pallas kernels: 0 us -> 124 us
  blocking collectives: 124 us -> 88.8 us
    dot_general x223 -> x6, matrix products: 499 us -> 8.25 us  [the longest x2 3.15 us: mm(): return jnp.dot(a, b, preferred_element_type=F32)]
    psum x1 -> x2, waiting for transfers between devices: 428 us -> 69.7 us  [the longest x1 40.5 us: local(): lax.psum(lax.psum_scatter(grad_cols, 'fsdp', scatter_dimension=0, tiled=T...]
    all_gather x5 -> x6, waiting for transfers between devices: 504 us -> 190 us  [the longest x3 169 us: reduce_experts(): full = lax.all_gather(part, every, axis=0)]
    reduce_scatter x8 -> x6, waiting for transfers between devices: 640 us -> 363 us  [the longest x3 277 us: reduce_experts(): lax.psum_scatter(g, every, scatter_dimension=1, tiled=True, axis_index_gr...]
    scatter-add x48 -> x0, other arithmetic: 191 us -> none  [the longest x16 92.7 us: expert_step(): total = total.at[row_index].add(weight_col * expert_out)]
    pallas_call x0 -> x5, Pallas kernels: none -> 124 us  [the longest x1 67.5 us: experts(): pl.pallas_call(functools.partial(experts_kernel, tile=tile), grid_spec=pl...]
    ppermute x0 -> x21, waiting for transfers between devices: none -> 109 us  [the longest x3 44.2 us: scatter_fsdp(): other = lax.ppermute(x[n:], 'fsdp', [(0, 1), (1, 0)])]
    gather x48 -> x4, local copies, waits for them, and re-layouts: 93.6 us -> 2.32 us  [the longest x1 0.59 us: local(): d_heads = jnp.take(d_heads, relative, axis=0)]
  transfers between devices with their start and end apart: 21 -> 35, of which waited for: 16 -> 24; matrix products, arithmetic and copies ran while one was open for 6% -> 9% of each run, Pallas kernels for 0% -> 3%
where the time goes in v1:
time: 1130 us
  waiting for transfers between devices  733 us (65%)
  Pallas kernels  124 us (11%)
  blocking collectives  88.8 us (8%)
  other arithmetic  70.5 us (6%)
  local copies, waits for them, and re-layouts  68.8 us (6%)
  starting transfers between devices  17.8 us (2%)
  between operations  15.7 us (1%)
    reduce_scatter x3, waiting for transfers between devices, reduce_experts(): lax.psum_scatter(g, every, scatter_dimension=1, tiled=True, axis_index_gr...  277 us
    all_gather x3, waiting for transfers between devices, reduce_experts(): full = lax.all_gather(part, every, axis=0)  169 us
    pallas_call x1, Pallas kernels, experts(): pl.pallas_call(functools.partial(experts_kernel, tile=tile), grid_spec=pl...  67.5 us
    psum x1, blocking collectives, local(): lax.psum(lax.psum_scatter(tiny, 'fsdp', scatter_dimension=0, tiled=True),...  62.4 us
    reduce_scatter x1, waiting for transfers between devices, local(): lax.psum_scatter(grad_cols, 'fsdp', scatter_dimension=0, tiled=True)  49 us
    ppermute x3, waiting for transfers between devices, scatter_fsdp(): other = lax.ppermute(x[n:], 'fsdp', [(0, 1), (1, 0)])  44.2 us
    ppermute x3, waiting for transfers between devices, gather_fsdp(): lax.ppermute(x, 'fsdp', [(0, 1), (1, 0)])  43.6 us
    psum x1, waiting for transfers between devices, local(): lax.psum(lax.psum_scatter(grad_cols, 'fsdp', scatter_dimension=0, tiled=T...  40.5 us
  transfers between devices with their start and end apart: 35, of which 24 were waited for; matrix products, arithmetic and copies ran while one was open for 9% of the time, Pallas kernels for 3%

profile of v1, /device:TPU:0, one launch (start us, length us, event | category | flops | bytes accessed | tf_op | source)
XLA Modules:
  0.0 1127.3 jit_solution(6872544772607082750)
XLA Ops:
  18.1 26.4 %all_gather.33 = bf16[1024,18]{0,1:T(8,128)(2,1)S(1)} all-gather(bf16[512,18]{0,1:T(8,128)(2,1)S(1)} %pad_maximum_fusion.9), channel_id=1, replica_groups=mesh['dp'=4,'seq'=4,'fsdp'=2] {'fsdp'}, dimensions={0}, use_global_device_ids=true | all-gather | bytes 55296 | tf_op jit(solution)/shard_map/all_gather | solution.py:468
  61.5 27.7 %collective-permute-done.3 = bf16[1280,256]{1,0:T(8,128)(2,1)S(1)} collective-permute-done((bf16[1280,256]{1,0:T(8,128)(2,1)}, bf16[1280,256]{1,0:T(8,128)(2,1)S(1)}, u32[]{:S(2)}, u32[]{:S(2)}) %collective-permute-start.3) | collective-permute-done | bytes 655392 | tf_op jit(solution)/shard_map/ppermute | solution.py:455
  90.3 27.3 %attend.1 = (f32[1280,256]{1,0:T(8,128)}, f32[8,8,640]{2,1,0:T(8,128)}) custom-call(s32[8]{0:T(128)} %copy-done.25, s32[16]{0:T(128)} %reshape.365.ktab_ref, s32[1]{0:T(128)} %copy.136.len_ref, bf16[1280,256]{1,0:T(8,128)(2,1)} %get-tuple-element.26.q_ref, bf16[2560,256]{1,0:T(8,128)(2,1)} %copy-done.5), custom_call_target="tpu_custom_call" | custom-call | tf_op jit(solution)/shard_map/attend/pallas_call | solution.py:233
  139.2 15.8 %collective-permute-done.7 = bf16[320,1152]{1,0:T(8,128)(2,1)S(1)} collective-permute-done((bf16[320,1152]{1,0:T(8,128)(2,1)S(1)}, bf16[320,1152]{1,0:T(8,128)(2,1)S(1)}, u32[]{:S(2)}, u32[]{:S(2)}) %collective-permute-start.7) | collective-permute-done | bytes 737312 | tf_op jit(solution)/shard_map/ppermute | solution.py:455
  163.7 67.5 %experts.1 = (bf16[1280,1024]{1,0:T(8,128)(2,1)}, bf16[1280,1152]{1,0:T(8,128)(2,1)}, bf16[4,1024,512]{2,1,0:T(8,128)(2,1)}, bf16[4,1024,512]{2,1,0:T(8,128)(2,1)}, bf16[4,512,1024]{2,1,0:T(8,128)(2,1)}) custom-call(s32[2]{0:T(128)} %pad_add_fusion.base_ref, bf16[1280,1152]{1,0:T(8,128)(2,1)} %pad_maximum_fusion.h_ref, ...), custom_call_target="tpu_custom_call" | custom-call | tf_op jit(solution)/shard_map/experts/pallas_call | solution.py:400
  239.6 16.6 %collective-permute-done.14 = bf16[320,1152]{1,0:T(8,128)(2,1)S(1)} collective-permute-done((bf16[320,1152]{1,0:T(8,128)(2,1)S(1)}, bf16[320,1152]{1,0:T(8,128)(2,1)S(1)}, u32[]{:S(2)}, u32[]{:S(2)}) %collective-permute-start.14) | collective-permute-done | bytes 737312 | tf_op jit(solution)/shard_map/ppermute | solution.py:462
  257.4 12.3 %collective-permute-done.12 = bf16[320,1024]{1,0:T(8,128)(2,1)S(1)} collective-permute-done((bf16[320,1024]{1,0:T(8,128)(2,1)S(1)}, bf16[320,1024]{1,0:T(8,128)(2,1)S(1)}, u32[]{:S(2)}, u32[]{:S(2)}) %collective-permute-start.12) | collective-permute-done | bytes 655392 | tf_op jit(solution)/shard_map/ppermute | solution.py:462
  288.2 12.8 %attend_back.1 = (bf16[1280,256]{1,0:T(8,128)(2,1)}, bf16[2560,256]{1,0:T(8,128)(2,1)}) custom-call(s32[8]{0:T(128)} %copy-done.25, s32[16]{0:T(128)} %reshape.365.ktab_ref, s32[1]{0:T(128)} %copy.136.len_ref, bf16[1280,256]{1,0:T(8,128)(2,1)} %get-tuple-element.26.q_ref, bf16[2560,256]{1,0:T(8,128)(2,1)} %copy-done.5, ...), custom_call_target="tpu_custom_call" | custom-call | tf_op jit(solution)/shard_map/attend_back/pallas_call | solution.py:317
  305.4 15.4 %collective-permute-done.18 = bf16[1280,256]{1,0:T(8,128)(2,1)S(1)} collective-permute-done((bf16[1280,256]{1,0:T(8,128)(2,1)S(1)}, bf16[1280,256]{1,0:T(8,128)(2,1)S(1)}, u32[]{:S(2)}, u32[]{:S(2)}) %collective-permute-start.18) | collective-permute-done | bytes 655392 | tf_op jit(solution)/shard_map/ppermute | solution.py:462
  334.5 49.0 %reduce-scatter.9.cloned.1.call-done = bf16[512,512]{1,0:T(8,128)(2,1)} async-done(((bf16[1024,512]{1,0:T(8,128)(2,1)}), bf16[512,512]{1,0:T(8,128)(2,1)}) %reduce-scatter.9.cloned.1.call-update) | async-done | bytes 524304 | tf_op jit(solution)/shard_map/reduce_scatter | solution.py:624
  387.0 31.1 %reduce-scatter.11.cloned.1.call-done = bf16[512,1024]{1,0:T(8,128)(2,1)} async-done(((bf16[1024,1024]{1,0:T(8,128)(2,1)}), bf16[512,1024]{1,0:T(8,128)(2,1)}) %reduce-scatter.11.cloned.1.call-update) | async-done | bytes 1048592 | tf_op jit(solution)/shard_map/reduce_scatter | solution.py:621
  418.2 40.5 %all-reduce.3.cloned.1.call-done = bf16[1,512,512]{2,1,0:T(8,128)(2,1)} async-done(((bf16[1,512,512]{2,1,0:T(8,128)(2,1)}), bf16[1,512,512]{2,1,0:T(8,128)(2,1)}) %all-reduce.3.cloned.1.call-update) | async-done | bytes 524304 | tf_op jit(solution)/shard_map/psum | solution.py:623
  458.7 92.3 %reduce-scatter.17.cloned.1.call-done = bf16[4,64,1024]{2,1,0:T(8,128)(2,1)} async-done(((bf16[4,512,1024]{2,1,0:T(8,128)(2,1)}), bf16[4,64,1024]{2,1,0:T(8,128)(2,1)}) %reduce-scatter.17.cloned.1.call-update) | async-done | bytes 524304 | tf_op jit(solution)/shard_map/reduce_scatter | solution.py:610
  551.1 92.7 %reduce-scatter.15.cloned.1.call-done = bf16[4,128,512]{2,1,0:T(8,128)(2,1)} async-done(((bf16[4,1024,512]{2,1,0:T(8,128)(2,1)}), bf16[4,128,512]{2,1,0:T(8,128)(2,1)}) %reduce-scatter.15.cloned.1.call-update) | async-done | bytes 524304 | tf_op jit(solution)/shard_map/reduce_scatter | solution.py:610
  643.8 92.2 %reduce-scatter.13.cloned.1.call-done = bf16[4,128,512]{2,1,0:T(8,128)(2,1)} async-done(((bf16[4,1024,512]{2,1,0:T(8,128)(2,1)}), bf16[4,128,512]{2,1,0:T(8,128)(2,1)}) %reduce-scatter.13.cloned.1.call-update) | async-done | bytes 524304 | tf_op jit(solution)/shard_map/reduce_scatter | solution.py:610
  748.1 62.4 %psum.21 = f32[512,18]{0,1:T(8,128)S(1)} all-reduce(f32[512,18]{0,1:T(8,128)} %reduce-scatter.7.cloned.1.call-done), channel_id=1, replica_groups=mesh['dp'=4,'seq'=4,'fsdp'=2] {'dp','seq'}, use_global_device_ids=true, to_apply=%region_11.13 | all-reduce | flops 9216 | bytes 73728 | tf_op jit(solution)/shard_map/psum | solution.py:635
  815.8 29.2 %all-reduce.5.cloned.1.call-done = bf16[512,1024]{1,0:T(8,128)(2,1)} async-done(((bf16[512,1024]{1,0:T(8,128)(2,1)}), bf16[512,1024]{1,0:T(8,128)(2,1)}) %all-reduce.5.cloned.1.call-update) | async-done | bytes 1048592 | tf_op jit(solution)/shard_map/psum | solution.py:620
  847.8 20.7 %all-gather.14.cloned.1.call-done = bf16[4,512,512]{2,1,0:T(8,128)(2,1)} async-done(((bf16[1,512,512]{2,1,0:T(8,128)(2,1)}), bf16[4,512,512]{2,1,0:T(8,128)(2,1)}) %all-gather.14.cloned.1.call-update) | async-done | bytes 2097168 | tf_op jit(solution)/shard_map/all_gather | solution.py:626
  879.9 65.8 %all-gather.20.cloned.1.call-done = bf16[64,64,1024]{2,1,0:T(8,128)(2,1)} async-done(((bf16[4,64,1024]{2,1,0:T(8,128)(2,1)}), bf16[64,64,1024]{2,1,0:T(8,128)(2,1)}) %all-gather.20.cloned.1.call-update) | async-done | bytes 8388624 | tf_op jit(solution)/shard_map/all_gather | solution.py:613
  957.5 12.0 %copy.127 = f32[2,4,4,2,64,1024]{5,4,3,2,1,0:T(8,128)} copy(f32[2,4,4,2,64,1024]{5,4,1,0,3,2:T(8,128)} %convert_bitcast_fusion) | data formatting | bytes 33554432 | tf_op jit(solution)/shard_map/convert_element_type | solution.py:617
  969.5 51.8 %all-gather.18.cloned.1.call-done = bf16[64,128,512]{2,1,0:T(8,128)(2,1)} async-done(((bf16[4,128,512]{2,1,0:T(8,128)(2,1)}), bf16[64,128,512]{2,1,0:T(8,128)(2,1)}) %all-gather.18.cloned.1.call-update) | async-done | bytes 8388624 | tf_op jit(solution)/shard_map/all_gather | solution.py:613
  1033.2 12.0 %copy.126 = f32[2,4,4,2,128,512]{5,4,3,2,1,0:T(8,128)} copy(f32[2,4,4,2,128,512]{5,4,1,0,3,2:T(8,128)} %convert_bitcast_fusion.1) | data formatting | bytes 33554432 | tf_op jit(solution)/shard_map/convert_element_type | solution.py:617
  1045.3 51.4 %all-gather.16.cloned.1.call-done = bf16[64,128,512]{2,1,0:T(8,128)(2,1)} async-done(((bf16[4,128,512]{2,1,0:T(8,128)(2,1)}), bf16[64,128,512]{2,1,0:T(8,128)(2,1)}) %all-gather.16.cloned.1.call-update) | async-done | bytes 8388624 | tf_op jit(solution)/shard_map/all_gather | solution.py:613
  1108.3 12.0 %copy.125 = f32[2,4,4,2,128,512]{5,4,3,2,1,0:T(8,128)} copy(f32[2,4,4,2,128,512]{5,4,1,0,3,2:T(8,128)} %convert_bitcast_fusion.2) | data formatting | bytes 33554432 | tf_op jit(solution)/shard_map/convert_element_type | solution.py:617
  (246 shorter events, 174.6 us)
Async XLA Ops:
  7.2 43.5 %all-gather.10.cloned.1.call-start = ((), (), s32[]{:S(2)}) async-start(), calls=%async_computation.6 | async-start | bytes 1572864 | tf_op jit(solution)/shard_map/all_gather | solution.py:468
  7.2 41.6 %collective-permute-start = (bf16[320,1024]{1,0:T(8,128)(2,1)}, bf16[320,1024]{1,0:T(8,128)(2,1)S(1)}, u32[]{:S(2)}, u32[]{:S(2)}) collective-permute-start(bf16[320,1024]{1,0:T(8,128)(2,1)} %bitcast.114), channel_id=1, source_target_pairs={{0,2},{2,0},{4,6},{6,4},{1,3},{3,1},{5,7},{7,5},{8,10},{10,8},{12,... | collective-permute-start | bytes 1966088 | tf_op jit(solution)/shard_map/ppermute | solution.py:432
  7.7 36.8 %collective-permute-start.1 = (bf16[320,1024]{1,0:T(8,128)(2,1)}, bf16[320,1024]{1,0:T(8,128)(2,1)S(1)}, u32[]{:S(2)}, u32[]{:S(2)}) collective-permute-start(bf16[320,1024]{1,0:T(8,128)(2,1)} %bitcast.115), channel_id=1, source_target_pairs={{0,4},{4,0},{2,6},{6,2},{1,5},{5,1},{3,7},{7,3},{8,12},{12,8},{10,... | collective-permute-start | bytes 1966088 | tf_op jit(solution)/shard_map/ppermute | solution.py:436
  13.5 116.9 %all-gather.12.cloned.1.call-start = ((), (), s32[]{:S(2)}) async-start(), calls=%async_computation.7 | async-start | bytes 3145728 | tf_op jit(solution)/shard_map/all_gather | solution.py:468
  16.4 120.4 %collective-permute-start.9 = (bf16[320,1024]{1,0:T(8,128)(2,1)}, bf16[320,1024]{1,0:T(8,128)(2,1)}, u32[]{:S(2)}, u32[]{:S(2)}) collective-permute-start(bf16[320,1024]{1,0:T(8,128)(2,1)} %bitcast_select_fusion), channel_id=1, source_target_pairs={{0,1},{1,0},{2,3},{3,2},{4,5},{5,4},{6,7},{7,6},{8,9},{9,8},{10,11... | collective-permute-start | bytes 1966088 | tf_op jit(solution)/shard_map/ppermute | solution.py:455
  17.9 365.6 %reduce-scatter.9.cloned.1.call-start = ((), (), s32[]{:S(2)}) async-start(), calls=%async_computation.9 | async-start | bytes 1572864 | tf_op jit(solution)/shard_map/reduce_scatter | solution.py:624
  57.3 31.9 %collective-permute-start.3 = (bf16[1280,256]{1,0:T(8,128)(2,1)}, bf16[1280,256]{1,0:T(8,128)(2,1)S(1)}, u32[]{:S(2)}, u32[]{:S(2)}) collective-permute-start(bf16[1280,256]{1,0:T(8,128)(2,1)} %get-tuple-element.27), channel_id=1, source_target_pairs={{0,1},{1,0},{2,3},{3,2},{4,5},{5,4},{6,7},{7,6},{8,9},{9,8},{10,11... | collective-permute-start | bytes 1966088 | tf_op jit(solution)/shard_map/ppermute | solution.py:455
  136.7 18.4 %collective-permute-start.7 = (bf16[320,1152]{1,0:T(8,128)(2,1)S(1)}, bf16[320,1152]{1,0:T(8,128)(2,1)S(1)}, u32[]{:S(2)}, u32[]{:S(2)}) collective-permute-start(bf16[320,1152]{1,0:T(8,128)(2,1)S(1)} %concatenate.63), channel_id=1, source_target_pairs={{0,1},{1,0},{2,3},{3,2},{4,5},{5,4},{6,7},{7,6},{8,9},{9,8},{10,11... | collective-permute-start | bytes 2211848 | tf_op jit(solution)/shard_map/ppermute | solution.py:455
  139.2 17.8 %collective-permute-start.10 = (bf16[640,1024]{1,0:T(8,128)(2,1)}, bf16[640,1024]{1,0:T(8,128)(2,1)}, u32[]{:S(2)}, u32[]{:S(2)}) collective-permute-start(bf16[640,1024]{1,0:T(8,128)(2,1)} %pad_maximum_fusion.4), channel_id=1, source_target_pairs={{0,2},{2,0},{4,6},{6,4},{1,3},{3,1},{5,7},{7,5},{8,10},{10,8},{12,... | collective-permute-start | bytes 3932168 | tf_op jit(solution)/shard_map/ppermute | solution.py:432
  236.8 19.4 %collective-permute-start.14 = (bf16[320,1152]{1,0:T(8,128)(2,1)S(1)}, bf16[320,1152]{1,0:T(8,128)(2,1)S(1)}, u32[]{:S(2)}, u32[]{:S(2)}) collective-permute-start(bf16[320,1152]{1,0:T(8,128)(2,1)S(1)} %slice.173), channel_id=1, source_target_pairs={{0,1},{1,0},{2,3},{3,2},{4,5},{5,4},{6,7},{7,6},{8,9},{9,8},{10,11... | collective-permute-start | bytes 2211848 | tf_op jit(solution)/shard_map/ppermute | solution.py:462
  238.8 30.8 %collective-permute-start.12 = (bf16[320,1024]{1,0:T(8,128)(2,1)S(1)}, bf16[320,1024]{1,0:T(8,128)(2,1)S(1)}, u32[]{:S(2)}, u32[]{:S(2)}) collective-permute-start(bf16[320,1024]{1,0:T(8,128)(2,1)S(1)} %slice.171), channel_id=1, source_target_pairs={{0,1},{1,0},{2,3},{3,2},{4,5},{5,4},{6,7},{7,6},{8,9},{9,8},{10,11... | collective-permute-start | bytes 1966088 | tf_op jit(solution)/shard_map/ppermute | solution.py:462
  302.2 18.6 %collective-permute-start.18 = (bf16[1280,256]{1,0:T(8,128)(2,1)S(1)}, bf16[1280,256]{1,0:T(8,128)(2,1)S(1)}, u32[]{:S(2)}, u32[]{:S(2)}) collective-permute-start(bf16[1280,256]{1,0:T(8,128)(2,1)S(1)} %slice.134), channel_id=1, source_target_pairs={{0,1},{1,0},{2,3},{3,2},{4,5},{5,4},{6,7},{7,6},{8,9},{9,8},{10,11... | collective-permute-start | bytes 1966088 | tf_op jit(solution)/shard_map/ppermute | solution.py:462
  331.8 86.4 %reduce-scatter.11.cloned.1.call-start = ((), (), s32[]{:S(2)}) async-start(), calls=%async_computation.12 | async-start | bytes 3145728 | tf_op jit(solution)/shard_map/reduce_scatter | solution.py:621
  334.4 124.2 %all-reduce.3.cloned.1.call-start = ((), (), s32[]{:S(2)}) async-start(), calls=%async_computation.10 | async-start | bytes 1048576 | tf_op jit(solution)/shard_map/psum | solution.py:623
  383.6 167.5 %reduce-scatter.17.cloned.1.call-start = ((), (), s32[]{:S(2)}) async-start(), calls=%async_computation.16 | async-start | bytes 4718592 | tf_op jit(solution)/shard_map/reduce_scatter | solution.py:610
  384.1 259.6 %reduce-scatter.15.cloned.1.call-start = ((), (), s32[]{:S(2)}) async-start(), calls=%async_computation.15 | async-start | bytes 4718592 | tf_op jit(solution)/shard_map/reduce_scatter | solution.py:610
  384.9 351.2 %reduce-scatter.13.cloned.1.call-start = ((), (), s32[]{:S(2)}) async-start(), calls=%async_computation.14 | async-start | bytes 4718592 | tf_op jit(solution)/shard_map/reduce_scatter | solution.py:610
  385.6 362.5 %reduce-scatter.7.cloned.1.call-start = ((), (), s32[]{:S(2)}) async-start(), calls=%async_computation.8 | async-start | bytes 147456 | tf_op jit(solution)/shard_map/reduce_scatter | solution.py:635
  387.0 458.1 %all-reduce.5.cloned.1.call-start = ((), (), s32[]{:S(2)}) async-start(), calls=%async_computation.13 | async-start | bytes 2097152 | tf_op jit(solution)/shard_map/psum | solution.py:620
  418.2 450.4 %all-gather.14.cloned.1.call-start = ((), (), s32[]{:S(2)}) async-start(), calls=%async_computation.11 | async-start | bytes 2621440 | tf_op jit(solution)/shard_map/all_gather | solution.py:626
  458.7 487.0 %all-gather.20.cloned.1.call-start = ((), (), s32[]{:S(2)}) async-start(), calls=%async_computation.19 | async-start | bytes 8912896 | tf_op jit(solution)/shard_map/all_gather | solution.py:613
  551.1 470.2 %all-gather.18.cloned.1.call-start = ((), (), s32[]{:S(2)}) async-start(), calls=%async_computation.18 | async-start | bytes 8912896 | tf_op jit(solution)/shard_map/all_gather | solution.py:613
  643.8 452.9 %all-gather.16.cloned.1.call-start = ((), (), s32[]{:S(2)}) async-start(), calls=%async_computation.17 | async-start | bytes 8912896 | tf_op jit(solution)/shard_map/all_gather | solution.py:613
  740.7 71.0 %collective-permute-start.20 = (bf16[320,1024]{1,0:T(8,128)(2,1)}, bf16[320,1024]{1,0:T(8,128)(2,1)}, u32[]{:S(2)}, u32[]{:S(2)}) collective-permute-start(bf16[320,1024]{1,0:T(8,128)(2,1)} %fusion.11), channel_id=1, source_target_pairs={{0,4},{4,0},{2,6},{6,2},{1,5},{5,1},{3,7},{7,3},{8,12},{12,8},{10,... | collective-permute-start | bytes 1966088 | tf_op jit(solution)/shard_map/ppermute | solution.py:436
  (43 other events, 762.0 us)
Sparse Core Ops, SparseCore 0:
  13.7 31.6 all-gather.9
  46.9 47.4 all-gather.11
  331.9 51.5 reduce-scatter.8
  386.3 31.8 reduce-scatter.10
  420.3 38.2 all-reduce.2
  462.7 88.2 reduce-scatter.16
  555.7 88.0 reduce-scatter.14
  648.0 88.0 reduce-scatter.12
  738.3 9.7 reduce-scatter.6
  751.8 93.1 all-reduce.4
  846.7 21.8 all-gather.13
  870.8 74.8 all-gather.19
  948.1 73.1 all-gather.17
  1023.5 73.1 all-gather.15

commit v2 on v1

--- a/solution.py
+++ b/solution.py
@@ -339,7 +339,7 @@
 
 
 def experts_kernel(
-    base_ref, h_ref, c_ref, wg_ref, wu_ref, wd_ref, moe_ref, dh_ref, gg_ref, gu_ref, gd_ref,
+    base_ref, h_ref, c_ref, wg_ref, wu_ref, wd_ref, moe_ref, dh_ref, grad_ref,
     moe, dh, dgates, s_act, s_gate, s_up, *, tile,
 ):
     step = pl.program_id(0)
@@ -377,13 +377,12 @@
         moe[at, :] += mm(act, wd)
         dh[at, :] += mm_nt(dgate, wg) + mm_nt(dup, wu)
 
-    for i in range(4):
-        n = width // 4
-        gg_ref[0, i * n : (i + 1) * n, :] = mm_tn(h_ref[:, i * n : (i + 1) * n], s_gate[...]).astype(BF)
-        gu_ref[0, i * n : (i + 1) * n, :] = mm_tn(h_ref[:, i * n : (i + 1) * n], s_up[...]).astype(BF)
+    block = grad_ref.shape[2]
     for i in range(2):
-        n = wd.shape[0] // 2
-        gd_ref[0, i * n : (i + 1) * n, :] = mm_tn(s_act[:, i * n : (i + 1) * n], c_ref[...]).astype(BF)
+        at = slice(i * block, (i + 1) * block)
+        grad_ref[0, i] = mm_tn(h_ref[:, at], s_gate[...]).astype(BF)
+        grad_ref[0, 2 + i] = mm_tn(h_ref[:, at], s_up[...]).astype(BF)
+        grad_ref[0, 4 + i] = mm_tn(s_act[...], c_ref[:, at]).astype(BF)
 
     @pl.when(step == pl.num_programs(0) - 1)
     def _():
@@ -396,7 +395,6 @@
     rows, width = c.shape
     ff = wg.shape[2]
     pick = lambda shape: pl.BlockSpec((1,) + shape, lambda e, s: (s[0] + e, 0, 0))
-    put = lambda shape: pl.BlockSpec((1,) + shape, lambda e, s: (e, 0, 0))
     return pl.pallas_call(
         functools.partial(experts_kernel, tile=tile),
         grid_spec=pltpu.PrefetchScalarGridSpec(
@@ -408,7 +406,7 @@
             ],
             out_specs=[
                 whole(c.shape), whole(h.shape),
-                put((width, ff)), put((width, ff)), put((ff, width)),
+                pl.BlockSpec((1, 6, ff, ff), lambda e, s: (e, 0, 0, 0)),
             ],
             scratch_shapes=[
                 pltpu.VMEM((rows, width), F32), pltpu.VMEM((rows, width), F32),
@@ -419,9 +417,7 @@
         out_shape=[
             jax.ShapeDtypeStruct(c.shape, BF),
             jax.ShapeDtypeStruct(h.shape, BF),
-            jax.ShapeDtypeStruct((count, width, ff), BF),
-            jax.ShapeDtypeStruct((count, width, ff), BF),
-            jax.ShapeDtypeStruct((count, ff, width), BF),
+            jax.ShapeDtypeStruct((count, 6, ff, ff), BF),
         ],
         compiler_params=params(),
         name="experts",
@@ -438,6 +434,10 @@
 
 def flip_both(x):
     return lax.ppermute(x, "seq", [(0, 3), (3, 0), (1, 2), (2, 1)])
+
+
+def flip_y(x):
+    return lax.ppermute(x, "fsdp", [(0, 1), (1, 0)])
 
 
 def gather_seq(x):
@@ -462,6 +462,296 @@
         other = lax.ppermute(x[n:], "fsdp", [(0, 1), (1, 0)])
         return x[:n].astype(F32) + other.astype(F32)
     return lax.psum_scatter(x, "fsdp", scatter_dimension=0, tiled=True).astype(F32)
+
+
+MESH = pl.DeviceIdType.MESH
+
+
+def reduce_kernel(
+    gm, eo, cols, tiny, gate, up, down, out, qkv, tiny_out,
+    mine, rc, pre, suf, oth, far, faro, stage, trecv,
+    s_mine, s_rc, s_pre, s_suf, s_oth, s_far, s_faro, s_out, s_tiny,
+    *, slots, groups, shards,
+):
+    z, s, f = lax.axis_index("dp"), lax.axis_index("seq"), lax.axis_index("fsdp")
+    core, x = s % 2, s // 2
+    peer_core = (z, s + 1 - 2 * core, f)
+    peer_x = (z, (s + 2) % 4, f)
+    right, left = (z + 1, s, f), (z - 1, s, f)
+    nb = gm.shape[0]
+    items = nb + 3
+    count = nb // 6
+    half = mine.shape[1]
+    ndev = slots * groups * shards
+    me = (z * groups + s) * shards + f
+
+    barrier = pltpu.get_barrier_semaphore()
+
+    def other(k):
+        q = (me + k) % ndev
+        return q // (groups * shards), (q // shards) % groups, q % shards
+
+    @pl.loop(1, ndev)
+    def _(k):
+        pl.semaphore_signal(barrier, inc=1, device_id=other(k), device_id_type=MESH)
+
+    def remote(src, dst, sems, b, dev):
+        return pltpu.make_async_remote_copy(
+            src_ref=src, dst_ref=dst, send_sem=sems.at[0, b], recv_sem=sems.at[1, b],
+            device_id=dev, device_id_type=MESH,
+        )
+
+    def load(src, b):
+        return pltpu.make_async_copy(src, mine.at[b], s_mine.at[b])
+
+    @pl.loop(0, nb)
+    def _(b):
+        load(gm.at[b, core], b).start()
+
+    load(eo.at[core], nb).start()
+    load(cols.at[0], nb + 1).start()
+    load(cols.at[1], nb + 2).start()
+    pl.semaphore_wait(barrier, ndev - 1)
+
+    @pl.loop(0, nb)
+    def _(b):
+        remote(gm.at[b, 1 - core], rc.at[b], s_rc, b, peer_core).start()
+
+    remote(eo.at[1 - core], rc.at[nb], s_rc, nb, peer_core).start()
+
+    def tiny_copy(k):
+        dev = other(k)
+        return remote(tiny.at[dev[2]], trecv.at[k], s_tiny, k, dev)
+
+    @pl.loop(1, ndev)
+    def _(k):
+        tiny_copy(k).start()
+
+    def emit(kind, b, ref):
+        slot = kind * 2 + b % 2
+        drained = pltpu.make_async_copy(
+            stage.at[slot], gate.at[0, pl.ds(0, half), :], s_out.at[slot]
+        )
+
+        @pl.when(b >= 2)
+        def _():
+            drained.wait()
+
+        which = x if kind < 2 else 1 - x
+        part = core if kind % 2 == 0 else 1 - core
+        rows = pl.ds(pl.multiple_of(part * half, half), half)
+        e, j = which * count + b // 6, b % 6
+        jj = j % 2
+
+        def put(src, dst):
+            pltpu.make_async_copy(src, dst, s_out.at[slot]).start()
+
+        @pl.when(b <= nb)
+        def _():
+            stage[slot] = ref[b].astype(F32)
+
+        for m, o in enumerate((gate, up)):
+            @pl.when((b < nb) & (j // 2 == m))
+            def _():
+                at = pl.multiple_of(jj * 2 * half + part * half, half)
+                put(stage.at[slot], o.at[e, pl.ds(at, half), :])
+
+        wide = pl.ds(pl.multiple_of(jj * 2 * half, 2 * half), 2 * half)
+
+        @pl.when((b < nb) & (j // 2 == 2))
+        def _():
+            put(stage.at[slot], down.at[e, rows, wide])
+
+        @pl.when(b == nb)
+        def _():
+            put(stage.at[slot], out.at[rows, pl.ds(pl.multiple_of(which * 2 * half, 2 * half), 2 * half)])
+
+        @pl.when(b > nb)
+        def _():
+            v = ref[b].astype(F32)
+            mid = v[:, 64:192]
+            low = lax.broadcasted_iota(jnp.int32, (half, 128), 1) < 64
+            stage[slot, :, :128] = jnp.where(low, v[:, :128], mid)
+            stage[slot, :, 128:256] = jnp.where(low, mid, v[:, 128:256])
+            stage[slot, :, 256:] = v[:, 256:]
+            owner = 2 * which + part
+            at = pl.ds(pl.multiple_of((b - nb - 1) * half, half), half)
+            put(stage.at[slot, :, pl.ds(0, 256)], qkv.at[at, pl.ds(pl.multiple_of(owner * 256, 256), 256)])
+            put(stage.at[slot, :, pl.ds(256, 128)], qkv.at[at, pl.ds(pl.multiple_of(1024 + owner * 128, 128), 128)])
+            put(stage.at[slot, :, pl.ds(384, 128)], qkv.at[at, pl.ds(pl.multiple_of(1536 + owner * 128, 128), 128)])
+
+    def add(a, b):
+        return a.astype(F32) + b.astype(F32)
+
+    def hop(buf, sems, b, dev):
+        return remote(buf.at[b], buf.at[b], sems, b, dev)
+
+    def spread(b):
+        remote(rc.at[b], oth.at[b], s_oth, b, peer_core).start()
+        remote(rc.at[b], far.at[b], s_far, b, peer_x).start()
+        emit(0, b, rc)
+
+    last = slots - 1
+    lag = 2
+
+    def begin(b):
+        load(gm.at[0, 0], b).wait()
+
+        @pl.when(b <= nb)
+        def _():
+            remote(gm.at[0, 0], rc.at[b], s_rc, b, peer_core).wait_recv()
+            mine[b] = add(mine[b], rc[b]).astype(BF)
+
+        @pl.when(z == 0)
+        def _():
+            remote(mine.at[b], pre.at[b], s_pre, b, right).start()
+
+        @pl.when(z == last)
+        def _():
+            remote(mine.at[b], suf.at[b], s_suf, b, left).start()
+
+    def prefix(b):
+        hop(pre, s_pre, b, peer_x).wait_recv()
+        got = pre[b].astype(F32)
+        own = got + mine[b].astype(F32)
+
+        @pl.when(z == last)
+        def _():
+            rc[b] = own.astype(BF)
+
+        @pl.when(z < last)
+        def _():
+            @pl.when(2 * z >= slots)
+            def _():
+                rc[b] = (got + suf[b].astype(F32)).astype(BF)
+
+            pre[b] = own.astype(BF)
+            hop(pre, s_pre, b, right).start()
+
+        @pl.when(2 * z >= slots)
+        def _():
+            spread(b)
+
+    def suffix(b):
+        hop(suf, s_suf, b, peer_x).wait_recv()
+        got = suf[b].astype(F32)
+        own = got + mine[b].astype(F32)
+
+        @pl.when(z == 0)
+        def _():
+            rc[b] = own.astype(BF)
+
+        @pl.when(z > 0)
+        def _():
+            @pl.when(2 * z < slots)
+            def _():
+                rc[b] = (got + pre[b].astype(F32)).astype(BF)
+
+            suf[b] = own.astype(BF)
+            hop(suf, s_suf, b, left).start()
+
+        @pl.when(2 * z < slots)
+        def _():
+            spread(b)
+
+    def forward(b):
+        hop(far, s_far, b, peer_x).wait_recv()
+        remote(far.at[b], faro.at[b], s_faro, b, peer_core).start()
+        emit(2, b, far)
+
+    def finish(b):
+        hop(oth, s_oth, b, peer_core).wait_recv()
+        emit(1, b, oth)
+        hop(faro, s_faro, b, peer_core).wait_recv()
+        emit(3, b, faro)
+
+    def within(b, cond=True):
+        return (b >= 0) & (b < items) & cond
+
+    @pl.loop(0, items + (last + 2) * lag)
+    def _(i):
+        for fn, b, cond in (
+            (begin, i, True),
+            (prefix, i - lag * z, z > 0),
+            (suffix, i - lag * (last - z), z < last),
+            (forward, i - lag * (last + 1), True),
+            (finish, i - lag * (last + 2), True),
+        ):
+            @pl.when(within(b, cond))
+            def _():
+                fn(b)
+
+    own = tiny[f].astype(F32)
+    trecv[0] = tiny[f]
+
+    @pl.loop(1, ndev)
+    def _(k):
+        tiny_copy(k).wait()
+
+    tiny_out[...] = lax.fori_loop(
+        1, ndev, lambda k, t: t + trecv[k].astype(F32), own
+    )
+
+    @pl.loop(0, items)
+    def _(b):
+        @pl.when(b <= nb)
+        def _():
+            remote(rc.at[b], rc.at[b], s_rc, b, peer_core).wait_send()
+
+        @pl.when(z < last)
+        def _():
+            hop(pre, s_pre, b, peer_x).wait_send()
+
+        @pl.when(z > 0)
+        def _():
+            hop(suf, s_suf, b, peer_x).wait_send()
+
+        hop(oth, s_oth, b, peer_core).wait_send()
+        hop(far, s_far, b, peer_x).wait_send()
+        hop(faro, s_faro, b, peer_core).wait_send()
+
+    @pl.loop(0, 8)
+    def _(slot):
+        pltpu.make_async_copy(
+            stage.at[slot], gate.at[0, pl.ds(0, half), :], s_out.at[slot]
+        ).wait()
+
+
+def reduce_grads(gm, eo, cols, tiny, slots, groups, shards):
+    count, _, ff, _ = gm.shape
+    width = 2 * ff
+    nb = 6 * count
+    half = ff // 2
+    items = nb + 3
+    ndev = slots * groups * shards
+    buf = lambda: pltpu.VMEM((items, half, ff), BF)
+    sems = lambda n: pltpu.SemaphoreType.DMA((2, n))
+    hbm = pl.BlockSpec(memory_space=pl.ANY)
+    vmem = pl.BlockSpec(memory_space=pltpu.VMEM)
+    return pl.pallas_call(
+        functools.partial(reduce_kernel, slots=slots, groups=groups, shards=shards),
+        in_specs=[hbm, hbm, hbm, vmem],
+        out_specs=[hbm] * 5 + [vmem],
+        out_shape=[
+            jax.ShapeDtypeStruct((2 * count, width, ff), F32),
+            jax.ShapeDtypeStruct((2 * count, width, ff), F32),
+            jax.ShapeDtypeStruct((2 * count, ff, width), F32),
+            jax.ShapeDtypeStruct((ff, width), F32),
+            jax.ShapeDtypeStruct((ff, 2 * width), F32),
+            jax.ShapeDtypeStruct(tiny.shape[1:], F32),
+        ],
+        scratch_shapes=[
+            buf(), buf(), buf(), buf(), buf(), buf(), buf(),
+            pltpu.VMEM((8, half, ff), F32),
+            pltpu.VMEM((ndev,) + tiny.shape[1:], BF),
+            pltpu.SemaphoreType.DMA((items,)),
+            sems(items), sems(items), sems(items), sems(items), sems(items), sems(items),
+            pltpu.SemaphoreType.DMA((8,)),
+            sems(ndev),
+        ],
+        compiler_params=params(collective_id=1, has_side_effects=True),
+        name="reduce_grads",
+    )(gm.reshape(nb, 2, half, ff), eo.reshape(2, half, ff), cols.reshape(2, half, ff), tiny)
 
 
 def gather_rows(x):
@@ -477,7 +767,7 @@
     slots = lax.axis_size("dp")
     assert groups == 4
     seq, fsdp = lax.axis_index("seq"), lax.axis_index("fsdp")
-    core = seq % 2
+    core, far = seq % 2, seq // 2
     rows, width = tokens.shape[1:]
     span = rows // 2
     x = tokens[0]
@@ -542,15 +832,19 @@
     masked_cot = jnp.where(own_valid, cotangent[0], jnp.zeros_like(cotangent[0]))
 
     def share(v):
-        near = gather_fsdp(v)
-        return jnp.concatenate([near, flip_core(near)])
+        if shards != 2:
+            near = gather_fsdp(v)
+            return jnp.concatenate([near, flip_x(near)])
+        n = rows // 2
+        up, over = flip_y(v), flip_x(v)
+        return jnp.concatenate([v, up, over, flip_y(over[:n]), flip_x(up[n:])])
 
     cot_all = share(masked_cot)
     extended = jnp.concatenate(
         [hidden_two, gates.astype(BF), jnp.zeros((rows, 128 - n_experts), BF)], axis=1
     )
     hid_all = share(extended)
-    base = jnp.stack([core * count, fsdp * owned + core * count]).astype(jnp.int32)
+    base = jnp.stack([far * count, fsdp * owned + far * count]).astype(jnp.int32)
     part = rows * 4
     moe_parts, dh_parts, weight_grads = [], [], None
     for i in range(hid_all.shape[0] // part):
@@ -561,16 +855,22 @@
         moe_parts.append(got[0])
         dh_parts.append(got[1])
         if weight_grads is None:
-            weight_grads = list(got[2:])
+            weight_grads = got[2]
         else:
-            weight_grads = [a.astype(F32) + b.astype(F32) for a, b in zip(weight_grads, got[2:])]
-            weight_grads = [a.astype(BF) for a in weight_grads]
+            weight_grads = (weight_grads.astype(F32) + got[2].astype(F32)).astype(BF)
 
     def give_back(parts):
         v = jnp.concatenate(parts) if len(parts) > 1 else parts[0]
-        n = v.shape[0] // 2
-        near = v[:n].astype(F32) + flip_core(v[n:]).astype(F32)
-        return scatter_fsdp(near.astype(BF))
+        if shards != 2:
+            n = v.shape[0] // 2
+            near = v[:n].astype(F32) + flip_x(v[n:]).astype(F32)
+            return scatter_fsdp(near.astype(BF))
+        v = v.reshape(4, 2, rows // 2, v.shape[1])
+        first = v[:2, 0].astype(F32) + flip_x(v[2:, 0]).astype(F32)
+        second = v[0::2, 1].astype(F32) + flip_y(v[1::2, 1]).astype(F32)
+        first = first[0] + flip_y(first[1].astype(BF)).astype(F32)
+        second = second[0] + flip_x(second[1].astype(BF)).astype(F32)
+        return jnp.concatenate([first, second])
 
     d_ext = give_back(dh_parts)
     d_gates = d_ext[:, width : width + n_experts]
@@ -603,39 +903,36 @@
         d_n - normed_one * jnp.mean(d_n * normed_one, axis=-1, keepdims=True)
     )
 
-    every = ("dp", "seq")
-    fold = [[d * groups + 2 * i + c for d in range(slots) for i in range(groups // 2)] for c in range(2)]
-
-    def reduce_experts(g):
-        part = lax.psum_scatter(
-            g, every, scatter_dimension=1, tiled=True, axis_index_groups=fold
-        )
-        full = lax.all_gather(part, every, axis=0)
-        n, r, m = part.shape
-        full = full.reshape(slots, groups // 2, 2, n, r, m)
-        full = jnp.transpose(full, (2, 3, 0, 1, 4, 5))
-        return full.reshape(2 * n, slots * groups // 2 * r, m).astype(F32)
-
-    grad_gate, grad_up, grad_down = [reduce_experts(g) for g in weight_grads]
-    shard_out = lax.psum(
-        lax.psum_scatter(grad_out, "fsdp", scatter_dimension=0, tiled=True), every
-    ).astype(F32)
-    shard_cols = lax.psum(
-        lax.psum_scatter(grad_cols, "fsdp", scatter_dimension=0, tiled=True), "dp"
-    )
-    cols = lax.all_gather(shard_cols, "seq", axis=0)
-    gq = cols[:, :, :qw].reshape(groups, -1, 2, 2, HEAD_WIDTH)
-    gq = jnp.transpose(gq, (1, 0, 3, 2, 4)).reshape(-1, groups * qw)
-    gk = jnp.transpose(cols[:, :, qw : qw + kw], (1, 0, 2)).reshape(-1, groups * kw)
-    gv = jnp.transpose(cols[:, :, qw + kw :], (1, 0, 2)).reshape(-1, groups * kw)
-    shard_qkv = jnp.concatenate([gq, gk, gv], axis=1).astype(F32)
+    block = w_gate.shape[2]
+
+    def to_owner(g):
+        if shards == 2:
+            half = g.reshape(2, -1, g.shape[1])
+            kept = lax.dynamic_index_in_dim(half, fsdp, 0, keepdims=False)
+            sent = lax.dynamic_index_in_dim(half, 1 - fsdp, 0, keepdims=False)
+            return (kept.astype(F32) + flip_y(sent).astype(F32)).astype(BF)
+        part = lax.psum_scatter(g, "fsdp", scatter_dimension=0, tiled=True)
+        return jnp.pad(part, ((0, block - part.shape[0]), (0, 0)))
+
+    shard_rows = width // shards
+    cols = to_owner(grad_cols)
+    mine = to_owner(grad_out).reshape(block, 2, block)
+    kept = lax.dynamic_index_in_dim(mine, far, 1, keepdims=False)
+    sent = lax.dynamic_index_in_dim(mine, 1 - far, 1, keepdims=False)
+    outs = (kept.astype(F32) + flip_x(sent).astype(F32)).astype(BF)
     tiny = jnp.concatenate(
-        [jnp.sum(grad_norm1, axis=0)[:, None], grad_norm2[:, None], grad_router], axis=1
-    )
-    tiny = lax.psum(lax.psum_scatter(tiny, "fsdp", scatter_dimension=0, tiled=True), every)
+        [jnp.sum(grad_norm1, axis=0)[None], grad_norm2[None], jnp.transpose(grad_router),
+         jnp.zeros((14, width), F32)]
+    )
+    tiny = jnp.transpose(tiny.reshape(32, shards, shard_rows), (1, 0, 2)).astype(BF)
+    grad_gate, grad_up, grad_down, shard_out, shard_qkv, tiny = reduce_grads(
+        weight_grads, outs, cols, tiny, slots, groups, shards
+    )
+    shard_out, shard_qkv = shard_out[:shard_rows], shard_qkv[:shard_rows]
+    tiny = jnp.transpose(tiny)
     layer_out = (middle + give_back(moe_parts)).astype(BF)
     return (
-        layer_out[None], d_inputs[None], tiny[:, 0], shard_qkv, shard_out, tiny[:, 1], tiny[:, 2:],
+        layer_out[None], d_inputs[None], tiny[:, 0], shard_qkv, shard_out, tiny[:, 1], tiny[:, 2 : 2 + n_experts],
         grad_gate, grad_up, grad_down,
     )
 

time: 1130 us -> 673 us (0.60)
  waiting for transfers between devices: 733 us -> 127 us
  Pallas kernels: 124 us -> 362 us
  blocking collectives: 88.8 us -> 14.5 us
  other arithmetic: 70.5 us -> 28.4 us
  local copies, waits for them, and re-layouts: 68.8 us -> 88.5 us
    reduce_scatter x6 -> x0, waiting for transfers between devices: 363 us -> none  [the longest x3 277 us: reduce_experts(): lax.psum_scatter(g, every, scatter_dimension=1, tiled=True, axis_index_gr...]
    pallas_call x0 -> x1, Pallas kernels: none -> 205 us  [reduce_grads(): pl.pallas_call(functools.partial(reduce_kernel, slots=slots, groups=group...]
    all_gather x4 -> x0, waiting for transfers between devices: 190 us -> none  [the longest x3 169 us: reduce_experts(): full = lax.all_gather(part, every, axis=0)]
    psum x2 -> x0, waiting for transfers between devices: 69.7 us -> none  [the longest x1 40.5 us: local(): lax.psum(lax.psum_scatter(grad_cols, 'fsdp', scatter_dimension=0, tiled=T...]
    psum x1 -> x0, blocking collectives: 62.4 us -> none  [local(): lax.psum(lax.psum_scatter(tiny, 'fsdp', scatter_dimension=0, tiled=True),...]
    unnamed x68 -> x101, local copies, waits for them, and re-layouts: 9.55 us -> 51.4 us
    ppermute x4 -> x13, waiting for transfers between devices: 6.7 us -> 45.4 us  [flip_x(): return lax.ppermute(x, 'seq', [(0, 2), (2, 0), (1, 3), (3, 1)])]
    convert_element_type x7 -> x4, other arithmetic: 41.6 us -> 4.2 us  [the longest x2 2.59 us: to_owner(): return (kept.astype(F32) + flip_y(sent).astype(F32)).astype(BF)]
  transfers between devices with their start and end apart: 35 -> 34, of which waited for: 24 -> 20; matrix products, arithmetic and copies ran while one was open for 9% -> 10% of each run, Pallas kernels for 3% -> 38%
where the time goes in v2:
time: 673 us; the launch traced here: 669 us
  Pallas kernels  362 us (54%)
  waiting for transfers between devices  127 us (19%)
  local copies, waits for them, and re-layouts  88.5 us (13%)
  other arithmetic  28.4 us (4%)
  starting transfers between devices  27.1 us (4%)
  between operations  15.4 us (2%)
  blocking collectives  14.5 us (2%)
  matrix products  6.91 us (1%)
    pallas_call x1, Pallas kernels, reduce_grads(): pl.pallas_call(functools.partial(reduce_kernel, slots=slots, groups=group...  205 us
    pallas_call x1, Pallas kernels, experts(): pl.pallas_call(functools.partial(experts_kernel, tile=tile), grid_spec=pl...  67.5 us
    unnamed x101, local copies, waits for them, and re-layouts  51.4 us
    ppermute x13, waiting for transfers between devices, flip_x(): return lax.ppermute(x, 'seq', [(0, 2), (2, 0), (1, 3), (3, 1)])  45.4 us
    pallas_call x1, Pallas kernels, attend_back(): pl.pallas_call(functools.partial(attend_back_kernel, span=span, kb=kb), g...  37.3 us
    ppermute x10, waiting for transfers between devices, flip_y(): return lax.ppermute(x, 'fsdp', [(0, 1), (1, 0)])  36.5 us
    pallas_call x1, Pallas kernels, attend(): pl.pallas_call(functools.partial(attend_kernel, span=span, kb=kb), grid_s...  35.8 us
    ppermute x1, waiting for transfers between devices, gather_fsdp(): lax.ppermute(x, 'fsdp', [(0, 1), (1, 0)])  26.5 us
  transfers between devices with their start and end apart: 34, of which 20 were waited for; matrix products, arithmetic and copies ran while one was open for 10% of the time, Pallas kernels for 38%

profile of v2, /device:TPU:0, one launch (start us, length us, event | category | flops | bytes accessed | tf_op | source)
XLA Modules:
  0.0 669.3 jit_solution(12390953277274330757)
XLA Ops:
  18.6 7.6 %collective-permute-done.1 = bf16[320,1024]{1,0:T(8,128)(2,1)} collective-permute-done((bf16[320,1024]{1,0:T(8,128)(2,1)}, bf16[320,1024]{1,0:T(8,128)(2,1)}, u32[]{:S(2)}, u32[]{:S(2)}) %collective-permute-start.1) | collective-permute-done | bytes 655392 | tf_op jit(solution)/shard_map/ppermute | solution.py:432
  29.9 14.5 %all_gather.9 = bf16[1024,18]{0,1:T(8,128)(2,1)S(1)} all-gather(bf16[512,18]{0,1:T(8,128)(2,1)S(1)} %pad_maximum_fusion.5), channel_id=1, replica_groups=mesh['dp'=4,'seq'=4,'fsdp'=2] {'fsdp'}, dimensions={0}, use_global_device_ids=true | all-gather | bytes 55296 | tf_op jit(solution)/shard_map/all_gather | solution.py:758
  49.0 6.5 project.1
  59.8 26.5 %collective-permute-done.3 = bf16[1280,256]{1,0:T(8,128)(2,1)} collective-permute-done((bf16[1280,256]{1,0:T(8,128)(2,1)}, bf16[1280,256]{1,0:T(8,128)(2,1)}, u32[]{:S(2)}, u32[]{:S(2)}) %collective-permute-start.3) | collective-permute-done | bytes 655392 | tf_op jit(solution)/shard_map/ppermute | solution.py:455
  88.5 35.8 %attend.1 = (f32[1280,256]{1,0:T(8,128)}, f32[8,8,640]{2,1,0:T(8,128)}) custom-call(s32[8]{0:T(128)} %copy-done.31, s32[16]{0:T(128)} %reshape.387.ktab_ref, s32[1]{0:T(128)} %copy.145.len_ref, bf16[1280,256]{1,0:T(8,128)(2,1)} %get-tuple-element.30.q_ref, bf16[2560,256]{1,0:T(8,128)(2,1)} %copy-done.5), custom_call_target="tpu_custom_call" | custom-call | tf_op jit(solution)/shard_map/attend/pallas_call | solution.py:233
  133.1 3.4 collective-permute-done.5
  153.8 11.4 %collective-permute-done.8 = bf16[320,1152]{1,0:T(8,128)(2,1)S(1)} collective-permute-done((bf16[320,1152]{1,0:T(8,128)(2,1)S(1)}, bf16[320,1152]{1,0:T(8,128)(2,1)S(1)}, u32[]{:S(2)}, u32[]{:S(2)}) %collective-permute-start.8) | collective-permute-done | bytes 737312 | tf_op jit(solution)/shard_map/ppermute | solution.py:432
  168.9 6.4 collective-permute-done.9
  177.2 67.5 %experts.1 = (bf16[1280,1024]{1,0:T(8,128)(2,1)}, bf16[1280,1152]{1,0:T(8,128)(2,1)}, bf16[4,6,512,512]{3,2,1,0:T(8,128)(2,1)}) custom-call(s32[2]{0:T(128)} %pad_add_fusion.base_ref, bf16[1280,1152]{1,0:T(8,128)(2,1)} %constant_dynamic-update-slice_fusion.2.h_ref, bf16[1280,1024]{1,0:T(8,128)(2,1)} %constant_dynamic-update-slice_fusion.7.c_ref, ...), custom_call_target="tpu_custom_call" | custom-call | tf_op jit(solution)/shard_map/experts/pallas_call | solution.py:398
  251.8 11.9 %collective-permute-done.15 = bf16[2,160,1024]{2,1,0:T(8,128)(2,1)S(1)} collective-permute-done((bf16[2,160,1024]{2,1,0:T(8,128)(2,1)S(1)}, bf16[2,160,1024]{2,1,0:T(8,128)(2,1)S(1)}, u32[]{:S(2)}, u32[]{:S(2)}) %collective-permute-start.15) | collective-permute-done | bytes 655392 | tf_op jit(solution)/shard_map/ppermute | solution.py:432
  267.3 13.2 %collective-permute-done.21 = bf16[2,160,1152]{2,1,0:T(8,128)(2,1)S(1)} collective-permute-done((bf16[2,160,1152]{2,1,0:T(8,128)(2,1)S(1)}, bf16[2,160,1152]{2,1,0:T(8,128)(2,1)S(1)}, u32[]{:S(2)}, u32[]{:S(2)}) %collective-permute-start.21) | collective-permute-done | bytes 737312 | tf_op jit(solution)/shard_map/ppermute | solution.py:440
  282.8 3.8 collective-permute-done.18
  287.6 6.3 collective-permute-done.20
  306.7 4.6 collective-permute-done.25
  314.2 37.3 %attend_back.1 = (bf16[1280,256]{1,0:T(8,128)(2,1)}, bf16[2560,256]{1,0:T(8,128)(2,1)}) custom-call(s32[8]{0:T(128)} %copy-done.31, s32[16]{0:T(128)} %reshape.387.ktab_ref, s32[1]{0:T(128)} %copy.145.len_ref, bf16[1280,256]{1,0:T(8,128)(2,1)} %get-tuple-element.30.q_ref, bf16[2560,256]{1,0:T(8,128)(2,1)} %copy-done.5, ...), custom_call_target="tpu_custom_call" | custom-call | tf_op jit(solution)/shard_map/attend_back/pallas_call | solution.py:317
  358.3 13.1 %collective-permute-done.26 = bf16[1280,256]{1,0:T(8,128)(2,1)} collective-permute-done((bf16[1280,256]{1,0:T(8,128)(2,1)}, bf16[1280,256]{1,0:T(8,128)(2,1)}, u32[]{:S(2)}, u32[]{:S(2)}) %collective-permute-start.26) | collective-permute-done | bytes 655392 | tf_op jit(solution)/shard_map/ppermute | solution.py:462
  373.9 9.7 %project_back.1 = (bf16[1280,1024]{1,0:T(8,128)(2,1)}, bf16[1024,512]{1,0:T(8,128)(2,1)}, f32[8,1024]{1,0:T(8,128)}) custom-call(bf16[1280,1024]{1,0:T(8,128)(2,1)} %bitcast.177, bf16[1280,1024]{1,0:T(8,128)(2,1)} %get-tuple-element.35.h_ref, bf16[1280,256]{1,0:T(8,128)(2,1)} %get-tuple-element.37.dq_ref, f32[1280,256]{1,0:T(8,128)} %convert_add_fusion.7.dkv_ref, ...), custom_call_target="tpu_custom_call" | custom-call | tf_op jit(solution)/shard_map/project_back/pallas_call | solution.py:135
  389.2 4.7 collective-permute-done.29
  400.9 3.9 collective-permute-done.31
  405.7 5.0 collective-permute-done.30
  413.6 205.2 %reduce_grads.1 = (f32[8,1024,512]{2,1,0:T(8,128)}, f32[8,1024,512]{2,1,0:T(8,128)}, f32[8,512,1024]{2,1,0:T(8,128)}, f32[512,1024]{1,0:T(8,128)}, f32[512,2048]{1,0:T(8,128)}, /*index=5*/f32[32,512]{1,0:T(8,128)}) custom-call(bf16[24,2,256,512]{3,2,1,0:T(8,128)(2,1)} %bitcast.184, bf16[2,256,512]{2,1,0:T(8,128)(2,1)} %bitcast.202, ...), custom_call_target="tpu_custom_call" | custom-call | tf_op jit(solution)/shard_map/reduce_grads/pallas_call | solution.py:731
  630.4 14.1 %copy.148 = f32[8,1024,512]{2,1,0:T(8,128)} copy(f32[8,1024,512]{2,1,0:T(8,128)} %get-tuple-element.121) | data formatting | bytes 33554432
  645.0 8.5 %copy.149 = f32[8,1024,512]{2,1,0:T(8,128)} copy(f32[8,1024,512]{2,1,0:T(8,128)S(1)} %bitcast.183) | data formatting | bytes 33554432
  656.3 6.2 copy.150
  (275 shorter events, 126.9 us)
Async XLA Ops:
  7.2 41.8 %all-gather.3.cloned.1.call-start = ((), (), s32[]{:S(2)}) async-start(), calls=%async_computation | async-start | bytes 1572864 | tf_op jit(solution)/shard_map/all_gather | solution.py:758
  7.2 38.4 %collective-permute-start = (bf16[320,1024]{1,0:T(8,128)(2,1)}, bf16[320,1024]{1,0:T(8,128)(2,1)}, u32[]{:S(2)}, u32[]{:S(2)}) collective-permute-start(bf16[320,1024]{1,0:T(8,128)(2,1)} %bitcast.178), channel_id=1, source_target_pairs={{0,2},{2,0},{4,6},{6,4},{1,3},{3,1},{5,7},{7,5},{8,10},{10,8},{12,... | collective-permute-start | bytes 1966088 | tf_op jit(solution)/shard_map/ppermute | solution.py:428
  7.7 18.5 %collective-permute-start.1 = (bf16[320,1024]{1,0:T(8,128)(2,1)}, bf16[320,1024]{1,0:T(8,128)(2,1)}, u32[]{:S(2)}, u32[]{:S(2)}) collective-permute-start(bf16[320,1024]{1,0:T(8,128)(2,1)} %bitcast.179), channel_id=1, source_target_pairs={{0,4},{4,0},{2,6},{6,2},{1,5},{5,1},{3,7},{7,3},{8,12},{12,8},{10,... | collective-permute-start | bytes 1966088 | tf_op jit(solution)/shard_map/ppermute | solution.py:432
  13.5 126.0 %all-gather.5.cloned.1.call-start = ((), (), s32[]{:S(2)}) async-start(), calls=%async_computation.1 | async-start | bytes 3145728 | tf_op jit(solution)/shard_map/all_gather | solution.py:758
  16.4 113.2 %collective-permute-start.12 = (bf16[320,1024]{1,0:T(8,128)(2,1)S(1)}, bf16[320,1024]{1,0:T(8,128)(2,1)S(1)}, u32[]{:S(2)}, u32[]{:S(2)}) collective-permute-start(bf16[320,1024]{1,0:T(8,128)(2,1)S(1)} %get-tuple-element.65), channel_id=1, source_target_pairs={{0,4},{4,0},{2,6},{6,2},{1,5},{5,1},{3,7},{7,3},{8,12},{12,8},{10,... | collective-permute-start | bytes 1966088 | tf_op jit(solution)/shard_map/ppermute | solution.py:432
  16.4 114.1 %collective-permute-start.11 = (bf16[320,1024]{1,0:T(8,128)(2,1)S(1)}, bf16[320,1024]{1,0:T(8,128)(2,1)S(1)}, u32[]{:S(2)}, u32[]{:S(2)}) collective-permute-start(bf16[320,1024]{1,0:T(8,128)(2,1)S(1)} %get-tuple-element.65), channel_id=1, source_target_pairs={{0,1},{1,0},{2,3},{3,2},{4,5},{5,4},{6,7},{7,6},{8,9},{9,8},{10,11... | collective-permute-start | bytes 1966088 | tf_op jit(solution)/shard_map/ppermute | solution.py:440
  26.2 19.5 %collective-permute-start.2 = (bf16[320,1024]{1,0:T(8,128)(2,1)}, bf16[320,1024]{1,0:T(8,128)(2,1)}, u32[]{:S(2)}, u32[]{:S(2)}) collective-permute-start(bf16[320,1024]{1,0:T(8,128)(2,1)} %collective-permute-done.1), channel_id=1, source_target_pairs={{0,2},{2,0},{4,6},{6,4},{1,3},{3,1},{5,7},{7,5},{8,10},{10,8},{12,... | collective-permute-start | bytes 1966088 | tf_op jit(solution)/shard_map/ppermute | solution.py:428
  55.5 30.8 %collective-permute-start.3 = (bf16[1280,256]{1,0:T(8,128)(2,1)}, bf16[1280,256]{1,0:T(8,128)(2,1)}, u32[]{:S(2)}, u32[]{:S(2)}) collective-permute-start(bf16[1280,256]{1,0:T(8,128)(2,1)} %get-tuple-element.31), channel_id=1, source_target_pairs={{0,1},{1,0},{2,3},{3,2},{4,5},{5,4},{6,7},{7,6},{8,9},{9,8},{10,11... | collective-permute-start | bytes 1966088 | tf_op jit(solution)/shard_map/ppermute | solution.py:455
  130.5 18.9 %collective-permute-start.13 = (bf16[160,1024]{1,0:T(8,128)(2,1)}, bf16[160,1024]{1,0:T(8,128)(2,1)}, u32[]{:S(2)}, u32[]{:S(2)}) collective-permute-start(bf16[160,1024]{1,0:T(8,128)(2,1)} %slice.212), channel_id=1, source_target_pairs={{0,1},{1,0},{2,3},{3,2},{4,5},{5,4},{6,7},{7,6},{8,9},{9,8},{10,11... | collective-permute-start | bytes 983048 | tf_op jit(solution)/shard_map/ppermute | solution.py:440
  131.3 19.9 %collective-permute-start.14 = (bf16[160,1024]{1,0:T(8,128)(2,1)}, bf16[160,1024]{1,0:T(8,128)(2,1)}, u32[]{:S(2)}, u32[]{:S(2)}) collective-permute-start(bf16[160,1024]{1,0:T(8,128)(2,1)} %slice.213), channel_id=1, source_target_pairs={{0,4},{4,0},{2,6},{6,2},{1,5},{5,1},{3,7},{7,3},{8,12},{12,8},{10,... | collective-permute-start | bytes 983048 | tf_op jit(solution)/shard_map/ppermute | solution.py:432
  146.4 18.8 %collective-permute-start.8 = (bf16[320,1152]{1,0:T(8,128)(2,1)S(1)}, bf16[320,1152]{1,0:T(8,128)(2,1)S(1)}, u32[]{:S(2)}, u32[]{:S(2)}) collective-permute-start(bf16[320,1152]{1,0:T(8,128)(2,1)S(1)} %concatenate.66), channel_id=1, source_target_pairs={{0,4},{4,0},{2,6},{6,2},{1,5},{5,1},{3,7},{7,3},{8,12},{12,8},{10,... | collective-permute-start | bytes 2211848 | tf_op jit(solution)/shard_map/ppermute | solution.py:432
  146.5 19.2 %collective-permute-start.7 = (bf16[320,1152]{1,0:T(8,128)(2,1)S(1)}, bf16[320,1152]{1,0:T(8,128)(2,1)S(1)}, u32[]{:S(2)}, u32[]{:S(2)}) collective-permute-start(bf16[320,1152]{1,0:T(8,128)(2,1)S(1)} %concatenate.66), channel_id=1, source_target_pairs={{0,1},{1,0},{2,3},{3,2},{4,5},{5,4},{6,7},{7,6},{8,9},{9,8},{10,11... | collective-permute-start | bytes 2211848 | tf_op jit(solution)/shard_map/ppermute | solution.py:440
  246.0 17.7 %collective-permute-start.15 = (bf16[2,160,1024]{2,1,0:T(8,128)(2,1)S(1)}, bf16[2,160,1024]{2,1,0:T(8,128)(2,1)S(1)}, u32[]{:S(2)}, u32[]{:S(2)}) collective-permute-start(bf16[2,160,1024]{2,1,0:T(8,128)(2,1)S(1)} %get-tuple-element.72), channel_id=1, source_target_pairs={{0,4},{4,0},{2,6},{6,2},{1,5},{5,1},{3,7},{7,3},{8,12},{12,8},{10,... | collective-permute-start | bytes 1966088 | tf_op jit(solution)/shard_map/ppermute | solution.py:432
  247.0 17.7 %collective-permute-start.17 = (bf16[2,160,1024]{2,1,0:T(8,128)(2,1)S(1)}, bf16[2,160,1024]{2,1,0:T(8,128)(2,1)S(1)}, u32[]{:S(2)}, u32[]{:S(2)}) collective-permute-start(bf16[2,160,1024]{2,1,0:T(8,128)(2,1)S(1)} %get-tuple-element.73), channel_id=1, source_target_pairs={{0,1},{1,0},{2,3},{3,2},{4,5},{5,4},{6,7},{7,6},{8,9},{9,8},{10,11... | collective-permute-start | bytes 1966088 | tf_op jit(solution)/shard_map/ppermute | solution.py:440
  249.7 30.7 %collective-permute-start.21 = (bf16[2,160,1152]{2,1,0:T(8,128)(2,1)S(1)}, bf16[2,160,1152]{2,1,0:T(8,128)(2,1)S(1)}, u32[]{:S(2)}, u32[]{:S(2)}) collective-permute-start(bf16[2,160,1152]{2,1,0:T(8,128)(2,1)S(1)} %get-tuple-element.68), channel_id=1, source_target_pairs={{0,1},{1,0},{2,3},{3,2},{4,5},{5,4},{6,7},{7,6},{8,9},{9,8},{10,11... | collective-permute-start | bytes 2211848 | tf_op jit(solution)/shard_map/ppermute | solution.py:440
  250.7 29.8 %collective-permute-start.19 = (bf16[2,160,1152]{2,1,0:T(8,128)(2,1)S(1)}, bf16[2,160,1152]{2,1,0:T(8,128)(2,1)S(1)}, u32[]{:S(2)}, u32[]{:S(2)}) collective-permute-start(bf16[2,160,1152]{2,1,0:T(8,128)(2,1)S(1)} %get-tuple-element.69), channel_id=1, source_target_pairs={{0,4},{4,0},{2,6},{6,2},{1,5},{5,1},{3,7},{7,3},{8,12},{12,8},{10,... | collective-permute-start | bytes 2211848 | tf_op jit(solution)/shard_map/ppermute | solution.py:432
  265.2 21.4 %collective-permute-start.18 = (bf16[160,1024]{1,0:T(8,128)(2,1)S(1)}, bf16[160,1024]{1,0:T(8,128)(2,1)S(1)}, u32[]{:S(2)}, u32[]{:S(2)}) collective-permute-start(bf16[160,1024]{1,0:T(8,128)(2,1)S(1)} %fusion.25), channel_id=1, source_target_pairs={{0,4},{4,0},{2,6},{6,2},{1,5},{5,1},{3,7},{7,3},{8,12},{12,8},{10,... | collective-permute-start | bytes 983048 | tf_op jit(solution)/shard_map/ppermute | solution.py:432
  266.5 21.0 %collective-permute-start.16 = (bf16[160,1024]{1,0:T(8,128)(2,1)S(1)}, bf16[160,1024]{1,0:T(8,128)(2,1)S(1)}, u32[]{:S(2)}, u32[]{:S(2)}) collective-permute-start(bf16[160,1024]{1,0:T(8,128)(2,1)S(1)} %fusion.24), channel_id=1, source_target_pairs={{0,1},{1,0},{2,3},{3,2},{4,5},{5,4},{6,7},{7,6},{8,9},{9,8},{10,11... | collective-permute-start | bytes 983048 | tf_op jit(solution)/shard_map/ppermute | solution.py:440
  280.8 13.0 %collective-permute-start.20 = (bf16[160,1152]{1,0:T(8,128)(2,1)S(1)}, bf16[160,1152]{1,0:T(8,128)(2,1)S(1)}, u32[]{:S(2)}, u32[]{:S(2)}) collective-permute-start(bf16[160,1152]{1,0:T(8,128)(2,1)S(1)} %fusion.22), channel_id=1, source_target_pairs={{0,1},{1,0},{2,3},{3,2},{4,5},{5,4},{6,7},{7,6},{8,9},{9,8},{10,11... | collective-permute-start | bytes 1105928 | tf_op jit(solution)/shard_map/ppermute | solution.py:440
  353.5 17.9 %collective-permute-start.26 = (bf16[1280,256]{1,0:T(8,128)(2,1)}, bf16[1280,256]{1,0:T(8,128)(2,1)}, u32[]{:S(2)}, u32[]{:S(2)}) collective-permute-start(bf16[1280,256]{1,0:T(8,128)(2,1)} %slice.177), channel_id=1, source_target_pairs={{0,1},{1,0},{2,3},{3,2},{4,5},{5,4},{6,7},{7,6},{8,9},{9,8},{10,11... | collective-permute-start | bytes 1966088 | tf_op jit(solution)/shard_map/ppermute | solution.py:462
  356.3 37.6 %collective-permute-start.29 = (bf16[512,1024]{0,1:T(8,128)(2,1)}, bf16[512,1024]{0,1:T(8,128)(2,1)}, u32[]{:S(2)}, u32[]{:S(2)}) collective-permute-start(bf16[512,1024]{0,1:T(8,128)(2,1)} %bitcast.203), channel_id=1, source_target_pairs={{0,1},{1,0},{2,3},{3,2},{4,5},{5,4},{6,7},{7,6},{8,9},{9,8},{10,11... | collective-permute-start | bytes 3145736 | tf_op jit(solution)/shard_map/ppermute | solution.py:440
  388.4 16.3 %collective-permute-start.31 = (bf16[512,512]{1,0:T(8,128)(2,1)S(1)}, bf16[512,512]{1,0:T(8,128)(2,1)S(1)}, u32[]{:S(2)}, u32[]{:S(2)}) collective-permute-start(bf16[512,512]{1,0:T(8,128)(2,1)S(1)} %dynamic-slice_bitcast_fusion), channel_id=1, source_target_pairs={{0,1},{1,0},{2,3},{3,2},{4,5},{5,4},{6,7},{7,6},{8,9},{9,8},{10,11... | collective-permute-start | bytes 1572872 | tf_op jit(solution)/shard_map/ppermute | solution.py:440
  395.6 15.0 %collective-permute-start.30 = (bf16[512,512]{0,1:T(8,128)(2,1)S(1)}, bf16[512,512]{0,1:T(8,128)(2,1)S(1)}, u32[]{:S(2)}, u32[]{:S(2)}) collective-permute-start(bf16[512,512]{0,1:T(8,128)(2,1)S(1)} %dynamic-slice_bitcast_fusion.1), channel_id=1, source_target_pairs={{0,4},{4,0},{2,6},{6,2},{1,5},{5,1},{3,7},{7,3},{8,12},{12,8},{10,... | collective-permute-start | bytes 1572872 | tf_op jit(solution)/shard_map/ppermute | solution.py:432
  400.6 221.0 %collective-permute-start.28 = (bf16[320,1024]{1,0:T(8,128)(2,1)}, bf16[320,1024]{1,0:T(8,128)(2,1)}, u32[]{:S(2)}, u32[]{:S(2)}) collective-permute-start(bf16[320,1024]{1,0:T(8,128)(2,1)} %fusion.19), channel_id=1, source_target_pairs={{0,4},{4,0},{2,6},{6,2},{1,5},{5,1},{3,7},{7,3},{8,12},{12,8},{10,... | collective-permute-start | bytes 1966088 | tf_op jit(solution)/shard_map/ppermute | solution.py:432
  (53 other events, 444.4 us)
Sparse Core Ops, SparseCore 0:
  13.6 31.5 all-gather.2
  46.8 46.9 all-gather.4

commit v3 on v1

--- a/solution.py
+++ b/solution.py
@@ -1,8 +1,10 @@
 import functools
 import math
+import types
 
 import jax
 import jax.numpy as jnp
+import numpy as np
 from jax import lax
 from jax.experimental import pallas as pl
 from jax.experimental.pallas import tpu as pltpu
@@ -96,6 +98,185 @@
     )(tok, gain, w, cos, sin)
 
 
+MESH = pl.DeviceIdType.MESH
+
+
+def rope_rows(w, cos, sin):
+    half = HEAD_WIDTH // 2
+    low_half = lax.broadcasted_iota(jnp.int32, w.shape, 1) % HEAD_WIDTH < half
+    rot = jnp.where(low_half, -pltpu.roll(w, 128 - half, 1), pltpu.roll(w, half, 1))
+    return w * cos + rot * sin
+
+
+def front_kernel(
+    spans, tok, w3, small, rtab, stab, tok_out, wc_out, small_all, h_out, q, kv, cos_out, sin_out,
+    tok_all, wc, h, cos, sin, s_tok, s_w, s_own, s_kv, s_end
+):
+    z, s, f = lax.axis_index("dp"), lax.axis_index("seq"), lax.axis_index("fsdp")
+    core = s % 2
+    peer_core = (z, s + 1 - 2 * core, f)
+    peer_x = (z, (s + 2) % 4, f)
+    peer_y = (z, s, 1 - f)
+    rows, width = tok.shape
+    part = small.shape[1]
+
+    barrier = pltpu.get_barrier_semaphore()
+    for dev in (peer_core, peer_x, peer_y):
+        pl.semaphore_signal(barrier, inc=1, device_id=dev, device_id_type=MESH)
+
+    def remote(src, dst, sems, b, dev):
+        return pltpu.make_async_remote_copy(
+            src_ref=src, dst_ref=dst, send_sem=sems.at[0, b], recv_sem=sems.at[1, b],
+            device_id=dev, device_id_type=MESH,
+        )
+
+    own_rows = pl.ds(pl.multiple_of(f * part, part), part)
+    pieces = []
+    for first, n, to in ((0, 256, 0), (width, 128, 256), (width + width // 2, 128, 384)):
+        src = w3.at[:, pl.ds(pl.multiple_of(first + s * n, 128), n)]
+        pieces.append((src, wc.at[own_rows, pl.ds(to, n)]))
+    local = [pltpu.make_async_copy(a, b, s_own.at[i]) for i, (a, b) in enumerate(pieces)]
+    for copy in local:
+        copy.start()
+    small_all[:, own_rows] = small[...]
+    tok_all[0] = tok[...]
+    pl.semaphore_wait(barrier, 3)
+    over = remote(tok, tok_all.at[2], s_tok, 1, peer_x)
+    near = remote(tok, tok_all.at[1], s_tok, 0, peer_core)
+    onward = remote(tok_all.at[2], tok_all.at[3], s_tok, 2, peer_core)
+    weights = [remote(a, b, s_w, i, peer_y) for i, (a, b) in enumerate(pieces)]
+    weights.append(remote(small, small_all.at[:, own_rows], s_w, 3, peer_y))
+    over.start()
+    for copy in weights:
+        copy.start()
+    near.start()
+    for copy in local:
+        copy.wait()
+    for copy in weights:
+        copy.wait_recv()
+    gain = small_all[16:17, :].astype(F32)
+
+    def kv_copy(t):
+        at = pl.ds(t * rows, rows)
+        return remote(kv.at[0, at], kv.at[1, at], s_kv, t, peer_y)
+
+    ends = [pltpu.make_async_copy(wc, wc_out, s_end.at[0])]
+    ends[0].start()
+    span = rows // 2
+    for k in range(8):
+        at = pl.ds(k * span, span)
+        row = pl.ds(spans[k], 1)
+        c, n = stab[0, row, :], stab[1, row, :]
+        cos[at, :] = rtab[0] * c - rtab[1] * n
+        sin[at, :] = rtab[1] * c + rtab[0] * n
+    for i, (src, dst) in enumerate(((cos, cos_out), (sin, sin_out))):
+        ends.append(pltpu.make_async_copy(src, dst, s_end.at[1 + i]))
+        ends[-1].start()
+
+    for t in range(4):
+        if t == 1:
+            near.wait_recv()
+        if t == 2:
+            over.wait_recv()
+            onward.start()
+        if t == 3:
+            onward.wait_recv()
+        at = pl.ds(t * rows, rows)
+        ends.append(pltpu.make_async_copy(tok_all.at[t], tok_out.at[t], s_end.at[3 + t]))
+        ends[-1].start()
+        normed, _ = rms_parts(tok_all[t].astype(F32))
+        hidden = (normed * gain).astype(BF)
+        h[at, :] = hidden
+        proj = mm(hidden, wc[...])
+        c, n = cos[at, :], sin[at, :]
+        kv[0, at, :128] = rope_rows(proj[:, 256:384], c, n).astype(BF)
+        kv[0, at, 128:] = proj[:, 384:].astype(BF)
+        kv_copy(t).start()
+        for k in range(2):
+            q[at, k * 128 : (k + 1) * 128] = rope_rows(proj[:, k * 128 : (k + 1) * 128], c, n).astype(BF)
+        ends.append(pltpu.make_async_copy(h.at[at], h_out.at[at], s_end.at[7 + t]))
+        ends[-1].start()
+    for t in range(4):
+        kv_copy(t).wait()
+    for copy in ends:
+        copy.wait()
+    for copy in (over, near, onward, *weights):
+        copy.wait_send()
+
+
+def front(spans, n_spans, tok, w3, small):
+    rows, width = tok.shape
+    span, half = rows // 2, HEAD_WIDTH // 2
+    freqs = np.exp(np.arange(half) * (-2.0 * math.log(ROPE_BASE) / HEAD_WIDTH)).astype(np.float32)
+
+    def table(positions):
+        angles = np.tile(positions[:, None].astype(np.float64) * freqs[None, :], (1, 4))
+        return jnp.asarray(np.stack([np.cos(angles), np.sin(angles)]), F32)
+
+    rtab, stab = table(np.arange(span)), table(np.arange(n_spans) * span)
+    vmem = pl.BlockSpec(memory_space=pltpu.VMEM)
+    hbm = pl.BlockSpec(memory_space=pl.ANY)
+    dma = pltpu.SemaphoreType.DMA
+    shape = jax.ShapeDtypeStruct
+    return pl.pallas_call(
+        front_kernel,
+        in_specs=[pl.BlockSpec(memory_space=pltpu.SMEM), vmem, hbm, vmem, vmem, vmem],
+        out_specs=[hbm, hbm, vmem, hbm, vmem, vmem, hbm, hbm],
+        out_shape=[
+            shape((4, rows, width), BF),
+            shape((width, 512), BF),
+            shape((small.shape[0], width), BF),
+            shape((4 * rows, width), BF),
+            shape((4 * rows, 256), BF),
+            shape((2, 4 * rows, 256), BF),
+            shape((4 * rows, 128), F32),
+            shape((4 * rows, 128), F32),
+        ],
+        scratch_shapes=[
+            pltpu.VMEM((4, rows, width), BF), pltpu.VMEM((width, 512), BF),
+            pltpu.VMEM((4 * rows, width), BF),
+            pltpu.VMEM((4 * rows, 128), F32), pltpu.VMEM((4 * rows, 128), F32),
+            dma((2, 3)), dma((2, 4)), dma((3,)), dma((2, 4)), dma((11,)),
+        ],
+        compiler_params=params(collective_id=2, has_side_effects=True),
+        name="front",
+    )(spans, tok, w3, small, rtab, stab)
+
+
+def widen_kernel(*refs):
+    n = (len(refs) - 4) // 2
+    ins, outs = refs[:n], refs[n + 1 : 2 * n + 1]
+    for a, b in zip(ins, outs):
+        b[...] = a[...].astype(F32)
+    tiny, (one, two, router) = refs[n], refs[2 * n + 1 :]
+
+    @pl.when(pl.program_id(0) == 0)
+    def _():
+        one[...] = tiny[16:17, :]
+        two[...] = tiny[17:18, :]
+        router[...] = jnp.transpose(tiny[...])[:, : router.shape[1]]
+
+
+def widen(arrays, tiny, n_experts):
+    flat = [a.reshape(-1, a.shape[-1]) for a in arrays]
+    steps = 16
+    wide = tiny.shape[1]
+    specs = [pl.BlockSpec((a.shape[0] // steps, a.shape[1]), lambda i: (i, 0)) for a in flat]
+    shape = jax.ShapeDtypeStruct
+    got = pl.pallas_call(
+        widen_kernel,
+        grid=(steps,),
+        in_specs=specs + [whole(tiny.shape)],
+        out_specs=specs + [whole((1, wide)), whole((1, wide)), whole((wide, n_experts))],
+        out_shape=[shape(a.shape, F32) for a in flat]
+        + [shape((1, wide), F32), shape((1, wide), F32), shape((wide, n_experts), F32)],
+        compiler_params=params(),
+        name="widen",
+    )(*flat, tiny)
+    n = len(arrays)
+    return [g.reshape(a.shape) for g, a in zip(got, arrays)] + [got[n][0], got[n + 1][0], got[n + 2]]
+
+
 def project_back_kernel(
     tok_ref, h_ref, dq_ref, dkv_ref, w_ref, cos_ref, sin_ref, dh_ref, gw_ref, gn_ref, acc
 ):
@@ -148,21 +329,24 @@
     )(tok, h, dq, dkv, w, cos, sin)
 
 
-def stack_heads(a, b):
+def stack_heads(a, b, dtype=BF):
+    a, b = a.astype(F32), b.astype(F32)
     low = lax.broadcasted_iota(jnp.int32, a.shape, 1) < HEAD_WIDTH
-    zero = jnp.zeros_like(a)
-    return jnp.concatenate(
-        [jnp.where(low, a, zero), jnp.where(low, b, zero), jnp.where(low, zero, a), jnp.where(low, zero, b)],
-        axis=0,
-    )
+    turn = lambda v: pltpu.roll(v, HEAD_WIDTH, 1)
+    rows = [
+        jnp.where(low, a, 0.0), jnp.where(low, turn(a), 0.0),
+        jnp.where(low, 0.0, turn(b)), jnp.where(low, 0.0, b),
+    ]
+    return jnp.concatenate(rows, axis=0).astype(dtype)
 
 
 def unstack_heads(x):
     n = x.shape[0] // 4
     low = lax.broadcasted_iota(jnp.int32, (n, 128), 1) < HEAD_WIDTH
+    turn = lambda v: pltpu.roll(v, HEAD_WIDTH, 1)
     return (
-        jnp.where(low, x[:n], x[2 * n : 3 * n]),
-        jnp.where(low, x[n : 2 * n], x[3 * n :]),
+        jnp.where(low, x[:n], turn(x[n : 2 * n])),
+        jnp.where(low, turn(x[2 * n : 3 * n]), x[3 * n :]),
     )
 
 
@@ -182,7 +366,7 @@
 
 
 def attend_kernel(
-    qtab_ref, ktab_ref, len_ref, q_ref, kv_ref, o_ref, lse_ref, ks, vs, *, span, kb
+    qtab_ref, ktab_ref, len_ref, q_ref, kv_ref, o_ref, low_ref, lse_ref, ks, vs, *, span, kb
 ):
     step = pl.program_id(0)
     count = ks.shape[0] // span
@@ -224,6 +408,8 @@
     a, b = unstack_heads(acc / total)
     o_ref[:, :128] = a
     o_ref[:, 128:] = b
+    low_ref[:, :128] = a.astype(BF)
+    low_ref[:, 128:] = b.astype(BF)
     lse = jnp.broadcast_to(top + jnp.log2(total), (rows, 128))
     lse_ref[0] = jnp.transpose(lse)[:8]
 
@@ -238,12 +424,14 @@
             in_specs=[pl.BlockSpec((span, 256), lambda i, *_: (i, 0)), whole(kv.shape)],
             out_specs=[
                 pl.BlockSpec((span, 256), lambda i, *_: (i, 0)),
+                pl.BlockSpec((span, 256), lambda i, *_: (i, 0)),
                 pl.BlockSpec((1, 8, 4 * span), lambda i, *_: (i, 0, 0)),
             ],
             scratch_shapes=[pltpu.VMEM((keys, 128), BF), pltpu.VMEM((keys, 128), BF)],
         ),
         out_shape=[
             jax.ShapeDtypeStruct((q.shape[0], 256), F32),
+            jax.ShapeDtypeStruct((q.shape[0], 256), BF),
             jax.ShapeDtypeStruct((steps, 8, 4 * span), F32),
         ],
         compiler_params=params(),
@@ -269,7 +457,7 @@
     q = stack_heads(q_ref[:, :128], q_ref[:, 128:])
     do = stack_heads(do_ref[:, :128], do_ref[:, 128:])
     rows = 4 * span
-    inner = do.astype(F32) * stack_heads(o_ref[:, :128], o_ref[:, 128:])
+    inner = do.astype(F32) * stack_heads(o_ref[:, :128], o_ref[:, 128:], F32)
     delta = jnp.sum(jnp.transpose(inner), axis=0, keepdims=True)
     lse = lse_ref[0, :1]
     limit = len_ref[0]
@@ -339,7 +527,7 @@
 
 
 def experts_kernel(
-    base_ref, h_ref, c_ref, wg_ref, wu_ref, wd_ref, moe_ref, dh_ref, gg_ref, gu_ref, gd_ref,
+    base_ref, h_ref, c_ref, wg_ref, wu_ref, wd_ref, moe_ref, dh_ref, grad_ref,
     moe, dh, dgates, s_act, s_gate, s_up, *, tile,
 ):
     step = pl.program_id(0)
@@ -377,13 +565,12 @@
         moe[at, :] += mm(act, wd)
         dh[at, :] += mm_nt(dgate, wg) + mm_nt(dup, wu)
 
-    for i in range(4):
-        n = width // 4
-        gg_ref[0, i * n : (i + 1) * n, :] = mm_tn(h_ref[:, i * n : (i + 1) * n], s_gate[...]).astype(BF)
-        gu_ref[0, i * n : (i + 1) * n, :] = mm_tn(h_ref[:, i * n : (i + 1) * n], s_up[...]).astype(BF)
+    block = grad_ref.shape[2]
     for i in range(2):
-        n = wd.shape[0] // 2
-        gd_ref[0, i * n : (i + 1) * n, :] = mm_tn(s_act[:, i * n : (i + 1) * n], c_ref[...]).astype(BF)
+        at = slice(i * block, (i + 1) * block)
+        grad_ref[0, i] = mm_tn(h_ref[:, at], s_gate[...]).astype(BF)
+        grad_ref[0, 2 + i] = mm_tn(h_ref[:, at], s_up[...]).astype(BF)
+        grad_ref[0, 4 + i] = mm_tn(s_act[...], c_ref[:, at]).astype(BF)
 
     @pl.when(step == pl.num_programs(0) - 1)
     def _():
@@ -396,7 +583,6 @@
     rows, width = c.shape
     ff = wg.shape[2]
     pick = lambda shape: pl.BlockSpec((1,) + shape, lambda e, s: (s[0] + e, 0, 0))
-    put = lambda shape: pl.BlockSpec((1,) + shape, lambda e, s: (e, 0, 0))
     return pl.pallas_call(
         functools.partial(experts_kernel, tile=tile),
         grid_spec=pltpu.PrefetchScalarGridSpec(
@@ -408,7 +594,7 @@
             ],
             out_specs=[
                 whole(c.shape), whole(h.shape),
-                put((width, ff)), put((width, ff)), put((ff, width)),
+                pl.BlockSpec((1, 6, ff, ff), lambda e, s: (e, 0, 0, 0)),
             ],
             scratch_shapes=[
                 pltpu.VMEM((rows, width), F32), pltpu.VMEM((rows, width), F32),
@@ -419,15 +605,359 @@
         out_shape=[
             jax.ShapeDtypeStruct(c.shape, BF),
             jax.ShapeDtypeStruct(h.shape, BF),
-            jax.ShapeDtypeStruct((count, width, ff), BF),
-            jax.ShapeDtypeStruct((count, width, ff), BF),
-            jax.ShapeDtypeStruct((count, ff, width), BF),
+            jax.ShapeDtypeStruct((count, 6, ff, ff), BF),
         ],
         compiler_params=params(),
         name="experts",
     )(base, h, c, wg, wu, wd)
 
 
+def moe_kernel(*refs, names, topk, count):
+    r = types.SimpleNamespace(**dict(zip(names, refs)))
+    z, s, f = lax.axis_index("dp"), lax.axis_index("seq"), lax.axis_index("fsdp")
+    core, x = s % 2, s // 2
+    flip = 1 - 2 * core
+    seqs = (s, s + flip, (s + 2) % 4, (s + 2) % 4 + flip)
+    peers = [(z, q, f) for q in seqs]
+    peer_x, peer_y = peers[2], (z, s, 1 - f)
+    att, att_in, tout, hx, cots = r.att, r.att_in, r.tout, r.hx, r.cots
+    rows, width = tout.shape
+    n = rows // 2
+    ext = hx.shape[1]
+    ff = r.wgs.shape[2]
+    owned = r.wg.shape[0]
+
+    barrier = pltpu.get_barrier_semaphore()
+    for dev in (*peers[1:], peer_y):
+        pl.semaphore_signal(barrier, inc=1, device_id=dev, device_id_type=MESH)
+
+    def remote(src, dst, sems, b, dev):
+        return pltpu.make_async_remote_copy(
+            src_ref=src, dst_ref=dst, send_sem=sems.at[0, b], recv_sem=sems.at[1, b],
+            device_id=dev, device_id_type=MESH,
+        )
+
+    def block(t):
+        return pl.ds(pl.multiple_of(t * rows, rows), rows)
+
+    load_cots = [
+        pltpu.make_async_copy(v, cots.at[block(i)], r.s_cot.at[i])
+        for i, v in enumerate((r.cot, r.cot_y, r.cot_x))
+    ]
+    for copy in load_cots:
+        copy.start()
+
+    def load_weights(e, act):
+        for i, (src, dst) in enumerate(((r.wg, r.wgs), (r.wu, r.wus), (r.wd, r.wds))):
+            act(pltpu.make_async_copy(src.at[x * count + e], dst.at[e], r.s_w.at[i, e]))
+
+    @pl.loop(0, count)
+    def _(e):
+        load_weights(e, lambda copy: copy.start())
+
+    pl.semaphore_wait(barrier, 4)
+    heads = [remote(att.at[m], att_in.at[m], r.s_att, m, peers[m]) for m in range(1, 4)]
+    for copy in heads:
+        copy.start()
+    diag = [
+        remote(r.cot_x.at[pl.ds(0, n)], cots.at[pl.ds(3 * rows, n)], r.s_diag, 0, peer_y),
+        remote(r.cot_y.at[pl.ds(n, n)], cots.at[pl.ds(3 * rows + n, n)], r.s_diag, 1, peer_x),
+    ]
+    for copy in diag:
+        copy.start()
+
+    small = r.small
+    table = r.table
+    table[...] = jnp.zeros_like(table)
+    table[: small.shape[0], :] = small[...]
+    n_exp = r.gates.shape[1]
+    gain = small[17:18, :].astype(F32)
+    own_cols = pl.ds(pl.multiple_of(f * ff, ff), ff)
+    away_cols = pl.ds(pl.multiple_of((1 - f) * ff, ff), ff)
+
+    def head_cols(m):
+        return pl.ds(pl.multiple_of(seqs[m] * 256, 256), 256)
+
+    tout[:, head_cols(0)] = att[0]
+    for m in range(1, 4):
+        heads[m - 1].wait_recv()
+        tout[:, head_cols(m)] = att_in[m]
+
+    shares = []
+    for i in range(2):
+        at = pl.ds(i * n, n)
+        middle = (
+            r.tok[at, :].astype(F32)
+            + mm(tout[at, own_cols], r.wo_own[...])
+            + mm(tout[at, away_cols], r.wo_there[...])
+        )
+        r.middle[at, :] = middle
+        normed, _ = rms_parts(middle)
+        hidden = (normed * gain).astype(BF)
+        logits = mm_nt(hidden, table[...])
+        lane = lax.broadcasted_iota(jnp.int32, logits.shape, 1)
+        chosen = lane == r.routes[at, 0:1]
+        for k in range(1, topk):
+            chosen = chosen | (lane == r.routes[at, k : k + 1])
+        top = jnp.max(jnp.where(chosen, logits, NEG), axis=-1, keepdims=True)
+        raised = jnp.where(chosen, jnp.exp(logits - top), 0.0)
+        gates = raised / jnp.sum(raised, axis=-1, keepdims=True)
+        r.gates[at, :] = gates
+        hx[at, :width] = hidden
+        hx[at, width:] = gates.astype(BF)
+        for j, dev in ((0, peer_y), (1, peer_x)):
+            to = pl.ds((j + 1) * rows + i * n, n)
+            copy = remote(hx.at[at], hx.at[to], r.s_h, 2 * j + i, dev)
+            copy.start()
+            shares.append(copy)
+    second = remote(
+        hx.at[pl.ds(rows + n, n)], hx.at[pl.ds(3 * rows + n, n)], r.s_h, 4, peer_x
+    )
+    first = remote(hx.at[pl.ds(2 * rows, n)], hx.at[pl.ds(3 * rows, n)], r.s_h, 5, peer_y)
+
+    dhs, moe, dh, dgates = r.dhs, r.moe_acc, r.dh_acc, r.dg_acc
+    back_y = remote(dhs.at[block(1)], r.rdh.at[0], r.s_d, 0, peer_y)
+    back_x = remote(dhs.at[block(2)], r.rdh.at[1], r.s_d, 1, peer_x)
+    hop_x = remote(dhs.at[pl.ds(3 * rows, n)], r.via.at[0], r.s_d, 2, peer_x)
+    hop_y = remote(dhs.at[pl.ds(3 * rows + n, n)], r.via.at[1], r.s_d, 3, peer_y)
+    end_y = remote(r.via.at[0], r.rdd.at[pl.ds(0, n)], r.s_d, 4, peer_y)
+    end_x = remote(r.via.at[1], r.rdd.at[pl.ds(n, n)], r.s_d, 5, peer_x)
+
+    moes = (r.moe0, r.moe1, r.moe2, r.moe3)
+
+    def moe_out(t):
+        return pltpu.make_async_copy(r.mstage.at[t % 2], moes[t], r.s_m.at[t])
+
+    @pl.loop(0, 4 * count)
+    def _(k):
+        t, e = k // count, k % count
+
+        @pl.when(k < count)
+        def _():
+            load_weights(e, lambda copy: copy.wait())
+
+        @pl.when(k == 0)
+        def _():
+            load_cots[0].wait()
+
+        @pl.when(k == count)
+        def _():
+            for copy in shares:
+                copy.wait_recv()
+            second.start()
+            first.start()
+            load_cots[1].wait()
+            load_cots[2].wait()
+
+        @pl.when(k == 3 * count)
+        def _():
+            first.wait_recv()
+            second.wait_recv()
+            for copy in diag:
+                copy.wait_recv()
+
+        at = block(t)
+        h, c = hx[at, :width], cots[at, :]
+        wg, wu, wd = r.wgs[e], r.wus[e], r.wds[e]
+        expert = f * owned + x * count + e
+        mine = lax.broadcasted_iota(jnp.int32, (rows, ext - width), 1) == expert
+        gate = jnp.sum(jnp.where(mine, hx[at, width:].astype(F32), 0.0), axis=1, keepdims=True)
+        g, u, zz = mm(h, wg), mm(h, wu), mm_nt(c, wd)
+        sig = jax.nn.sigmoid(g)
+        silu = g * sig
+        act = silu * u
+        dgate_col = jnp.where(mine, jnp.sum(act * zz, axis=1, keepdims=True), 0.0)
+        act = (act * gate).astype(BF)
+        dact = zz * gate
+        dgate = (dact * u * sig * (1.0 + g * (1.0 - sig))).astype(BF)
+        dup = (dact * silu).astype(BF)
+        r.s_act[e, at, :] = act
+        r.s_gate[e, at, :] = dgate
+        r.s_up[e, at, :] = dup
+
+        @pl.when(e == 0)
+        def _():
+            moe[...] = mm(act, wd)
+            dh[...] = mm_nt(dgate, wg) + mm_nt(dup, wu)
+            dgates[...] = dgate_col
+
+        @pl.when(e > 0)
+        def _():
+            moe[...] += mm(act, wd)
+            dh[...] += mm_nt(dgate, wg) + mm_nt(dup, wu)
+            dgates[...] += dgate_col
+
+        @pl.when(e == count - 1)
+        def _():
+            for k in range(4):
+                @pl.when(t == k)
+                def _():
+                    if k >= 2:
+                        moe_out(k - 2).wait()
+                    r.mstage[k % 2] = moe[...].astype(BF)
+                    moe_out(k).start()
+
+            dhs[at, :width] = dh[...].astype(BF)
+            dhs[at, width:] = dgates[...].astype(BF)
+
+            @pl.when(t == 1)
+            def _():
+                back_y.start()
+
+            @pl.when(t == 2)
+            def _():
+                back_x.start()
+
+            @pl.when(t == 3)
+            def _():
+                hop_x.start()
+                hop_y.start()
+
+    stage = r.stage
+
+    def grad_copy(b, slot):
+        return pltpu.make_async_copy(stage.at[slot], r.grads.at[b], r.s_g.at[slot])
+
+    dattn, dto, dsend = r.dattn, r.dto, r.dsend
+    returns = [remote(dsend.at[m], r.do.at[m], r.s_back, m, peers[m]) for m in range(1, 4)]
+
+    def middle_back():
+        for copy in (back_y, back_x, end_y, end_x):
+            copy.wait_recv()
+        gn = jnp.zeros((1, width), F32)
+        rg = jnp.zeros((table.shape[0], width), F32)
+        for i in range(2):
+            at = pl.ds(i * n, n)
+            total = (
+                dhs[at, :].astype(F32) + r.rdh[0, at, :].astype(F32)
+                + r.rdh[1, at, :].astype(F32) + r.rdd[at, :].astype(F32)
+            )
+            dg, gates = total[:, width:], r.gates[at, :]
+            dl = (gates * (dg - jnp.sum(gates * dg, axis=-1, keepdims=True))).astype(BF)
+            rg += mm_tn(dl, hx[at, :width])
+            d_hidden = total[:, :width] + mm(dl, table[...])
+            normed, factor = rms_parts(r.middle[at, :])
+            gn += jnp.sum(d_hidden * normed, axis=0, keepdims=True)
+            d_n = d_hidden * gain
+            d_mid = cots[at, :].astype(F32) + factor * (
+                d_n - normed * jnp.mean(d_n * normed, axis=-1, keepdims=True)
+            )
+            r.dmid[at, :] = d_mid
+            low = d_mid.astype(BF)
+            dattn[at, :] = low
+            dto[at, own_cols] = mm_nt(low, r.wo_own[...]).astype(BF)
+            dto[at, away_cols] = mm_nt(low, r.wo_there[...]).astype(BF)
+        for m in range(1, 4):
+            dsend[m] = dto[:, head_cols(m)]
+            returns[m - 1].start()
+        r.do[0] = dto[:, head_cols(0)]
+        top = rg[:32]
+        row = lax.broadcasted_iota(jnp.int32, top.shape, 0)
+        top = jnp.where(row == 17, gn, jnp.where(row < 16, top, 0.0))
+        r.tiny[0] = top[:, : width // 2]
+        r.tiny[1] = top[:, width // 2 :]
+        for i in range(4):
+            at = slice(i * 256, (i + 1) * 256)
+            r.gout[at, :] = mm_tn(tout[:, at], dattn[...]).astype(BF)
+
+    def forward():
+        hop_x.wait_recv()
+        end_y.start()
+        hop_y.wait_recv()
+        end_x.start()
+
+    @pl.loop(0, 3 * count)
+    def _(k):
+        e, j = k // 3, k % 3
+        pl.when(k == 5)(forward)
+        pl.when(k == 3 * count - 2)(middle_back)
+
+        @pl.when(k > 0)
+        def _():
+            grad_copy(0, 0).wait()
+            grad_copy(0, 1).wait()
+
+        for which, left, right in ((0, hx, r.s_gate), (1, hx, r.s_up), (2, cots, r.s_act)):
+            @pl.when(j == which)
+            def _():
+                for i in range(2):
+                    at = slice(i * ff, (i + 1) * ff)
+                    if which < 2:
+                        v = mm_tn(left[:, at], right[e])
+                    else:
+                        v = mm_tn(right[e], left[:, at])
+                    stage[i] = v.astype(BF)
+
+        for i in range(2):
+            grad_copy(6 * e + 2 * j + i, i).start()
+
+    grad_copy(0, 0).wait()
+    grad_copy(0, 1).wait()
+    moe_out(2).wait()
+    moe_out(3).wait()
+    for copy in returns:
+        copy.wait()
+    for copy in (*heads, *diag, *shares, first, second, back_y, back_x, hop_x, hop_y, end_y, end_x):
+        copy.wait_send()
+
+
+def moe_layer(att, tok, wo_own, wo_there, small, routes, cot, cot_y, cot_x, wg, wu, wd):
+    rows, width = tok.shape
+    owned, _, ff = wg.shape
+    count = owned // 2
+    ext = width + 128
+    hbm = pl.BlockSpec(memory_space=pl.ANY)
+    vmem = pl.BlockSpec(memory_space=pltpu.VMEM)
+    dma = pltpu.SemaphoreType.DMA
+    args = dict(
+        att=(att.reshape(4, rows, 256), vmem), tok=(tok, vmem), wo_own=(wo_own, vmem),
+        wo_there=(wo_there, vmem), small=(small, vmem), routes=(routes, vmem),
+        cot=(cot, hbm), cot_y=(cot_y, hbm), cot_x=(cot_x, hbm),
+        wg=(wg, hbm), wu=(wu, hbm), wd=(wd, hbm),
+    )
+    shape = jax.ShapeDtypeStruct
+    outs = dict(
+        middle=(shape((rows, width), F32), vmem),
+        moe0=(shape((rows, width), BF), hbm), moe1=(shape((rows, width), BF), hbm),
+        moe2=(shape((rows, width), BF), hbm), moe3=(shape((rows, width), BF), hbm),
+        dmid=(shape((rows, width), F32), vmem),
+        do=(shape((4, rows, 256), BF), vmem),
+        grads=(shape((6 * count, ff, ff), BF), hbm),
+        gout=(shape((width, width), BF), vmem),
+        tiny=(shape((2, 32, width // 2), F32), vmem),
+    )
+    stash = pltpu.VMEM((count, 4 * rows, ff), BF)
+    scratch = dict(
+        att_in=pltpu.VMEM((4, rows, 256), BF), tout=pltpu.VMEM((rows, width), BF),
+        hx=pltpu.VMEM((4 * rows, ext), BF), cots=pltpu.VMEM((4 * rows, width), BF),
+        table=pltpu.VMEM((128, width), BF), gates=pltpu.VMEM((rows, 128), F32),
+        wgs=pltpu.VMEM((count, width, ff), BF), wus=pltpu.VMEM((count, width, ff), BF),
+        wds=pltpu.VMEM((count, ff, width), BF),
+        s_act=stash, s_gate=stash, s_up=stash,
+        moe_acc=pltpu.VMEM((rows, width), F32), dh_acc=pltpu.VMEM((rows, width), F32),
+        dg_acc=pltpu.VMEM((rows, 128), F32), mstage=pltpu.VMEM((2, rows, width), BF),
+        dhs=pltpu.VMEM((4 * rows, ext), BF), rdh=pltpu.VMEM((2, rows, ext), BF),
+        via=pltpu.VMEM((2, rows // 2, ext), BF), rdd=pltpu.VMEM((rows, ext), BF),
+        dattn=pltpu.VMEM((rows, width), BF), dto=pltpu.VMEM((rows, width), BF),
+        dsend=pltpu.VMEM((4, rows, 256), BF), stage=pltpu.VMEM((2, ff, ff), BF),
+        s_att=dma((2, 4)), s_diag=dma((2, 2)), s_h=dma((2, 6)), s_d=dma((2, 6)), s_back=dma((2, 4)),
+        s_cot=dma((3,)), s_w=dma((3, count)), s_m=dma((4,)), s_g=dma((2,)),
+    )
+    names = tuple(args) + tuple(outs) + tuple(scratch)
+    got = pl.pallas_call(
+        functools.partial(moe_kernel, names=names, topk=routes.shape[1], count=count),
+        in_specs=[v[1] for v in args.values()],
+        out_specs=[v[1] for v in outs.values()],
+        out_shape=[v[0] for v in outs.values()],
+        scratch_shapes=list(scratch.values()),
+        compiler_params=pltpu.CompilerParams(
+            vmem_limit_bytes=67043328, collective_id=3, has_side_effects=True
+        ),
+        name="moe_layer",
+    )(*[v[0] for v in args.values()])
+    return types.SimpleNamespace(**dict(zip(outs, got)))
+
+
 def flip_core(x):
     return lax.ppermute(x, "seq", [(0, 1), (1, 0), (2, 3), (3, 2)])
 
@@ -438,6 +968,15 @@
 
 def flip_both(x):
     return lax.ppermute(x, "seq", [(0, 3), (3, 0), (1, 2), (2, 1)])
+
+
+def flip_y(x):
+    return lax.ppermute(x, "fsdp", [(0, 1), (1, 0)])
+
+
+def flip_xy(x):
+    perm = [(2 * q + f, 2 * ((q + 2) % 4) + 1 - f) for q in range(4) for f in range(2)]
+    return lax.ppermute(x, ("seq", "fsdp"), perm)
 
 
 def gather_seq(x):
@@ -462,6 +1001,468 @@
         other = lax.ppermute(x[n:], "fsdp", [(0, 1), (1, 0)])
         return x[:n].astype(F32) + other.astype(F32)
     return lax.psum_scatter(x, "fsdp", scatter_dimension=0, tiled=True).astype(F32)
+
+
+def rope_back(w, cos, sin, low_half):
+    half = HEAD_WIDTH // 2
+    y = w * sin
+    return w * cos + jnp.where(low_half, pltpu.roll(y, 128 - half, 1), -pltpu.roll(y, half, 1))
+
+
+def reduce_kernel(*refs, names, slots, shards, fused):
+    r = types.SimpleNamespace(**dict(zip(names, refs)))
+    gm, mine, rc, pre, suf = r.gm, r.mine, r.rc, r.pre, r.suf
+    gate, up, down, out, qkv = r.gate, r.up, r.down, r.out, r.qkv
+    z, s, f = lax.axis_index("dp"), lax.axis_index("seq"), lax.axis_index("fsdp")
+    core, x = s % 2, s // 2
+    peer_core = (z, s + 1 - 2 * core, f)
+    peer_x = (z, (s + 2) % 4, f)
+    peer_y = (z, s, 1 - f)
+    right, left = (z + 1, s, f), (z - 1, s, f)
+    nb = gm.shape[0]
+    n_moe, n_out, items = 2 * nb, 2 * nb + 2, 2 * nb + 6
+    count = nb // 6
+    piece = mine.shape[1]
+    half, block = 2 * piece, 4 * piece
+    last = slots - 1
+
+    def other_z(k):
+        return ((z + k) % slots, s, f)
+
+    barrier = pltpu.get_barrier_semaphore()
+    peers = [other_z(k) for k in range(1, slots)] + [peer_core, peer_x] + [peer_y] * fused
+    for dev in peers:
+        pl.semaphore_signal(barrier, inc=1, device_id=dev, device_id_type=MESH)
+
+    def remote(src, dst, sems, b, dev):
+        return pltpu.make_async_remote_copy(
+            src_ref=src, dst_ref=dst, send_sem=sems.at[0, b], recv_sem=sems.at[1, b],
+            device_id=dev, device_id_type=MESH,
+        )
+
+    def load(src, b):
+        return pltpu.make_async_copy(src, mine.at[b], r.s_mine.at[b])
+
+    @pl.loop(0, n_moe)
+    def _(b):
+        load(gm.at[b // 2, core, b % 2], b).start()
+
+    if fused:
+        loads = [
+            pltpu.make_async_copy(a, b, r.s_in.at[i])
+            for i, (a, b) in enumerate((
+                (r.dkv.at[pl.ds(0, r.dkvs.shape[0])], r.dkvs), (r.dq, r.dq_in), (r.wc, r.wc_in),
+                (r.cos, r.cos_in), (r.sin, r.sin_in), (r.h, r.h_in), (r.tok, r.tok_in),
+                (r.gout, r.gout_in), (r.dmid, r.dmid_in),
+            ))
+        ]
+        for copy in loads:
+            copy.start()
+    else:
+        for i in range(2):
+            load(r.eo.at[core, i], n_moe + i).start()
+        for i in range(4):
+            load(r.cols.at[i], n_out + i).start()
+    pl.semaphore_wait(barrier, len(peers))
+
+    @pl.loop(0, n_moe)
+    def _(b):
+        remote(gm.at[b // 2, 1 - core, b % 2], rc.at[b], r.s_rc, b, peer_core).start()
+
+    if not fused:
+        for i in range(2):
+            remote(r.eo.at[1 - core, i], rc.at[n_moe + i], r.s_rc, n_moe + i, peer_core).start()
+
+    def place(b, which, part, act):
+        first_row = part * half + b % 2 * piece
+        rows = pl.ds(pl.multiple_of(first_row, piece), piece)
+        e, j = which * count + b // 12, b // 2 % 6
+        jj = j % 2
+        wide = pl.ds(pl.multiple_of(jj * block, block), block)
+        at = pl.ds(pl.multiple_of(jj * block + first_row, piece), piece)
+        for m, o in enumerate((gate, up)):
+            @pl.when((b < n_moe) & (j // 2 == m))
+            def _():
+                act(o.at[e, at, :])
+
+        @pl.when((b < n_moe) & (j // 2 == 2))
+        def _():
+            act(down.at[e, rows, wide])
+
+        @pl.when((b >= n_moe) & (b < n_out))
+        def _():
+            act(out.at[rows, pl.ds(pl.multiple_of(which * block, block), block)])
+
+        @pl.when(b >= n_out)
+        def _():
+            at = pl.ds(pl.multiple_of((b - n_out) * piece, piece), piece)
+            wide = 2 * block
+            for first, n, to in ((0, 256, 0), (wide, 128, 256), (wide + wide // 2, 128, 384)):
+                col = pl.multiple_of(first + (2 * which + part) * n, 128)
+                act(qkv.at[at, pl.ds(col, n)], pl.ds(to, n))
+
+    def add(a, b):
+        return a.astype(F32) + b.astype(F32)
+
+    def hop(buf, sems, b, dev):
+        return remote(buf.at[b], buf.at[b], sems, b, dev)
+
+    def spread(b):
+        def act(dst, cut=None):
+            src = rc.at[b] if cut is None else rc.at[b, :, cut]
+            remote(src, dst, r.s_oth, 0, peer_core).start()
+            pltpu.make_async_copy(src, dst, r.s_out.at[0]).start()
+            remote(src, dst, r.s_far, b, peer_x).start()
+
+        place(b, x, core, act)
+
+    lag = 2
+    ahead = 16
+
+    def begin(b):
+        @pl.when(b < (n_moe if fused else items))
+        def _():
+            load(gm.at[0, 0, 0], b).wait()
+
+        @pl.when(b < n_out)
+        def _():
+            remote(gm.at[0, 0, 0], rc.at[b], r.s_rc, b, peer_core).wait_recv()
+            mine[b] = add(mine[b], rc[b]).astype(BF)
+
+        @pl.when(z == 0)
+        def _():
+            remote(mine.at[b], pre.at[b], r.s_pre, b, right).start()
+
+        @pl.when(z == last)
+        def _():
+            remote(mine.at[b], suf.at[b], r.s_suf, b, left).start()
+
+    def prefix(b):
+        hop(pre, r.s_pre, b, peer_x).wait_recv()
+        got = pre[b].astype(F32)
+        own = got + mine[b].astype(F32)
+
+        @pl.when(z == last)
+        def _():
+            rc[b] = own.astype(BF)
+
+        @pl.when(z < last)
+        def _():
+            @pl.when(2 * z >= slots)
+            def _():
+                rc[b] = (got + suf[b].astype(F32)).astype(BF)
+
+            pre[b] = own.astype(BF)
+            hop(pre, r.s_pre, b, right).start()
+
+        @pl.when(2 * z >= slots)
+        def _():
+            spread(b)
+
+    def suffix(b):
+        hop(suf, r.s_suf, b, peer_x).wait_recv()
+        got = suf[b].astype(F32)
+        own = got + mine[b].astype(F32)
+
+        @pl.when(z == 0)
+        def _():
+            rc[b] = own.astype(BF)
+
+        @pl.when(z > 0)
+        def _():
+            @pl.when(2 * z < slots)
+            def _():
+                rc[b] = (got + pre[b].astype(F32)).astype(BF)
+
+            suf[b] = own.astype(BF)
+            hop(suf, r.s_suf, b, left).start()
+
+        @pl.when(2 * z < slots)
+        def _():
+            spread(b)
+
+    def forward(b):
+        remote(rc.at[b], rc.at[b], r.s_far, b, peer_x).wait_recv()
+
+        def act(dst, cut=None):
+            remote(dst, dst, r.s_faro, 0, peer_core).start()
+
+        place(b, 1 - x, core, act)
+
+    def within(b, cond=True):
+        return (b >= 0) & (b < items) & cond
+
+    tsum, trecv, s_tiny = r.tsum, r.trecv, r.s_tiny
+
+    def tiny_swap(k, dev):
+        return remote(tsum.at[k], trecv.at[k], s_tiny, k, dev)
+
+    def tiny_add(k):
+        tiny_swap(k, peer_x).wait_recv()
+        tsum[k + 1] = add(tsum[k], trecv[k]).astype(BF)
+
+    def tiny_x():
+        tiny_swap(0, peer_x).start()
+
+    def tiny_core():
+        tiny_add(0)
+        tiny_swap(1, peer_core).start()
+
+    def tiny_spread():
+        tiny_add(1)
+        for k in range(1, slots):
+            remote(tsum.at[2], trecv.at[1 + k], s_tiny, 1 + k, other_z(k)).start()
+
+    def tiny_end():
+        total = tsum[2].astype(F32)
+        for k in range(1, slots):
+            remote(tsum.at[2], trecv.at[1 + k], s_tiny, 1 + k, other_z(k)).wait_recv()
+            total = total + trecv[1 + k].astype(F32)
+        r.tiny_out[...] = total
+
+    steps = {}
+    if fused:
+        s_fg = r.s_fg
+        dh, osum = r.dh, r.osum
+        keys = r.dkvs.shape[0]
+        tile = dh.shape[1]
+        owner = pl.multiple_of(f * block, block)
+        away = pl.multiple_of((1 - f) * block, block)
+        mine_rows, away_rows = pl.ds(owner, block), pl.ds(away, block)
+        near_cols = pl.ds(pl.multiple_of(x * block, block), block)
+        far_cols = pl.ds(pl.multiple_of((1 - x) * block, block), block)
+
+        send_dkv = remote(r.dkv.at[pl.ds(keys, keys)], r.rdkv, s_fg, 0, peer_y)
+        send_out = remote(r.gout.at[away_rows], r.rout, s_fg, 1, peer_y)
+        send_dh3 = remote(dh.at[3], r.rdh.at[1], s_fg, 2, peer_core)
+        send_dh1 = remote(dh.at[1], r.rdh.at[0], s_fg, 3, peer_core)
+        send_dhx = remote(r.dhx, r.rdx, s_fg, 4, peer_x)
+        send_cols = remote(r.cbuf.at[away_rows], r.rcol, s_fg, 5, peer_y)
+        send_outx = remote(r.osend, r.rox, s_fg, 6, peer_x)
+        send_tiny = remote(r.tbuf.at[1 - f], r.rtiny, s_fg, 7, peer_y)
+        eo_core = [
+            remote(r.eo.at[1 - core, i], rc.at[n_moe + i], r.s_rc, n_moe + i, peer_core)
+            for i in range(2)
+        ]
+        send_dkv.start()
+        send_out.start()
+
+        def sum_dkv():
+            for copy in loads:
+                copy.wait()
+            send_dkv.wait_recv()
+            r.dkvs[...] = add(r.dkvs[...], r.rdkv[...]).astype(BF)
+
+        def back_tile(t, first=False):
+            at = pl.ds(t * tile, tile)
+            cos, sin = r.cos_in[at, :], r.sin_in[at, :]
+            low_half = lax.broadcasted_iota(jnp.int32, cos.shape, 1) % HEAD_WIDTH < HEAD_WIDTH // 2
+            parts = []
+            for k in range(3):
+                w = r.dq_in[at, k * 128 : (k + 1) * 128] if k < 2 else r.dkvs[at, :128]
+                parts.append(rope_back(w.astype(F32), cos, sin, low_half).astype(BF))
+            parts.append(r.dkvs[at, 128:])
+            dproj = jnp.concatenate(parts, axis=1)
+            grad = mm_tn(r.h_in[at, :], dproj)
+            back = mm_nt(dproj, r.wc_in[...])
+            dh[t] = back.astype(BF)
+            normed, _ = rms_parts(r.tok_in[at, :].astype(F32))
+            gain = jnp.sum((back * normed).reshape(-1, 8, back.shape[1]), axis=0)
+            if first:
+                r.acc[...] = grad
+                r.gn[...] = gain
+            else:
+                r.acc[...] += grad
+                r.gn[...] += gain
+
+        def tile3():
+            back_tile(3, True)
+            send_dh3.start()
+
+        def tile1():
+            back_tile(1)
+            send_dh1.start()
+
+        def tile2():
+            back_tile(2)
+            send_dh3.wait_recv()
+            r.dhx[...] = add(dh[2], r.rdh[1]).astype(BF)
+            send_dhx.start()
+
+        def tile0():
+            back_tile(0)
+            r.cbuf[...] = r.acc[...].astype(BF)
+            send_cols.start()
+            total = jnp.sum(r.gn[...], axis=0, keepdims=True)
+            wide = tsum.shape[2]
+            row = lax.broadcasted_iota(jnp.int32, (tsum.shape[1], wide), 0) == 16
+            for k in range(2):
+                part = total[:, k * wide : (k + 1) * wide]
+                r.tbuf[k] = jnp.where(row, part, r.tiny[k]).astype(BF)
+            send_tiny.start()
+
+        def sum_out():
+            send_out.wait_recv()
+            osum[...] = add(r.gout_in[mine_rows, :], r.rout[...]).astype(BF)
+            r.osend[...] = osum[:, far_cols]
+            send_outx.start()
+
+        def tiny_y():
+            send_tiny.wait_recv()
+            tsum[0] = add(r.tbuf[f], r.rtiny[...]).astype(BF)
+            tiny_x()
+
+        def sum_cols():
+            send_cols.wait_recv()
+            v = add(r.cbuf[mine_rows, :], r.rcol[...]).astype(BF)
+            for i in range(4):
+                mine[n_out + i] = v[i * piece : (i + 1) * piece]
+
+        def sum_outx():
+            send_outx.wait_recv()
+            v = add(osum[:, near_cols], r.rox[...]).astype(BF)
+            for i in range(4):
+                r.eo[i // 2, i % 2] = v[i * piece : (i + 1) * piece]
+            for i in range(2):
+                eo_core[i].start()
+                mine[n_moe + i] = r.eo[core, i]
+
+        def inputs_back():
+            send_dh1.wait_recv()
+            send_dhx.wait_recv()
+            up_grad = add(dh[0], r.rdh[0]) + r.rdx[...].astype(F32)
+            normed, factor = rms_parts(r.tok_in[:tile].astype(F32))
+            d_n = up_grad * r.small[16:17, :].astype(F32)
+            r.dtok[...] = r.dmid_in[...] + factor * (
+                d_n - normed * jnp.mean(d_n * normed, axis=-1, keepdims=True)
+            )
+
+        order = [
+            None, sum_dkv, tile3, tile1, tile2, tile0, sum_out, tiny_y, sum_cols, tiny_core,
+            sum_outx, inputs_back, tiny_spread,
+        ]
+        steps = {2 * i + ahead - 2: fn for i, fn in enumerate(order) if fn is not None}
+    else:
+        tsum[0] = r.tiny[...].astype(BF)
+        tiny_x()
+        steps = {1: tiny_core, 2: tiny_spread}
+
+    @pl.loop(0, items + ahead + (last + 1) * lag)
+    def _(i):
+        for fn, b, cond in (
+            (begin, i, True),
+            (prefix, i - ahead - lag * z, z > 0),
+            (suffix, i - ahead - lag * (last - z), z < last),
+            (forward, i - ahead - lag * (last + 1), True),
+        ):
+            @pl.when(within(b, cond))
+            def _():
+                fn(b)
+
+        for k, fn in steps.items():
+            pl.when(i == k)(fn)
+
+    tiny_end()
+
+    @pl.loop(0, items)
+    def _(b):
+        one = rc.at[b]
+
+        @pl.when(b < n_out)
+        def _():
+            remote(one, one, r.s_rc, b, peer_core).wait_send()
+
+        @pl.when(z < last)
+        def _():
+            hop(pre, r.s_pre, b, peer_x).wait_send()
+
+        @pl.when(z > 0)
+        def _():
+            hop(suf, r.s_suf, b, peer_x).wait_send()
+
+        remote(one, one, r.s_far, b, peer_x).wait_send()
+
+    remote(rc, rc, r.s_oth, 0, peer_core).wait()
+    remote(rc, rc, r.s_faro, 0, peer_core).wait()
+    pltpu.make_async_copy(rc, rc, r.s_out.at[0]).wait()
+    tiny_swap(0, peer_x).wait_send()
+    tiny_swap(1, peer_core).wait_send()
+    for k in range(1, slots):
+        remote(tsum.at[2], trecv.at[1 + k], s_tiny, 1 + k, other_z(k)).wait_send()
+    if fused:
+        for copy in (send_dkv, send_out, send_dh3, send_dh1, send_dhx, send_cols, send_outx, send_tiny):
+            copy.wait_send()
+
+
+def reduce_grads(gm, tiny, slots, shards, eo=None, cols=None, fused=None):
+    count, _, ff, _ = gm.shape
+    width = 2 * ff
+    nb = 6 * count
+    piece = ff // 4
+    items = 2 * nb + 6
+    hbm = pl.BlockSpec(memory_space=pl.ANY)
+    vmem = pl.BlockSpec(memory_space=pltpu.VMEM)
+    dma = pltpu.SemaphoreType.DMA
+    args = dict(gm=(gm.reshape(nb, 2, 2, piece, ff), hbm), tiny=(tiny, vmem))
+    outs = dict(
+        gate=(jax.ShapeDtypeStruct((2 * count, width, ff), BF), hbm),
+        up=(jax.ShapeDtypeStruct((2 * count, width, ff), BF), hbm),
+        down=(jax.ShapeDtypeStruct((2 * count, ff, width), BF), hbm),
+        out=(jax.ShapeDtypeStruct((ff, width), BF), hbm),
+        qkv=(jax.ShapeDtypeStruct((ff, 2 * width), BF), hbm),
+        tiny_out=(jax.ShapeDtypeStruct(tiny.shape[-2:], F32), vmem),
+    )
+    buf = pltpu.VMEM((items, piece, ff), BF)
+    scratch = dict(
+        mine=buf, rc=buf, pre=buf, suf=buf,
+        tsum=pltpu.VMEM((3,) + tiny.shape[-2:], BF),
+        trecv=pltpu.VMEM((slots + 1,) + tiny.shape[-2:], BF),
+        s_tiny=dma((2, slots + 1)), s_mine=dma((items,)), s_out=dma((1,)),
+    )
+    each = dma((2, items))
+    scratch.update(s_rc=each, s_pre=each, s_suf=each, s_far=each)
+    scratch.update(s_oth=dma((2, 1)), s_faro=dma((2, 1)))
+    if fused is None:
+        args.update(
+            eo=(eo.reshape(2, 2, piece, ff), hbm), cols=(cols.reshape(4, piece, ff), hbm)
+        )
+    else:
+        inner = {}
+        for k, v in fused.items():
+            args[k] = (v, hbm)
+            inner[k] = pltpu.VMEM(v.shape, v.dtype)
+        args.update(small=(fused.pop("small"), vmem))
+        rows = args["dmid"][0].shape[0]
+        keys = args["dkv"][0].shape[0] // 2
+        outs.update(dtok=(jax.ShapeDtypeStruct((rows, width), F32), vmem))
+        scratch.update(
+            rdkv=pltpu.VMEM((keys, 256), BF), dkvs=pltpu.VMEM((keys, 256), BF),
+            rout=pltpu.VMEM((ff, width), BF), osum=pltpu.VMEM((ff, width), BF),
+            osend=pltpu.VMEM((ff, ff), BF), rox=pltpu.VMEM((ff, ff), BF),
+            eo=pltpu.VMEM((2, 2, piece, ff), BF),
+            dq_in=inner["dq"], wc_in=inner["wc"], cos_in=inner["cos"], sin_in=inner["sin"],
+            h_in=inner["h"], tok_in=inner["tok"], gout_in=inner["gout"], dmid_in=inner["dmid"],
+            s_in=dma((9,)),
+            dh=pltpu.VMEM((4, rows, width), BF), rdh=pltpu.VMEM((2, rows, width), BF),
+            dhx=pltpu.VMEM((rows, width), BF), rdx=pltpu.VMEM((rows, width), BF),
+            acc=pltpu.VMEM((width, ff), F32), gn=pltpu.VMEM((8, width), F32),
+            cbuf=pltpu.VMEM((width, ff), BF), rcol=pltpu.VMEM((ff, ff), BF),
+            tbuf=pltpu.VMEM(tiny.shape, BF), rtiny=pltpu.VMEM(tiny.shape[-2:], BF),
+            s_fg=dma((2, 8)),
+        )
+    names = tuple(args) + tuple(outs) + tuple(scratch)
+    got = pl.pallas_call(
+        functools.partial(
+            reduce_kernel, names=names, slots=slots, shards=shards, fused=fused is not None
+        ),
+        in_specs=[v[1] for v in args.values()],
+        out_specs=[v[1] for v in outs.values()],
+        out_shape=[v[0] for v in outs.values()],
+        scratch_shapes=list(scratch.values()),
+        compiler_params=params(collective_id=1, has_side_effects=True),
+        name="reduce_grads",
+    )(*[v[0] for v in args.values()])
+    return types.SimpleNamespace(**dict(zip(outs, got)))
 
 
 def gather_rows(x):
@@ -477,7 +1478,7 @@
     slots = lax.axis_size("dp")
     assert groups == 4
     seq, fsdp = lax.axis_index("seq"), lax.axis_index("fsdp")
-    core = seq % 2
+    core, far = seq % 2, seq // 2
     rows, width = tokens.shape[1:]
     span = rows // 2
     x = tokens[0]
@@ -496,146 +1497,168 @@
         held = jnp.arange(shards)
     ktab = jnp.transpose(jnp.take(table, held, axis=1), (1, 0, 2)).reshape(-1)
     qpos = (qtab[:, None] * span + jnp.arange(span, dtype=jnp.int32)[None, :]).reshape(-1)
-    half = HEAD_WIDTH // 2
-    freqs = jnp.exp(jnp.arange(half, dtype=F32) * (-2.0 * math.log(ROPE_BASE) / HEAD_WIDTH))
-    angles = qpos.astype(F32)[:, None] * freqs[None, :]
-    cos = jnp.tile(jnp.cos(angles), (1, 4))
-    sin = jnp.tile(jnp.sin(angles), (1, 4))
 
     heads = QUERY_HEADS // groups
     qw, kw = heads * HEAD_WIDTH, KEY_VALUE_HEADS // groups * HEAD_WIDTH
     w3 = query_key_value_weight
-    wq = lax.dynamic_slice_in_dim(w3, seq * qw, qw, 1).reshape(-1, 2, 2, HEAD_WIDTH)
-    wq = jnp.swapaxes(wq, 1, 2).reshape(-1, qw)
-    wk = lax.dynamic_slice_in_dim(w3, QUERY_HEADS * HEAD_WIDTH + seq * kw, kw, 1)
-    wv = lax.dynamic_slice_in_dim(w3, (QUERY_HEADS + KEY_VALUE_HEADS) * HEAD_WIDTH + seq * kw, kw, 1)
-    wcols = gather_rows(jnp.concatenate([wq, wk, wv], axis=1))
-    small = jnp.concatenate([norm1[:, None], norm2[:, None], router], axis=1)
-    small = gather_rows(small)
-    gain_one = small[:, 0].astype(F32)
-    gain_two = small[:, 1].astype(F32)
-    route_full = small[:, 2:]
-    out_full = gather_rows(w_out)
-
-    tok = gather_seq(x).reshape(groups * rows, width)
-    hidden_one, q, kv_own = project(tok, gain_one[None], wcols, cos, sin, rows)
-    kv = gather_fsdp(kv_own)
+    small = jnp.concatenate(
+        [jnp.transpose(router), norm1[None], norm2[None], jnp.zeros((14, norm1.shape[0]), BF)]
+    )
+    if shards == 2:
+        tok, wcols, small, hidden_one, q, kv, cos, sin = front(qtab, order.shape[0], x, w3, small)
+        tok, kv = tok.reshape(groups * rows, width), kv.reshape(-1, 256)
+        w_out, cotangent, kv = lax.optimization_barrier((w_out, cotangent, kv))
+    else:
+        half = HEAD_WIDTH // 2
+        freqs = jnp.exp(jnp.arange(half, dtype=F32) * (-2.0 * math.log(ROPE_BASE) / HEAD_WIDTH))
+        angles = qpos.astype(F32)[:, None] * freqs[None, :]
+        cos, sin = jnp.tile(jnp.cos(angles), (1, 4)), jnp.tile(jnp.sin(angles), (1, 4))
+        wq = lax.dynamic_slice_in_dim(w3, seq * qw, qw, 1)
+        wk = lax.dynamic_slice_in_dim(w3, QUERY_HEADS * HEAD_WIDTH + seq * kw, kw, 1)
+        wv = lax.dynamic_slice_in_dim(
+            w3, (QUERY_HEADS + KEY_VALUE_HEADS) * HEAD_WIDTH + seq * kw, kw, 1
+        )
+        wcols = gather_rows(jnp.concatenate([wq, wk, wv], axis=1))
+        small = lax.all_gather(small, "fsdp", axis=1, tiled=True)
+        tok = gather_seq(x).reshape(groups * rows, width)
+        hidden_one, q, kv_own = project(tok, small[16:17].astype(F32), wcols, cos, sin, rows)
+        kv = gather_fsdp(kv_own)
+    gain_one, gain_two = small[16].astype(F32), small[17].astype(F32)
+    route_rows = small[:n_experts]
+
     kb = 4 * span
-    attended, lse = attend(qtab, ktab, limit, q, kv, span, kb)
-    sent = attended.astype(BF).reshape(groups, rows, qw)
-    got = jnp.stack(swap_seq([sent[m] for m in range(groups)]))
-    got = jnp.take(got, relative, axis=0).reshape(groups, rows, 2, 2, HEAD_WIDTH)
-    token_out = jnp.transpose(got, (1, 0, 3, 2, 4)).reshape(rows, groups * qw)
-
     own_valid = (qpos[:rows] < limit[0])[:, None]
+    masked_cot = jnp.where(own_valid, cotangent[0], jnp.zeros_like(cotangent[0]))
+    if shards == 2:
+        wo_there, cot_y, cot_x = flip_y(w_out), flip_y(masked_cot), flip_x(masked_cot)
+    attended, low, lse = attend(qtab, ktab, limit, q, kv, span, kb)
     inputs = x.astype(F32)
-    middle = inputs + mm(token_out, out_full)
-    normed_two, factor_two = rms_parts(middle)
-    hidden_two = (normed_two * gain_two).astype(BF)
-    logits = mm(hidden_two, route_full)
-    chosen = jnp.any(
-        routes[0][:, :, None] == jnp.arange(n_experts, dtype=jnp.int32)[None, None, :], axis=1
+    if shards == 2:
+        out = moe_layer(
+            low, x, w_out, wo_there, small, routes[0], masked_cot, cot_y, cot_x, w_gate, w_up, w_down
+        )
+        parts = [out.moe0, flip_y(out.moe1), flip_x(out.moe2), flip_xy(out.moe3)]
+        d_heads = out.do.reshape(groups * rows, qw)
+        middle, d_middle, grad_out, tiny = out.middle, out.dmid, out.gout, out.tiny
+        weight_grads = out.grads.reshape(count, 6, w_gate.shape[2], -1)
+    else:
+        sent = low.reshape(groups, rows, qw)
+        got = jnp.stack(swap_seq([sent[m] for m in range(groups)]))
+        got = jnp.take(got, relative, axis=0)
+        token_out = jnp.transpose(got, (1, 0, 2)).reshape(rows, groups * qw)
+        out_full = gather_rows(w_out)
+
+        middle = inputs + mm(token_out, out_full)
+        normed_two, factor_two = rms_parts(middle)
+        hidden_two = (normed_two * gain_two).astype(BF)
+        logits = mm_nt(hidden_two, route_rows)
+        chosen = jnp.any(
+            routes[0][:, :, None] == jnp.arange(n_experts, dtype=jnp.int32)[None, None, :], axis=1
+        )
+        top = jnp.max(jnp.where(chosen, logits, NEG), axis=-1, keepdims=True)
+        raised = jnp.where(chosen, jnp.exp(logits - top), 0.0)
+        gates = raised / jnp.sum(raised, axis=-1, keepdims=True)
+
+        def share(v):
+            near = gather_rows(v)
+            return jnp.concatenate([near, flip_x(near)])
+
+        cot_all = share(masked_cot)
+        extended = jnp.concatenate(
+            [hidden_two, gates.astype(BF), jnp.zeros((rows, 128 - n_experts), BF)], axis=1
+        )
+        hid_all = share(extended)
+        base = jnp.stack([far * count, fsdp * owned + far * count]).astype(jnp.int32)
+        part = rows * 4
+        moe_parts, dh_parts, weight_grads = [], [], None
+        for i in range(hid_all.shape[0] // part):
+            got = experts(
+                base, count, hid_all[i * part : (i + 1) * part], cot_all[i * part : (i + 1) * part],
+                w_gate, w_up, w_down, rows,
+            )
+            moe_parts.append(got[0])
+            dh_parts.append(got[1])
+            if weight_grads is None:
+                weight_grads = got[2]
+            else:
+                weight_grads = (weight_grads.astype(F32) + got[2].astype(F32)).astype(BF)
+
+        def give_back(parts):
+            v = jnp.concatenate(parts) if len(parts) > 1 else parts[0]
+            n = v.shape[0] // 2
+            near = v[:n].astype(F32) + flip_x(v[n:]).astype(F32)
+            return lax.psum_scatter(near.astype(BF), "fsdp", scatter_dimension=0, tiled=True).astype(F32)
+
+        d_ext = give_back(dh_parts)
+        d_gates = d_ext[:, width : width + n_experts]
+        d_logits = (gates * (d_gates - jnp.sum(gates * d_gates, axis=-1, keepdims=True))).astype(BF)
+        grad_router = mm_tn(hidden_two, d_logits)
+        d_hidden = d_ext[:, :width] + mm(d_logits, route_rows)
+        grad_norm2 = jnp.sum(d_hidden * normed_two, axis=0)
+        d_n = d_hidden * gain_two
+        d_middle = masked_cot.astype(F32) + factor_two * (
+            d_n - normed_two * jnp.mean(d_n * normed_two, axis=-1, keepdims=True)
+        )
+        d_attn = d_middle.astype(BF)
+        grad_out = mm_tn(token_out, d_attn).astype(BF)
+        d_token_out = mm_nt(d_attn, out_full).astype(BF)
+        d_heads = jnp.transpose(d_token_out.reshape(rows, groups, qw), (1, 0, 2))
+        d_heads = jnp.take(d_heads, relative, axis=0)
+        d_heads = jnp.concatenate(swap_seq([d_heads[m] for m in range(groups)]))
+    dq, dkv = attend_back(qtab, ktab, limit, q, kv, d_heads, attended, lse, span, kb)
+
+    block = w_gate.shape[2]
+    shard_rows = width // shards
+
+    def tiny_rows(first):
+        return jnp.concatenate(
+            [jnp.transpose(grad_router), first[None], grad_norm2[None], jnp.zeros((14, width), F32)]
+        ).reshape(32, shards, shard_rows).transpose(1, 0, 2)
+
+    if shards == 2:
+        got = reduce_grads(
+            weight_grads, tiny, slots, shards,
+            fused=dict(
+                dkv=dkv, dq=dq, tok=tok, h=hidden_one, wc=wcols, cos=cos, sin=sin,
+                small=small, dmid=d_middle, gout=grad_out,
+            ),
+        )
+        d_inputs = got.dtok
+    else:
+        dh_one, grad_cols, grad_norm1 = project_back(
+            tok, hidden_one, dq, scatter_fsdp(dkv), wcols, cos, sin, rows
+        )
+        dh_one = dh_one.reshape(groups, rows, width)
+        near = dh_one[0::2].astype(F32) + flip_core(dh_one[1::2]).astype(F32)
+        d_hidden_one = near[0] + flip_x(near[1].astype(BF)).astype(F32)
+        normed_one, factor_one = rms_parts(inputs)
+        d_n = d_hidden_one * gain_one
+        d_inputs = d_middle + factor_one * (
+            d_n - normed_one * jnp.mean(d_n * normed_one, axis=-1, keepdims=True)
+        )
+
+        def to_owner(g):
+            part = lax.psum_scatter(g, "fsdp", scatter_dimension=0, tiled=True)
+            return jnp.pad(part, ((0, block - part.shape[0]), (0, 0)))
+
+        cols = to_owner(grad_cols)
+        mine = to_owner(grad_out).reshape(block, 2, block)
+        kept = lax.dynamic_index_in_dim(mine, far, 1, keepdims=False)
+        sent = lax.dynamic_index_in_dim(mine, 1 - far, 1, keepdims=False)
+        outs = (kept.astype(F32) + flip_x(sent).astype(F32)).astype(BF)
+        tiny = tiny_rows(jnp.sum(grad_norm1, axis=0))
+        tiny = lax.psum_scatter(tiny, "fsdp", scatter_dimension=0, tiled=True)[0]
+        got = reduce_grads(weight_grads, tiny, slots, shards, eo=outs, cols=cols)
+    grad_gate, grad_up, grad_down, shard_out, shard_qkv, *tiny = widen(
+        [got.gate, got.up, got.down, got.out, got.qkv], got.tiny_out, n_experts
     )
-    top = jnp.max(jnp.where(chosen, logits, NEG), axis=-1, keepdims=True)
-    raised = jnp.where(chosen, jnp.exp(logits - top), 0.0)
-    gates = raised / jnp.sum(raised, axis=-1, keepdims=True)
-    masked_cot = jnp.where(own_valid, cotangent[0], jnp.zeros_like(cotangent[0]))
-
-    def share(v):
-        near = gather_fsdp(v)
-        return jnp.concatenate([near, flip_core(near)])
-
-    cot_all = share(masked_cot)
-    extended = jnp.concatenate(
-        [hidden_two, gates.astype(BF), jnp.zeros((rows, 128 - n_experts), BF)], axis=1
-    )
-    hid_all = share(extended)
-    base = jnp.stack([core * count, fsdp * owned + core * count]).astype(jnp.int32)
-    part = rows * 4
-    moe_parts, dh_parts, weight_grads = [], [], None
-    for i in range(hid_all.shape[0] // part):
-        got = experts(
-            base, count, hid_all[i * part : (i + 1) * part], cot_all[i * part : (i + 1) * part],
-            w_gate, w_up, w_down, rows,
-        )
-        moe_parts.append(got[0])
-        dh_parts.append(got[1])
-        if weight_grads is None:
-            weight_grads = list(got[2:])
-        else:
-            weight_grads = [a.astype(F32) + b.astype(F32) for a, b in zip(weight_grads, got[2:])]
-            weight_grads = [a.astype(BF) for a in weight_grads]
-
-    def give_back(parts):
-        v = jnp.concatenate(parts) if len(parts) > 1 else parts[0]
-        n = v.shape[0] // 2
-        near = v[:n].astype(F32) + flip_core(v[n:]).astype(F32)
-        return scatter_fsdp(near.astype(BF))
-
-    d_ext = give_back(dh_parts)
-    d_gates = d_ext[:, width : width + n_experts]
-    d_logits = (gates * (d_gates - jnp.sum(gates * d_gates, axis=-1, keepdims=True))).astype(BF)
-    grad_router = mm_tn(hidden_two, d_logits)
-    d_hidden = d_ext[:, :width] + mm_nt(d_logits, route_full)
-    grad_norm2 = jnp.sum(d_hidden * normed_two, axis=0)
-    d_n = d_hidden * gain_two
-    d_middle = masked_cot.astype(F32) + factor_two * (
-        d_n - normed_two * jnp.mean(d_n * normed_two, axis=-1, keepdims=True)
-    )
-    d_attn = d_middle.astype(BF)
-    grad_out = mm_tn(token_out, d_attn).astype(BF)
-    d_token_out = mm_nt(d_attn, out_full).astype(BF)
-    d_heads = d_token_out.reshape(rows, groups, 2, 2, HEAD_WIDTH)
-    d_heads = jnp.transpose(d_heads, (1, 0, 3, 2, 4)).reshape(groups, rows, qw)
-    d_heads = jnp.take(d_heads, relative, axis=0)
-    d_heads = jnp.concatenate(swap_seq([d_heads[m] for m in range(groups)]))
-    dq, dkv = attend_back(qtab, ktab, limit, q, kv, d_heads, attended, lse, span, kb)
-    dkv = scatter_fsdp(dkv)
-    dh_one, grad_cols, grad_norm1 = project_back(
-        tok, hidden_one, dq, dkv, wcols, cos, sin, rows
-    )
-    dh_one = dh_one.reshape(groups, rows, width)
-    near = dh_one[0::2].astype(F32) + flip_core(dh_one[1::2]).astype(F32)
-    d_hidden_one = near[0] + flip_x(near[1].astype(BF)).astype(F32)
-    normed_one, factor_one = rms_parts(inputs)
-    d_n = d_hidden_one * gain_one
-    d_inputs = d_middle + factor_one * (
-        d_n - normed_one * jnp.mean(d_n * normed_one, axis=-1, keepdims=True)
-    )
-
-    every = ("dp", "seq")
-    fold = [[d * groups + 2 * i + c for d in range(slots) for i in range(groups // 2)] for c in range(2)]
-
-    def reduce_experts(g):
-        part = lax.psum_scatter(
-            g, every, scatter_dimension=1, tiled=True, axis_index_groups=fold
-        )
-        full = lax.all_gather(part, every, axis=0)
-        n, r, m = part.shape
-        full = full.reshape(slots, groups // 2, 2, n, r, m)
-        full = jnp.transpose(full, (2, 3, 0, 1, 4, 5))
-        return full.reshape(2 * n, slots * groups // 2 * r, m).astype(F32)
-
-    grad_gate, grad_up, grad_down = [reduce_experts(g) for g in weight_grads]
-    shard_out = lax.psum(
-        lax.psum_scatter(grad_out, "fsdp", scatter_dimension=0, tiled=True), every
-    ).astype(F32)
-    shard_cols = lax.psum(
-        lax.psum_scatter(grad_cols, "fsdp", scatter_dimension=0, tiled=True), "dp"
-    )
-    cols = lax.all_gather(shard_cols, "seq", axis=0)
-    gq = cols[:, :, :qw].reshape(groups, -1, 2, 2, HEAD_WIDTH)
-    gq = jnp.transpose(gq, (1, 0, 3, 2, 4)).reshape(-1, groups * qw)
-    gk = jnp.transpose(cols[:, :, qw : qw + kw], (1, 0, 2)).reshape(-1, groups * kw)
-    gv = jnp.transpose(cols[:, :, qw + kw :], (1, 0, 2)).reshape(-1, groups * kw)
-    shard_qkv = jnp.concatenate([gq, gk, gv], axis=1).astype(F32)
-    tiny = jnp.concatenate(
-        [jnp.sum(grad_norm1, axis=0)[:, None], grad_norm2[:, None], grad_router], axis=1
-    )
-    tiny = lax.psum(lax.psum_scatter(tiny, "fsdp", scatter_dimension=0, tiled=True), every)
-    layer_out = (middle + give_back(moe_parts)).astype(BF)
+    shard_out, shard_qkv = shard_out[:shard_rows], shard_qkv[:shard_rows]
+    if shards == 2:
+        layer_out = (middle + sum(p.astype(F32) for p in parts)).astype(BF)
+    else:
+        layer_out = (middle + give_back(moe_parts)).astype(BF)
     return (
-        layer_out[None], d_inputs[None], tiny[:, 0], shard_qkv, shard_out, tiny[:, 1], tiny[:, 2:],
+        layer_out[None], d_inputs[None], tiny[0], shard_qkv, shard_out, tiny[1], tiny[2],
         grad_gate, grad_up, grad_down,
     )
 

time: 1130 us -> 488 us (0.43)
  waiting for transfers between devices: 733 us -> 0.02 us
  Pallas kernels: 124 us -> 457 us
  blocking collectives: 88.8 us -> 0 us
  other arithmetic: 70.5 us -> 4.53 us
  local copies, waits for them, and re-layouts: 68.8 us -> 9.64 us
  between operations: 15.7 us -> 1.49 us
    reduce_scatter x6 -> x0, waiting for transfers between devices: 363 us -> none  [the longest x3 277 us: reduce_experts(): lax.psum_scatter(g, every, scatter_dimension=1, tiled=True, axis_index_gr...]
    pallas_call x3 -> x4, Pallas kernels: 83.9 us -> 390 us  [the longest x1 218 us: reduce_grads(): pl.pallas_call(functools.partial(reduce_kernel, names=names, slots=slots,...]
    all_gather x6 -> x0, waiting for transfers between devices: 190 us -> none  [the longest x3 169 us: reduce_experts(): full = lax.all_gather(part, every, axis=0)]
    ppermute x17 -> x4, waiting for transfers between devices: 102 us -> 0.01 us  [the longest x3 0.01 us: flip_y(): return lax.ppermute(x, 'fsdp', [(0, 1), (1, 0)])]
    psum x2 -> x0, waiting for transfers between devices: 69.7 us -> none  [the longest x1 40.5 us: local(): lax.psum(lax.psum_scatter(grad_cols, 'fsdp', scatter_dimension=0, tiled=T...]
    psum x1 -> x0, blocking collectives: 62.4 us -> none  [local(): lax.psum(lax.psum_scatter(tiny, 'fsdp', scatter_dimension=0, tiled=True),...]
    convert_element_type x12 -> x0, other arithmetic: 44.8 us -> none  [the longest x3 35.3 us: reduce_experts(): return full.reshape(2 * n, slots * groups // 2 * r, m).astype(F32)]
    convert_element_type x6 -> x0, local copies, waits for them, and re-layouts: 38.5 us -> none  [the longest x3 36.1 us: reduce_experts(): return full.reshape(2 * n, slots * groups // 2 * r, m).astype(F32)]
  transfers between devices with their start and end apart: 35 -> 6, of which waited for: 24 -> 0; matrix products, arithmetic and copies ran while one was open for 9% -> 1% of each run, Pallas kernels for 3% -> 65%
where the time goes in v3:
time: 488 us; the launch traced here: 482 us
  Pallas kernels  457 us (94%)
  local copies, waits for them, and re-layouts  9.64 us (2%)
  starting transfers between devices  9.38 us (2%)
    pallas_call x1, Pallas kernels, reduce_grads(): pl.pallas_call(functools.partial(reduce_kernel, names=names, slots=slots,...  218 us
    pallas_call x1, Pallas kernels, moe_layer(): pl.pallas_call(functools.partial(moe_kernel, names=names, topk=routes.sha...  106 us
    pallas_call x1, Pallas kernels, front(): pl.pallas_call(front_kernel, in_specs=[pl.BlockSpec(memory_space=pltpu.SM...  35.2 us
    pallas_call x1, Pallas kernels, attend_back(): pl.pallas_call(functools.partial(attend_back_kernel, span=span, kb=kb), g...  34.7 us
    pallas_call x1, Pallas kernels, attend(): pl.pallas_call(functools.partial(attend_kernel, span=span, kb=kb), grid_s...  32.7 us
    pallas_call x1, Pallas kernels, widen(): pl.pallas_call(widen_kernel, grid=(steps,), in_specs=specs + [whole(tiny....  30.6 us
  transfers between devices with their start and end apart: 6, of which 0 were waited for; matrix products, arithmetic and copies ran while one was open for 1% of the time, Pallas kernels for 65%

profile of v3, /device:TPU:0, one launch (start us, length us, event | category | flops | bytes accessed | tf_op | source)
XLA Modules:
  0.0 482.3 jit_solution(5241244161026874826)
XLA Ops:
  0.7 0.8 broadcast_in_dim.52
  1.5 0.7 broadcast_in_dim.53
  2.2 0.7 reshape.198
  2.9 0.6 gather_fusion
  3.6 0.6 select_n.71.spans.qtab_ref
  4.3 1.4 maximum_maximum_fusion.small
  5.7 35.2 %front.1 = (bf16[4,320,1024]{2,1,0:T(8,128)(2,1)}, bf16[1024,512]{1,0:T(8,128)(2,1)}, bf16[32,1024]{1,0:T(8,128)(2,1)}, bf16[1280,1024]{1,0:T(8,128)(2,1)}, bf16...) custom-call(s32[8]{0:T(128)} %select_n.71.spans.qtab_ref, ...), custom_call_target="tpu_custom_call" | custom-call | tf_op jit(solution)/shard_map/front/pallas_call | solution.py:221
  40.9 1.6 collective-permute-start
  43.5 1.5 collective-permute-start.2
  44.9 0.6 collective-permute-start.1
  45.7 0.6 gather_fusion.1
  46.6 0.6 reshape.199.ktab_ref
  47.2 0.8 copy.34
  48.0 32.7 %attend.1 = (f32[1280,256]{1,0:T(8,128)}, bf16[1280,256]{1,0:T(8,128)(2,1)}, f32[8,8,640]{2,1,0:T(8,128)}) custom-call(s32[8]{0:T(128)} %select_n.71.spans.qtab_ref, s32[16]{0:T(128)} %reshape.199.ktab_ref, s32[1]{0:T(128)} %copy.37.len_ref, bf16[1280,256]{1,0:T(8,128)(2,1)} %get-tuple-element.51.q_ref, bf16[2560,256]{1,0:T(8,128)(2,1)} %bitcast.36), custom_call_target="tpu_custom_call" | custom-call | tf_op jit(solution)/shard_map/attend/pallas_call | solution.py:419
  80.7 1.0 copy-done.4
  81.9 106.2 %moe_layer.1 = (f32[320,1024]{1,0:T(8,128)}, bf16[320,1024]{1,0:T(8,128)(2,1)}, bf16[320,1024]{1,0:T(8,128)(2,1)}, bf16[320,1024]{1,0:T(8,128)(2,1)}, bf16[320,1...) custom-call(bf16[4,320,256]{2,1,0:T(8,128)(2,1)} %bitcast.44, ...), custom_call_target="tpu_custom_call" | custom-call | tf_op jit(solution)/shard_map/moe_layer/pallas_call | solution.py:947
  188.1 4.2 collective-permute-start.3
  192.3 1.2 collective-permute-start.4
  193.8 34.7 %attend_back.1 = (bf16[1280,256]{1,0:T(8,128)(2,1)}, bf16[2560,256]{1,0:T(8,128)(2,1)}) custom-call(s32[8]{0:T(128)} %select_n.71.spans.qtab_ref, s32[16]{0:T(128)} %reshape.199.ktab_ref, s32[1]{0:T(128)} %copy.37.len_ref, bf16[1280,256]{1,0:T(8,128)(2,1)} %get-tuple-element.51.q_ref, bf16[2560,256]{1,0:T(8,128)(2,1)} %bitcast.37, ...), custom_call_target="tpu_custom_call" | custom-call | tf_op jit(solution)/shard_map/attend_back/pallas_call | solution.py:505
  228.5 217.9 %reduce_grads.1 = (bf16[8,1024,512]{2,1,0:T(8,128)(2,1)}, bf16[8,1024,512]{2,1,0:T(8,128)(2,1)}, bf16[8,512,1024]{2,1,0:T(8,128)(2,1)}, bf16[512,1024]{1,0:T(8,1...) custom-call(bf16[24,2,2,128,512]{4,3,2,1,0:T(8,128)(2,1)} %bitcast.32, ...), custom_call_target="tpu_custom_call" | custom-call | tf_op jit(solution)/shard_map/reduce_grads/pallas_call | solution.py:1454
  446.4 30.6 %widen.1 = (f32[8192,512]{1,0:T(8,128)}, f32[8192,512]{1,0:T(8,128)}, f32[4096,1024]{1,0:T(8,128)}, f32[512,1024]{1,0:T(8,128)}, f32[512,2048]{1,0:T(8,128)}, /*...) custom-call(bf16[8192,512]{1,0:T(8,128)(2,1)} %bitcast.33, bf16[8192,512]{1,0:T(8,128)(2,1)} %bitcast.34, ...), custom_call_target="tpu_custom_call" | custom-call | tf_op jit(solution)/shard_map/widen/pallas_call | solution.py:266
  477.0 1.7 copy.35
  478.7 2.6 fusion
  481.3 1.1 copy.38
  (43 shorter events, 1.5 us)
Async XLA Ops:
  0.6 40.3 %copy-start.3 = (bf16[512,1024]{1,0:T(8,128)(2,1)S(1)}, bf16[512,1024]{1,0:T(8,128)(2,1)}, u32[]{:S(2)}) copy-start(bf16[512,1024]{1,0:T(8,128)(2,1)} %refs_2_) | copy-start | bytes 3145732
  0.7 42.7 %copy-start.6 = (bf16[1,320,1024]{2,1,0:T(8,128)(2,1)S(1)}, bf16[1,320,1024]{2,1,0:T(8,128)(2,1)}, u32[]{:S(2)}) copy-start(bf16[1,320,1024]{2,1,0:T(8,128)(2,1)} %param.16) | copy-start | bytes 1966084
  4.2 38.3 %copy-start.9 = (s32[8]{0:T(128)S(1)}, s32[8]{0:T(128)}, u32[]{:S(2)}) copy-start(s32[8]{0:T(128)} %select_n.71.spans.qtab_ref) | copy-start | bytes 100
  5.7 41.5 %copy-start.8 = (s32[1,320,8]{1,2,0:T(8,128)S(1)}, s32[1,320,8]{1,2,0:T(8,128)}, u32[]{:S(2)}) copy-start(s32[1,320,8]{1,2,0:T(8,128)} %param.19) | copy-start | bytes 30724
  40.9 39.7 %collective-permute-start = (bf16[512,1024]{1,0:T(8,128)(2,1)S(1)}, bf16[512,1024]{1,0:T(8,128)(2,1)S(1)}, u32[]{:S(2)}, u32[]{:S(2)}) collective-permute-start(bf16[512,1024]{1,0:T(8,128)(2,1)S(1)} %copy-done.3), channel_id=1, source_target_pairs={{0,1},{1,0},{2,3},{3,2},{4,5},{5,4},{6,7},{7,6},{8,9},{9,8},{10,11... | collective-permute-start | bytes 3145736 | tf_op jit(solution)/shard_map/ppermute | solution.py:974
  43.5 1.5 copy-start
  43.5 37.2 %collective-permute-start.2 = (bf16[320,1024]{1,0:T(8,128)(2,1)S(1)}, bf16[320,1024]{1,0:T(8,128)(2,1)S(1)}, u32[]{:S(2)}, u32[]{:S(2)}) collective-permute-start(bf16[320,1024]{1,0:T(8,128)(2,1)S(1)} %bitcast_select_fusion.refs_6_), channel_id=1, source_target_pairs={{0,4},{4,0},{2,6},{6,2},{1,5},{5,1},{3,7},{7,3},{8,12},{12,8},{10,... | collective-permute-start | bytes 1966088 | tf_op jit(solution)/shard_map/ppermute | solution.py:966
  44.9 35.7 %collective-permute-start.1 = (bf16[320,1024]{1,0:T(8,128)(2,1)S(1)}, bf16[320,1024]{1,0:T(8,128)(2,1)}, u32[]{:S(2)}, u32[]{:S(2)}) collective-permute-start(bf16[320,1024]{1,0:T(8,128)(2,1)S(1)} %bitcast_select_fusion.refs_6_), channel_id=1, source_target_pairs={{0,1},{1,0},{2,3},{3,2},{4,5},{5,4},{6,7},{7,6},{8,9},{9,8},{10,11... | collective-permute-start | bytes 1966088 | tf_op jit(solution)/shard_map/ppermute | solution.py:974
  80.7 1.2 copy-start.7
  80.7 1.0 copy-start.4
  188.1 290.6 %collective-permute-start.3 = (bf16[320,1024]{1,0:T(8,128)(2,1)}, bf16[320,1024]{1,0:T(8,128)(2,1)S(1)}, u32[]{:S(2)}, u32[]{:S(2)}) collective-permute-start(bf16[320,1024]{1,0:T(8,128)(2,1)} %get-tuple-element.60), channel_id=1, source_target_pairs={{0,1},{1,0},{2,3},{3,2},{4,5},{5,4},{6,7},{7,6},{8,9},{9,8},{10,11... | collective-permute-start | bytes 1966088 | tf_op jit(solution)/shard_map/ppermute | solution.py:974
  192.3 286.4 %collective-permute-start.4 = (bf16[320,1024]{1,0:T(8,128)(2,1)}, bf16[320,1024]{1,0:T(8,128)(2,1)S(1)}, u32[]{:S(2)}, u32[]{:S(2)}) collective-permute-start(bf16[320,1024]{1,0:T(8,128)(2,1)} %get-tuple-element.61), channel_id=1, source_target_pairs={{0,4},{4,0},{2,6},{6,2},{1,5},{5,1},{3,7},{7,3},{8,12},{12,8},{10,... | collective-permute-start | bytes 1966088 | tf_op jit(solution)/shard_map/ppermute | solution.py:966
  193.4 285.2 %collective-permute-start.5 = (bf16[320,1024]{1,0:T(8,128)(2,1)}, bf16[320,1024]{1,0:T(8,128)(2,1)}, u32[]{:S(2)}, u32[]{:S(2)}) collective-permute-start(bf16[320,1024]{1,0:T(8,128)(2,1)} %get-tuple-element.62), channel_id=1, source_target_pairs={{0,5},{1,4},{2,7},{3,6},{4,1},{5,0},{6,3},{7,2},{8,13},{9,12},{10,... | collective-permute-start | bytes 1966088 | tf_op jit(solution)/shard_map/ppermute | solution.py:979
  446.4 32.3 %copy-start.2 = (f32[320,1024]{1,0:T(8,128)S(1)}, f32[320,1024]{1,0:T(8,128)}, u32[]{:S(2)}) copy-start(f32[320,1024]{1,0:T(8,128)} %get-tuple-element.58) | copy-start | bytes 3932164
  446.4 32.3 %copy-start.5 = (bf16[320,1024]{1,0:T(8,128)(2,1)S(1)}, bf16[320,1024]{1,0:T(8,128)(2,1)}, u32[]{:S(2)}) copy-start(bf16[320,1024]{1,0:T(8,128)(2,1)} %get-tuple-element.59) | copy-start | bytes 1966084
  478.7 2.6 copy-start.1

commit v4 on v3

--- a/solution.py
+++ b/solution.py
@@ -22,6 +22,7 @@
 BF = jnp.bfloat16
 F32 = jnp.float32
 VMEM_LIMIT = 60 * 1024 * 1024
+OUT_STEP = 6
 
 NT_DIMS = (((1,), (1,)), ((), ()))
 TN_DIMS = (((0,), (0,)), ((), ()))
@@ -157,7 +158,7 @@
     gain = small_all[16:17, :].astype(F32)
 
     def kv_copy(t):
-        at = pl.ds(t * rows, rows)
+        at = pl.ds(pl.multiple_of(t * rows, rows), rows)
         return remote(kv.at[0, at], kv.at[1, at], s_kv, t, peer_y)
 
     ends = [pltpu.make_async_copy(wc, wc_out, s_end.at[0])]
@@ -173,17 +174,24 @@
         ends.append(pltpu.make_async_copy(src, dst, s_end.at[1 + i]))
         ends[-1].start()
 
-    for t in range(4):
-        if t == 1:
-            near.wait_recv()
-        if t == 2:
+    def end(t):
+        at = pl.ds(pl.multiple_of(t * rows, rows), rows)
+        return [
+            pltpu.make_async_copy(tok_all.at[t], tok_out.at[t], s_end.at[3 + t]),
+            pltpu.make_async_copy(h.at[at], h_out.at[at], s_end.at[7 + t]),
+        ]
+
+    @pl.loop(0, 4)
+    def _(t):
+        pl.when(t == 1)(near.wait_recv)
+
+        @pl.when(t == 2)
+        def _():
             over.wait_recv()
             onward.start()
-        if t == 3:
-            onward.wait_recv()
-        at = pl.ds(t * rows, rows)
-        ends.append(pltpu.make_async_copy(tok_all.at[t], tok_out.at[t], s_end.at[3 + t]))
-        ends[-1].start()
+
+        pl.when(t == 3)(onward.wait_recv)
+        at = pl.ds(pl.multiple_of(t * rows, rows), rows)
         normed, _ = rms_parts(tok_all[t].astype(F32))
         hidden = (normed * gain).astype(BF)
         h[at, :] = hidden
@@ -194,8 +202,11 @@
         kv_copy(t).start()
         for k in range(2):
             q[at, k * 128 : (k + 1) * 128] = rope_rows(proj[:, k * 128 : (k + 1) * 128], c, n).astype(BF)
-        ends.append(pltpu.make_async_copy(h.at[at], h_out.at[at], s_end.at[7 + t]))
-        ends[-1].start()
+        for copy in end(t):
+            copy.start()
+
+    for t in range(4):
+        ends.extend(end(t))
     for t in range(4):
         kv_copy(t).wait()
     for copy in ends:
@@ -259,7 +270,7 @@
 
 def widen(arrays, tiny, n_experts):
     flat = [a.reshape(-1, a.shape[-1]) for a in arrays]
-    steps = 16
+    steps = 8
     wide = tiny.shape[1]
     specs = [pl.BlockSpec((a.shape[0] // steps, a.shape[1]), lambda i: (i, 0)) for a in flat]
     shape = jax.ShapeDtypeStruct
@@ -414,10 +425,63 @@
     lse_ref[0] = jnp.transpose(lse)[:8]
 
 
+def attend_short_kernel(
+    qtab_ref, ktab_ref, len_ref, q_ref, kv_ref, o_ref, low_ref, lse_ref, ks, vs, *, span, kb
+):
+    step = pl.program_id(0)
+    count = ks.shape[0] // span
+
+    @pl.when(step == 0)
+    def _():
+        sort_spans(ktab_ref, kv_ref, ks, slice(0, 128), span, count)
+        sort_spans(ktab_ref, kv_ref, vs, slice(128, 256), span, count)
+
+    q = stack_heads(q_ref[:, :128], q_ref[:, 128:])
+    rows = 2 * span
+    limit = len_ref[0]
+    span_id = qtab_ref[step]
+    _, blocks = block_counts(span_id, limit, span, kb)
+    qpos = span_id * span + lax.broadcasted_iota(jnp.int32, (rows, kb), 0) % span
+    last = jnp.minimum(qpos, limit - 1)
+    col = lax.broadcasted_iota(jnp.int32, (rows, kb), 1)
+
+    def run(n):
+        outs, sums = [], []
+        for g in range(2):
+            part = q[g * rows : (g + 1) * rows]
+            scores = []
+            for i in range(n):
+                v = mm_nt(part, ks[i * kb : (i + 1) * kb, :]) * (HEAD_WIDTH**-0.5 * LOG2E)
+                if i == n - 1:
+                    v = jnp.where(col + i * kb <= last, v, NEG)
+                scores.append(v)
+            tops = [jnp.max(v, axis=1, keepdims=True) for v in scores]
+            top = functools.reduce(jnp.maximum, tops)
+            total = jnp.zeros((rows, 1), F32)
+            acc = jnp.zeros((rows, 128), F32)
+            for i in range(n):
+                p = jnp.exp2(scores[i] - top)
+                total = total + jnp.sum(p, axis=1, keepdims=True)
+                acc = acc + mm(p.astype(BF), vs[i * kb : (i + 1) * kb, :])
+            outs.append(acc / total)
+            sums.append(top + jnp.log2(total))
+        a, b = unstack_heads(jnp.concatenate(outs, axis=0))
+        o_ref[:, :128] = a
+        o_ref[:, 128:] = b
+        low_ref[:, :128] = a.astype(BF)
+        low_ref[:, 128:] = b.astype(BF)
+        lse = jnp.broadcast_to(jnp.concatenate(sums, axis=0), (2 * rows, 128))
+        lse_ref[0] = jnp.transpose(lse)[:8]
+
+    for n in range(1, ks.shape[0] // kb + 1):
+        pl.when(blocks == n)(functools.partial(run, n))
+
+
 def attend(qtab, ktab, limit, q, kv, span, kb):
     steps, keys = q.shape[0] // span, kv.shape[0]
+    body = attend_short_kernel if keys <= 4 * kb else attend_kernel
     return pl.pallas_call(
-        functools.partial(attend_kernel, span=span, kb=kb),
+        functools.partial(body, span=span, kb=kb),
         grid_spec=pltpu.PrefetchScalarGridSpec(
             num_scalar_prefetch=3,
             grid=(steps,),
@@ -656,13 +720,23 @@
         load_weights(e, lambda copy: copy.start())
 
     pl.semaphore_wait(barrier, 4)
-    heads = [remote(att.at[m], att_in.at[m], r.s_att, m, peers[m]) for m in range(1, 4)]
+    def head(m, i):
+        at = pl.ds(pl.multiple_of(i * n, n), n)
+        return remote(att.at[m, at], att_in.at[m, at], r.s_att, 2 * m + i, peers[m])
+
+    heads = [head(m, i) for i in range(2) for m in (3, 2, 1)]
     for copy in heads:
         copy.start()
     diag = [
         remote(r.cot_x.at[pl.ds(0, n)], cots.at[pl.ds(3 * rows, n)], r.s_diag, 0, peer_y),
         remote(r.cot_y.at[pl.ds(n, n)], cots.at[pl.ds(3 * rows + n, n)], r.s_diag, 1, peer_x),
     ]
+    wo_rows = pl.ds(pl.multiple_of(core * (ff // 2), ff // 2), ff // 2)
+    wo_there = r.wo_there
+    wo_copy = pltpu.make_async_copy(r.wo_near, wo_there.at[wo_rows], r.s_wo.at[0])
+    wo_share = remote(r.wo_near, wo_there.at[wo_rows], r.s_diag, 2, peers[1])
+    wo_copy.start()
+    wo_share.start()
     for copy in diag:
         copy.start()
 
@@ -678,18 +752,25 @@
     def head_cols(m):
         return pl.ds(pl.multiple_of(seqs[m] * 256, 256), 256)
 
-    tout[:, head_cols(0)] = att[0]
-    for m in range(1, 4):
-        heads[m - 1].wait_recv()
-        tout[:, head_cols(m)] = att_in[m]
-
-    shares = []
-    for i in range(2):
-        at = pl.ds(i * n, n)
+    wo_copy.wait()
+    wo_share.wait_recv()
+    def share(i, j, dev):
+        at = pl.multiple_of(i * n, n)
+        return remote(
+            hx.at[pl.ds(at, n)], hx.at[pl.ds((j + 1) * rows + at, n)], r.s_h, 2 * j + i, dev
+        )
+
+    @pl.loop(0, 2)
+    def _(i):
+        at = pl.ds(pl.multiple_of(i * n, n), n)
+        tout[at, head_cols(0)] = att[0, at, :]
+        for m in range(1, 4):
+            head(m, i).wait_recv()
+            tout[at, head_cols(m)] = att_in[m, at, :]
         middle = (
             r.tok[at, :].astype(F32)
             + mm(tout[at, own_cols], r.wo_own[...])
-            + mm(tout[at, away_cols], r.wo_there[...])
+            + mm(tout[at, away_cols], wo_there[...])
         )
         r.middle[at, :] = middle
         normed, _ = rms_parts(middle)
@@ -705,32 +786,45 @@
         r.gates[at, :] = gates
         hx[at, :width] = hidden
         hx[at, width:] = gates.astype(BF)
-        for j, dev in ((0, peer_y), (1, peer_x)):
-            to = pl.ds((j + 1) * rows + i * n, n)
-            copy = remote(hx.at[at], hx.at[to], r.s_h, 2 * j + i, dev)
-            copy.start()
-            shares.append(copy)
+        share(i, 0, peer_y).start()
+        share(i, 1, peer_x).start()
+
+    shares = [share(i, j, dev) for i in range(2) for j, dev in ((0, peer_y), (1, peer_x))]
     second = remote(
         hx.at[pl.ds(rows + n, n)], hx.at[pl.ds(3 * rows + n, n)], r.s_h, 4, peer_x
     )
     first = remote(hx.at[pl.ds(2 * rows, n)], hx.at[pl.ds(3 * rows, n)], r.s_h, 5, peer_y)
 
     dhs, moe, dh, dgates = r.dhs, r.moe_acc, r.dh_acc, r.dg_acc
-    back_y = remote(dhs.at[block(1)], r.rdh.at[0], r.s_d, 0, peer_y)
-    back_x = remote(dhs.at[block(2)], r.rdh.at[1], r.s_d, 1, peer_x)
-    hop_x = remote(dhs.at[pl.ds(3 * rows, n)], r.via.at[0], r.s_d, 2, peer_x)
-    hop_y = remote(dhs.at[pl.ds(3 * rows + n, n)], r.via.at[1], r.s_d, 3, peer_y)
-    end_y = remote(r.via.at[0], r.rdd.at[pl.ds(0, n)], r.s_d, 4, peer_y)
-    end_x = remote(r.via.at[1], r.rdd.at[pl.ds(n, n)], r.s_d, 5, peer_x)
+    few = 3 * rows // 4
+    half_rows = [(0, n), (n, n)]
+    back_y = [
+        remote(dhs.at[pl.ds(rows + a, k)], r.rdh.at[0, pl.ds(a, k)], r.s_d, i, peer_y)
+        for i, (a, k) in enumerate(half_rows)
+    ]
+    back_x = remote(dhs.at[block(2)], r.rdh.at[1], r.s_d, 2, peer_x)
+
+    def two_hops(a, k, sem, first_dev, second_dev):
+        via = r.via.at[pl.ds(a, k)]
+        return (
+            remote(dhs.at[pl.ds(3 * rows + a, k)], via, r.s_d, sem, first_dev),
+            remote(via, r.rdd.at[pl.ds(a, k)], r.s_d, sem + 1, second_dev),
+        )
+
+    hop_y0, end_x0 = two_hops(0, n, 3, peer_y, peer_x)
+    hop_y1, end_x1 = two_hops(n, few - n, 5, peer_y, peer_x)
+    hop_x, end_y = two_hops(few, rows - few, 7, peer_x, peer_y)
+    moe_x = remote(r.moe2, r.got2, r.s_d, 9, peer_x)
 
     moes = (r.moe0, r.moe1, r.moe2, r.moe3)
 
     def moe_out(t):
-        return pltpu.make_async_copy(r.mstage.at[t % 2], moes[t], r.s_m.at[t])
+        return pltpu.make_async_copy(r.mstage.at[(0, 1, 1, 0)[t]], moes[t], r.s_m.at[t])
 
     @pl.loop(0, 4 * count)
     def _(k):
-        t, e = k // count, k % count
+        turn, e = k // count, k % count
+        t = 2 * turn - turn // 2 - 4 * (turn // 3)
 
         @pl.when(k < count)
         def _():
@@ -749,7 +843,7 @@
             load_cots[1].wait()
             load_cots[2].wait()
 
-        @pl.when(k == 3 * count)
+        @pl.when(k == 2 * count)
         def _():
             first.wait_recv()
             second.wait_recv()
@@ -789,12 +883,12 @@
 
         @pl.when(e == count - 1)
         def _():
-            for k in range(4):
+            for i, k in enumerate((0, 2, 3, 1)):
                 @pl.when(t == k)
                 def _():
-                    if k >= 2:
-                        moe_out(k - 2).wait()
-                    r.mstage[k % 2] = moe[...].astype(BF)
+                    if i >= 2:
+                        moe_out((0, 2)[i - 2]).wait()
+                    r.mstage[i % 2] = moe[...].astype(BF)
                     moe_out(k).start()
 
             dhs[at, :width] = dh[...].astype(BF)
@@ -802,7 +896,8 @@
 
             @pl.when(t == 1)
             def _():
-                back_y.start()
+                for copy in back_y:
+                    copy.start()
 
             @pl.when(t == 2)
             def _():
@@ -810,8 +905,9 @@
 
             @pl.when(t == 3)
             def _():
+                hop_y0.start()
                 hop_x.start()
-                hop_y.start()
+                hop_y1.start()
 
     stage = r.stage
 
@@ -819,58 +915,81 @@
         return pltpu.make_async_copy(stage.at[slot], r.grads.at[b], r.s_g.at[slot])
 
     dattn, dto, dsend = r.dattn, r.dto, r.dsend
-    returns = [remote(dsend.at[m], r.do.at[m], r.s_back, m, peers[m]) for m in range(1, 4)]
-
-    def middle_back():
-        for copy in (back_y, back_x, end_y, end_x):
-            copy.wait_recv()
-        gn = jnp.zeros((1, width), F32)
-        rg = jnp.zeros((table.shape[0], width), F32)
-        for i in range(2):
-            at = pl.ds(i * n, n)
-            total = (
-                dhs[at, :].astype(F32) + r.rdh[0, at, :].astype(F32)
-                + r.rdh[1, at, :].astype(F32) + r.rdd[at, :].astype(F32)
-            )
-            dg, gates = total[:, width:], r.gates[at, :]
-            dl = (gates * (dg - jnp.sum(gates * dg, axis=-1, keepdims=True))).astype(BF)
-            rg += mm_tn(dl, hx[at, :width])
-            d_hidden = total[:, :width] + mm(dl, table[...])
-            normed, factor = rms_parts(r.middle[at, :])
-            gn += jnp.sum(d_hidden * normed, axis=0, keepdims=True)
-            d_n = d_hidden * gain
-            d_mid = cots[at, :].astype(F32) + factor * (
-                d_n - normed * jnp.mean(d_n * normed, axis=-1, keepdims=True)
-            )
-            r.dmid[at, :] = d_mid
-            low = d_mid.astype(BF)
-            dattn[at, :] = low
-            dto[at, own_cols] = mm_nt(low, r.wo_own[...]).astype(BF)
-            dto[at, away_cols] = mm_nt(low, r.wo_there[...]).astype(BF)
+    returns = [
+        [
+            remote(dsend.at[m, pl.ds(i * n, n)], r.do.at[m, pl.ds(i * n, n)], r.s_back, 2 * m + i, peers[m])
+            for m in (3, 2, 1)
+        ]
+        for i in range(2)
+    ]
+
+    def middle_back(i):
+        at = pl.ds(i * n, n)
+        total = (
+            dhs[at, :].astype(F32) + r.rdh[0, at, :].astype(F32)
+            + r.rdh[1, at, :].astype(F32) + r.rdd[at, :].astype(F32)
+        )
+        dg, gates = total[:, width:], r.gates[at, :]
+        dl = (gates * (dg - jnp.sum(gates * dg, axis=-1, keepdims=True))).astype(BF)
+        rg = mm_tn(dl, hx[at, :width])[:32]
+        d_hidden = total[:, :width] + mm(dl, table[...])
+        normed, factor = rms_parts(r.middle[at, :])
+        gn = jnp.sum(d_hidden * normed, axis=0, keepdims=True)
+        d_n = d_hidden * gain
+        d_mid = cots[at, :].astype(F32) + factor * (
+            d_n - normed * jnp.mean(d_n * normed, axis=-1, keepdims=True)
+        )
+        r.dmid[at, :] = d_mid
+        low = d_mid.astype(BF)
+        dattn[at, :] = low
+        dto[at, own_cols] = mm_nt(low, r.wo_own[...]).astype(BF)
+        dto[at, away_cols] = mm_nt(low, wo_there[...]).astype(BF)
         for m in range(1, 4):
-            dsend[m] = dto[:, head_cols(m)]
-            returns[m - 1].start()
-        r.do[0] = dto[:, head_cols(0)]
-        top = rg[:32]
-        row = lax.broadcasted_iota(jnp.int32, top.shape, 0)
-        top = jnp.where(row == 17, gn, jnp.where(row < 16, top, 0.0))
+            dsend[m, at, :] = dto[at, head_cols(m)]
+        for copy in returns[i]:
+            copy.start()
+        r.do[0, at, :] = dto[at, head_cols(0)]
+        if i == 0:
+            r.rg[...] = rg
+            r.gn[:1, :] = gn
+            return
+        rg, gn = r.rg[...] + rg, r.gn[:1, :] + gn
+        row = lax.broadcasted_iota(jnp.int32, rg.shape, 0)
+        top = jnp.where(row == 17, gn, jnp.where(row < 16, rg, 0.0))
         r.tiny[0] = top[:, : width // 2]
         r.tiny[1] = top[:, width // 2 :]
-        for i in range(4):
-            at = slice(i * 256, (i + 1) * 256)
-            r.gout[at, :] = mm_tn(tout[:, at], dattn[...]).astype(BF)
-
-    def forward():
+        for k in range(4):
+            cols = slice(k * 256, (k + 1) * 256)
+            r.gout[cols, :] = mm_tn(tout[:, cols], dattn[...]).astype(BF)
+
+    def forward0():
+        hop_y0.wait_recv()
+        end_x0.start()
+
+    def forward1():
+        hop_y1.wait_recv()
+        end_x1.start()
         hop_x.wait_recv()
         end_y.start()
-        hop_y.wait_recv()
-        end_x.start()
+        moe_x.start()
+
+    def back0():
+        for copy in (back_y[0], back_x, end_x0):
+            copy.wait_recv()
+        middle_back(0)
+
+    def back1():
+        for copy in (back_y[1], end_x1, end_y):
+            copy.wait_recv()
+        middle_back(1)
 
     @pl.loop(0, 3 * count)
     def _(k):
         e, j = k // 3, k % 3
-        pl.when(k == 5)(forward)
-        pl.when(k == 3 * count - 2)(middle_back)
+        pl.when(k == 0)(forward0)
+        pl.when(k == 2)(forward1)
+        pl.when(k == 3 * count - 6)(back0)
+        pl.when(k == 3 * count - 1)(back1)
 
         @pl.when(k > 0)
         def _():
@@ -893,15 +1012,15 @@
 
     grad_copy(0, 0).wait()
     grad_copy(0, 1).wait()
-    moe_out(2).wait()
     moe_out(3).wait()
-    for copy in returns:
+    moe_out(1).wait()
+    for copy in (*returns[0], *returns[1], moe_x):
         copy.wait()
-    for copy in (*heads, *diag, *shares, first, second, back_y, back_x, hop_x, hop_y, end_y, end_x):
+    for copy in (*heads, *diag, wo_share, *shares, first, second, *back_y, back_x, hop_x, hop_y0, hop_y1, end_y, end_x0, end_x1):
         copy.wait_send()
 
 
-def moe_layer(att, tok, wo_own, wo_there, small, routes, cot, cot_y, cot_x, wg, wu, wd):
+def moe_layer(att, tok, wo_own, wo_near, small, routes, cot, cot_y, cot_x, wg, wu, wd):
     rows, width = tok.shape
     owned, _, ff = wg.shape
     count = owned // 2
@@ -911,7 +1030,7 @@
     dma = pltpu.SemaphoreType.DMA
     args = dict(
         att=(att.reshape(4, rows, 256), vmem), tok=(tok, vmem), wo_own=(wo_own, vmem),
-        wo_there=(wo_there, vmem), small=(small, vmem), routes=(routes, vmem),
+        wo_near=(wo_near, hbm), small=(small, vmem), routes=(routes, vmem),
         cot=(cot, hbm), cot_y=(cot_y, hbm), cot_x=(cot_x, hbm),
         wg=(wg, hbm), wu=(wu, hbm), wd=(wd, hbm),
     )
@@ -920,6 +1039,7 @@
         middle=(shape((rows, width), F32), vmem),
         moe0=(shape((rows, width), BF), hbm), moe1=(shape((rows, width), BF), hbm),
         moe2=(shape((rows, width), BF), hbm), moe3=(shape((rows, width), BF), hbm),
+        got2=(shape((rows, width), BF), hbm),
         dmid=(shape((rows, width), F32), vmem),
         do=(shape((4, rows, 256), BF), vmem),
         grads=(shape((6 * count, ff, ff), BF), hbm),
@@ -930,18 +1050,19 @@
     scratch = dict(
         att_in=pltpu.VMEM((4, rows, 256), BF), tout=pltpu.VMEM((rows, width), BF),
         hx=pltpu.VMEM((4 * rows, ext), BF), cots=pltpu.VMEM((4 * rows, width), BF),
-        table=pltpu.VMEM((128, width), BF), gates=pltpu.VMEM((rows, 128), F32),
+        wo_there=pltpu.VMEM((ff, width), BF), rg=pltpu.VMEM((32, width), F32),
+        gn=pltpu.VMEM((8, width), F32), table=pltpu.VMEM((128, width), BF), gates=pltpu.VMEM((rows, 128), F32),
         wgs=pltpu.VMEM((count, width, ff), BF), wus=pltpu.VMEM((count, width, ff), BF),
         wds=pltpu.VMEM((count, ff, width), BF),
         s_act=stash, s_gate=stash, s_up=stash,
         moe_acc=pltpu.VMEM((rows, width), F32), dh_acc=pltpu.VMEM((rows, width), F32),
         dg_acc=pltpu.VMEM((rows, 128), F32), mstage=pltpu.VMEM((2, rows, width), BF),
         dhs=pltpu.VMEM((4 * rows, ext), BF), rdh=pltpu.VMEM((2, rows, ext), BF),
-        via=pltpu.VMEM((2, rows // 2, ext), BF), rdd=pltpu.VMEM((rows, ext), BF),
+        via=pltpu.VMEM((rows, ext), BF), rdd=pltpu.VMEM((rows, ext), BF),
         dattn=pltpu.VMEM((rows, width), BF), dto=pltpu.VMEM((rows, width), BF),
         dsend=pltpu.VMEM((4, rows, 256), BF), stage=pltpu.VMEM((2, ff, ff), BF),
-        s_att=dma((2, 4)), s_diag=dma((2, 2)), s_h=dma((2, 6)), s_d=dma((2, 6)), s_back=dma((2, 4)),
-        s_cot=dma((3,)), s_w=dma((3, count)), s_m=dma((4,)), s_g=dma((2,)),
+        s_att=dma((2, 8)), s_diag=dma((2, 3)), s_h=dma((2, 6)), s_d=dma((2, 10)), s_back=dma((2, 8)),
+        s_cot=dma((3,)), s_wo=dma((1,)), s_w=dma((3, count)), s_m=dma((4,)), s_g=dma((2,)),
     )
     names = tuple(args) + tuple(outs) + tuple(scratch)
     got = pl.pallas_call(
@@ -972,11 +1093,6 @@
 
 def flip_y(x):
     return lax.ppermute(x, "fsdp", [(0, 1), (1, 0)])
-
-
-def flip_xy(x):
-    perm = [(2 * q + f, 2 * ((q + 2) % 4) + 1 - f) for q in range(4) for f in range(2)]
-    return lax.ppermute(x, ("seq", "fsdp"), perm)
 
 
 def gather_seq(x):
@@ -1030,7 +1146,8 @@
         return ((z + k) % slots, s, f)
 
     barrier = pltpu.get_barrier_semaphore()
-    peers = [other_z(k) for k in range(1, slots)] + [peer_core, peer_x] + [peer_y] * fused
+    peer_xy = (z, (s + 2) % 4, 1 - f)
+    peers = [other_z(k) for k in range(1, slots)] + [peer_core, peer_x] + [peer_y, peer_xy] * fused
     for dev in peers:
         pl.semaphore_signal(barrier, inc=1, device_id=dev, device_id_type=MESH)
 
@@ -1051,9 +1168,11 @@
         loads = [
             pltpu.make_async_copy(a, b, r.s_in.at[i])
             for i, (a, b) in enumerate((
-                (r.dkv.at[pl.ds(0, r.dkvs.shape[0])], r.dkvs), (r.dq, r.dq_in), (r.wc, r.wc_in),
+                (r.q, r.q_in), (r.kv, r.kv_in), (r.do, r.do_in), (r.o, r.o_in), (r.lse, r.lse_in),
+                (r.wc, r.wc_in),
                 (r.cos, r.cos_in), (r.sin, r.sin_in), (r.h, r.h_in), (r.tok, r.tok_in),
-                (r.gout, r.gout_in), (r.dmid, r.dmid_in),
+                (r.gout.at[pl.ds(pl.multiple_of(f * block, block), block)], r.gout_in),
+                (r.dmid, r.dmid_in),
             ))
         ]
         for copy in loads:
@@ -1117,7 +1236,7 @@
         place(b, x, core, act)
 
     lag = 2
-    ahead = 16
+    ahead = 4
 
     def begin(b):
         @pl.when(b < (n_moe if fused else items))
@@ -1223,19 +1342,22 @@
     steps = {}
     if fused:
         s_fg = r.s_fg
-        dh, osum = r.dh, r.osum
         keys = r.dkvs.shape[0]
-        tile = dh.shape[1]
+        tile = r.dhx.shape[0]
+        dh = [r.h_in.at[pl.ds(t * tile, tile)] for t in range(4)]
         owner = pl.multiple_of(f * block, block)
         away = pl.multiple_of((1 - f) * block, block)
         mine_rows, away_rows = pl.ds(owner, block), pl.ds(away, block)
         near_cols = pl.ds(pl.multiple_of(x * block, block), block)
         far_cols = pl.ds(pl.multiple_of((1 - x) * block, block), block)
 
-        send_dkv = remote(r.dkv.at[pl.ds(keys, keys)], r.rdkv, s_fg, 0, peer_y)
-        send_out = remote(r.gout.at[away_rows], r.rout, s_fg, 1, peer_y)
-        send_dh3 = remote(dh.at[3], r.rdh.at[1], s_fg, 2, peer_core)
-        send_dh1 = remote(dh.at[1], r.rdh.at[0], s_fg, 3, peer_core)
+        send_dkv = remote(r.kv_in.at[pl.ds(keys, keys)], r.rdkv, s_fg, 0, peer_y)
+        send_out = [
+            remote(r.gout.at[away_rows, cols], r.rout.at[i], s_fg, (1, 8)[i], peer_y)
+            for i, cols in enumerate((far_cols, near_cols))
+        ]
+        send_dh3 = remote(dh[3], r.rdh.at[1], s_fg, 2, peer_core)
+        send_dh1 = remote(dh[1], r.rdh.at[0], s_fg, 3, peer_core)
         send_dhx = remote(r.dhx, r.rdx, s_fg, 4, peer_x)
         send_cols = remote(r.cbuf.at[away_rows], r.rcol, s_fg, 5, peer_y)
         send_outx = remote(r.osend, r.rox, s_fg, 6, peer_x)
@@ -1244,14 +1366,75 @@
             remote(r.eo.at[1 - core, i], rc.at[n_moe + i], r.s_rc, n_moe + i, peer_core)
             for i in range(2)
         ]
-        send_dkv.start()
-        send_out.start()
+        moe_back = [
+            remote(r.moe3, r.got3, r.s_moe, 1, peer_xy), remote(r.moe1, r.got1, r.s_moe, 0, peer_y),
+        ]
+        moe_back[0].start()
+        for copy in send_out:
+            copy.start()
+        moe_back[1].start()
+
+        span, kb = tile // 2, 2 * tile
+        parts = 2 * keys // kb
+        n_steps = 8 * parts
+        scale = HEAD_WIDTH**-0.5
+
+        def attention(n):
+            j, m = n // parts, n % parts
+            at = pl.ds(pl.multiple_of(j * span, span), span)
+
+            @pl.when(n == 0)
+            def _():
+                r.dk[...] = jnp.zeros_like(r.dk)
+                r.dv[...] = jnp.zeros_like(r.dv)
+                inside = lax.broadcasted_iota(jnp.int32, (span, 1), 0)
+                for k in range(2 * keys // span):
+                    r.kpos[k * span : (k + 1) * span, :] = r.ktab[k] * span + inside
+                across = lax.broadcasted_iota(jnp.int32, (8, 4 * span), 1) % span
+                for k in range(8):
+                    r.last[k] = jnp.minimum(r.qtab[k] * span + across, r.limit[0] - 1)
+
+            @pl.when(m == 0)
+            def _():
+                r.qs[...] = stack_heads(r.q_in[at, :128], r.q_in[at, 128:])
+                do = stack_heads(r.do_in[at, :128], r.do_in[at, 128:])
+                r.dos[...] = do
+                inner = do.astype(F32) * stack_heads(r.o_in[at, :128], r.o_in[at, 128:], F32)
+                delta = jnp.sum(jnp.transpose(inner), axis=0, keepdims=True)
+                r.delta[...] = jnp.broadcast_to(delta, r.delta.shape)
+
+            key = pl.ds(pl.multiple_of(m * kb, kb), kb)
+            k, v = r.kv_in[key, :128], r.kv_in[key, 128:]
+            q, do = r.qs[...], r.dos[...]
+            p = jnp.exp2(mm_nt(k, q) * (scale * LOG2E) - r.lse_in[j, :1])
+            p = jnp.where(r.kpos[key, :] <= r.last[j, :1], p, 0.0)
+            ds = (p * (mm_nt(v, do) - r.delta[:1])).astype(BF)
+            r.dk[key, :] += mm(ds, q)
+            r.dv[key, :] += mm(p.astype(BF), do)
+            dq = mm_tn(ds, k)
+
+            @pl.when(m == 0)
+            def _():
+                r.dqa[...] = dq
+
+            @pl.when(m > 0)
+            def _():
+                r.dqa[...] += dq
+
+            @pl.when(m == parts - 1)
+            def _():
+                a, b = unstack_heads(r.dqa[...] * scale)
+                r.dq_in[at, :128] = a.astype(BF)
+                r.dq_in[at, 128:] = b.astype(BF)
+
+        def send_keys():
+            r.kv_in[:, :128] = (r.dk[...] * scale).astype(BF)
+            r.kv_in[:, 128:] = r.dv[...].astype(BF)
+            send_dkv.start()
 
         def sum_dkv():
-            for copy in loads:
-                copy.wait()
             send_dkv.wait_recv()
-            r.dkvs[...] = add(r.dkvs[...], r.rdkv[...]).astype(BF)
+            r.dkvs[...] = add(r.kv_in[:keys], r.rdkv[...]).astype(BF)
 
         def back_tile(t, first=False):
             at = pl.ds(t * tile, tile)
@@ -1265,7 +1448,7 @@
             dproj = jnp.concatenate(parts, axis=1)
             grad = mm_tn(r.h_in[at, :], dproj)
             back = mm_nt(dproj, r.wc_in[...])
-            dh[t] = back.astype(BF)
+            dh[t][...] = back.astype(BF)
             normed, _ = rms_parts(r.tok_in[at, :].astype(F32))
             gain = jnp.sum((back * normed).reshape(-1, 8, back.shape[1]), axis=0)
             if first:
@@ -1286,7 +1469,7 @@
         def tile2():
             back_tile(2)
             send_dh3.wait_recv()
-            r.dhx[...] = add(dh[2], r.rdh[1]).astype(BF)
+            r.dhx[...] = add(dh[2][...], r.rdh[1]).astype(BF)
             send_dhx.start()
 
         def tile0():
@@ -1302,9 +1485,8 @@
             send_tiny.start()
 
         def sum_out():
-            send_out.wait_recv()
-            osum[...] = add(r.gout_in[mine_rows, :], r.rout[...]).astype(BF)
-            r.osend[...] = osum[:, far_cols]
+            send_out[0].wait_recv()
+            r.osend[...] = add(r.gout_in[:, far_cols], r.rout[0]).astype(BF)
             send_outx.start()
 
         def tiny_y():
@@ -1319,8 +1501,10 @@
                 mine[n_out + i] = v[i * piece : (i + 1) * piece]
 
         def sum_outx():
+            send_out[1].wait_recv()
             send_outx.wait_recv()
-            v = add(osum[:, near_cols], r.rox[...]).astype(BF)
+            v = add(r.gout_in[:, near_cols], r.rout[1]) + r.rox[...].astype(F32)
+            v = v.astype(BF)
             for i in range(4):
                 r.eo[i // 2, i % 2] = v[i * piece : (i + 1) * piece]
             for i in range(2):
@@ -1330,18 +1514,25 @@
         def inputs_back():
             send_dh1.wait_recv()
             send_dhx.wait_recv()
-            up_grad = add(dh[0], r.rdh[0]) + r.rdx[...].astype(F32)
+            up_grad = add(dh[0][...], r.rdh[0]) + r.rdx[...].astype(F32)
             normed, factor = rms_parts(r.tok_in[:tile].astype(F32))
             d_n = up_grad * r.small[16:17, :].astype(F32)
             r.dtok[...] = r.dmid_in[...] + factor * (
                 d_n - normed * jnp.mean(d_n * normed, axis=-1, keepdims=True)
             )
 
+        def arrive():
+            for copy in loads:
+                copy.wait()
+
+        first_step = 1
+        done = first_step + n_steps
         order = [
-            None, sum_dkv, tile3, tile1, tile2, tile0, sum_out, tiny_y, sum_cols, tiny_core,
-            sum_outx, inputs_back, tiny_spread,
+            send_keys, None, None, sum_outx, None, sum_dkv, tile3, tile1, tile2, tile0, None, None,
+            tiny_y, sum_cols, None, inputs_back, tiny_core, None, tiny_spread,
         ]
-        steps = {2 * i + ahead - 2: fn for i, fn in enumerate(order) if fn is not None}
+        steps = {done + i: fn for i, fn in enumerate(order) if fn is not None}
+        steps.update({0: arrive, OUT_STEP: sum_out})
     else:
         tsum[0] = r.tiny[...].astype(BF)
         tiny_x()
@@ -1359,6 +1550,11 @@
             def _():
                 fn(b)
 
+        if fused:
+            @pl.when((i >= first_step) & (i < done))
+            def _():
+                attention(i - first_step)
+
         for k, fn in steps.items():
             pl.when(i == k)(fn)
 
@@ -1390,11 +1586,13 @@
     for k in range(1, slots):
         remote(tsum.at[2], trecv.at[1 + k], s_tiny, 1 + k, other_z(k)).wait_send()
     if fused:
-        for copy in (send_dkv, send_out, send_dh3, send_dh1, send_dhx, send_cols, send_outx, send_tiny):
+        for copy in (send_dkv, *send_out, send_dh3, send_dh1, send_dhx, send_cols, send_outx, send_tiny):
             copy.wait_send()
-
-
-def reduce_grads(gm, tiny, slots, shards, eo=None, cols=None, fused=None):
+        for copy in moe_back:
+            copy.wait()
+
+
+def reduce_grads(gm, tiny, slots, shards, eo=None, cols=None, fused=None, small=None, tables=None, moes=None):
     count, _, ff, _ = gm.shape
     width = 2 * ff
     nb = 6 * count
@@ -1430,25 +1628,36 @@
         inner = {}
         for k, v in fused.items():
             args[k] = (v, hbm)
-            inner[k] = pltpu.VMEM(v.shape, v.dtype)
-        args.update(small=(fused.pop("small"), vmem))
+            inner[k + "_in"] = pltpu.VMEM(v.shape, v.dtype)
+        smem = pl.BlockSpec(memory_space=pltpu.SMEM)
+        qtab, ktab, limit = tables
+        args.update(
+            small=(small, vmem), qtab=(qtab, smem), ktab=(ktab, smem), limit=(limit, smem),
+            moe1=(moes[0], hbm), moe3=(moes[1], hbm),
+        )
+        outs.update({k: (jax.ShapeDtypeStruct(moes[0].shape, BF), hbm) for k in ("got1", "got3")})
         rows = args["dmid"][0].shape[0]
-        keys = args["dkv"][0].shape[0] // 2
+        keys = args["kv"][0].shape[0] // 2
+        inner.update(gout_in=pltpu.VMEM((ff, width), BF))
+        scratch.update(inner)
         outs.update(dtok=(jax.ShapeDtypeStruct((rows, width), F32), vmem))
         scratch.update(
             rdkv=pltpu.VMEM((keys, 256), BF), dkvs=pltpu.VMEM((keys, 256), BF),
-            rout=pltpu.VMEM((ff, width), BF), osum=pltpu.VMEM((ff, width), BF),
+            rout=pltpu.VMEM((2, ff, ff), BF),
             osend=pltpu.VMEM((ff, ff), BF), rox=pltpu.VMEM((ff, ff), BF),
             eo=pltpu.VMEM((2, 2, piece, ff), BF),
-            dq_in=inner["dq"], wc_in=inner["wc"], cos_in=inner["cos"], sin_in=inner["sin"],
-            h_in=inner["h"], tok_in=inner["tok"], gout_in=inner["gout"], dmid_in=inner["dmid"],
-            s_in=dma((9,)),
-            dh=pltpu.VMEM((4, rows, width), BF), rdh=pltpu.VMEM((2, rows, width), BF),
+            dq_in=pltpu.VMEM((keys, 256), BF),
+            dk=pltpu.VMEM((2 * keys, 128), F32), dv=pltpu.VMEM((2 * keys, 128), F32),
+            qs=pltpu.VMEM((2 * rows, 128), BF), dos=pltpu.VMEM((2 * rows, 128), BF),
+            delta=pltpu.VMEM((8, 2 * rows), F32), dqa=pltpu.VMEM((2 * rows, 128), F32),
+            kpos=pltpu.VMEM((2 * keys, 1), jnp.int32), last=pltpu.VMEM((8, 8, 2 * rows), jnp.int32),
+            s_in=dma((len(fused),)), s_moe=dma((2, 2)),
+            rdh=pltpu.VMEM((2, rows, width), BF),
             dhx=pltpu.VMEM((rows, width), BF), rdx=pltpu.VMEM((rows, width), BF),
             acc=pltpu.VMEM((width, ff), F32), gn=pltpu.VMEM((8, width), F32),
             cbuf=pltpu.VMEM((width, ff), BF), rcol=pltpu.VMEM((ff, ff), BF),
             tbuf=pltpu.VMEM(tiny.shape, BF), rtiny=pltpu.VMEM(tiny.shape[-2:], BF),
-            s_fg=dma((2, 8)),
+            s_fg=dma((2, 9)),
         )
     names = tuple(args) + tuple(outs) + tuple(scratch)
     got = pl.pallas_call(
@@ -1459,7 +1668,9 @@
         out_specs=[v[1] for v in outs.values()],
         out_shape=[v[0] for v in outs.values()],
         scratch_shapes=list(scratch.values()),
-        compiler_params=params(collective_id=1, has_side_effects=True),
+        compiler_params=pltpu.CompilerParams(
+            vmem_limit_bytes=67043328, collective_id=1, has_side_effects=True
+        ),
         name="reduce_grads",
     )(*[v[0] for v in args.values()])
     return types.SimpleNamespace(**dict(zip(outs, got)))
@@ -1530,14 +1741,16 @@
     own_valid = (qpos[:rows] < limit[0])[:, None]
     masked_cot = jnp.where(own_valid, cotangent[0], jnp.zeros_like(cotangent[0]))
     if shards == 2:
-        wo_there, cot_y, cot_x = flip_y(w_out), flip_y(masked_cot), flip_x(masked_cot)
+        shared = w_out.shape[0] // 2
+        wo_near = flip_y(lax.dynamic_slice_in_dim(w_out, core * shared, shared, 0))
+        cot_y, cot_x = flip_y(masked_cot), flip_x(masked_cot)
     attended, low, lse = attend(qtab, ktab, limit, q, kv, span, kb)
     inputs = x.astype(F32)
     if shards == 2:
         out = moe_layer(
-            low, x, w_out, wo_there, small, routes[0], masked_cot, cot_y, cot_x, w_gate, w_up, w_down
+            low, x, w_out, wo_near, small, routes[0], masked_cot, cot_y, cot_x, w_gate, w_up, w_down
         )
-        parts = [out.moe0, flip_y(out.moe1), flip_x(out.moe2), flip_xy(out.moe3)]
+        moes = (out.moe1, out.moe3)
         d_heads = out.do.reshape(groups * rows, qw)
         middle, d_middle, grad_out, tiny = out.middle, out.dmid, out.gout, out.tiny
         weight_grads = out.grads.reshape(count, 6, w_gate.shape[2], -1)
@@ -1605,8 +1818,6 @@
         d_heads = jnp.transpose(d_token_out.reshape(rows, groups, qw), (1, 0, 2))
         d_heads = jnp.take(d_heads, relative, axis=0)
         d_heads = jnp.concatenate(swap_seq([d_heads[m] for m in range(groups)]))
-    dq, dkv = attend_back(qtab, ktab, limit, q, kv, d_heads, attended, lse, span, kb)
-
     block = w_gate.shape[2]
     shard_rows = width // shards
 
@@ -1619,12 +1830,14 @@
         got = reduce_grads(
             weight_grads, tiny, slots, shards,
             fused=dict(
-                dkv=dkv, dq=dq, tok=tok, h=hidden_one, wc=wcols, cos=cos, sin=sin,
-                small=small, dmid=d_middle, gout=grad_out,
+                q=q, kv=kv, do=d_heads, o=attended, lse=lse,
+                tok=tok, h=hidden_one, wc=wcols, cos=cos, sin=sin, dmid=d_middle, gout=grad_out,
             ),
+            small=small, tables=(qtab, ktab, limit), moes=moes,
         )
         d_inputs = got.dtok
     else:
+        dq, dkv = attend_back(qtab, ktab, limit, q, kv, d_heads, attended, lse, span, kb)
         dh_one, grad_cols, grad_norm1 = project_back(
             tok, hidden_one, dq, scatter_fsdp(dkv), wcols, cos, sin, rows
         )
@@ -1654,6 +1867,7 @@
     )
     shard_out, shard_qkv = shard_out[:shard_rows], shard_qkv[:shard_rows]
     if shards == 2:
+        parts = (out.moe0, got.got1, out.got2, got.got3)
         layer_out = (middle + sum(p.astype(F32) for p in parts)).astype(BF)
     else:
         layer_out = (middle + give_back(moe_parts)).astype(BF)

time: 488 us -> 429 us (0.88); the launches traced: 482 us -> 429 us
  Pallas kernels: 457 us -> 406 us
  starting transfers between devices: 9.38 us -> 3.65 us
    pallas_call x2 -> x1, Pallas kernels: 67.3 us -> 18.1 us  [attend(): pl.pallas_call(functools.partial(body, span=span, kb=kb), grid_spec=pltpu...]
  transfers between devices with their start and end apart: 6 -> 3, of which waited for: 0 -> 1; matrix products, arithmetic and copies ran while one was open for 1% -> 1% of each run, Pallas kernels for 65% -> 4%
where the time goes in v4:
time: 429 us
  Pallas kernels  406 us (95%)
  local copies, waits for them, and re-layouts  9.63 us (2%)
  other arithmetic  4.54 us (1%)
    pallas_call x1, Pallas kernels, reduce_grads(): pl.pallas_call(functools.partial(reduce_kernel, names=names, slots=slots,...  219 us
    pallas_call x1, Pallas kernels, moe_layer(): pl.pallas_call(functools.partial(moe_kernel, names=names, topk=routes.sha...  105 us
    pallas_call x1, Pallas kernels, front(): pl.pallas_call(front_kernel, in_specs=[pl.BlockSpec(memory_space=pltpu.SM...  35.4 us
    pallas_call x1, Pallas kernels, widen(): pl.pallas_call(widen_kernel, grid=(steps,), in_specs=specs + [whole(tiny....  28.9 us
    pallas_call x1, Pallas kernels, attend(): pl.pallas_call(functools.partial(body, span=span, kb=kb), grid_spec=pltpu...  18.1 us
  transfers between devices with their start and end apart: 3, of which 1 were waited for; matrix products, arithmetic and copies ran while one was open for 1% of the time, Pallas kernels for 4%

profile of v4, /device:TPU:0, one launch (start us, length us, event | category | flops | bytes accessed | tf_op | source)
XLA Modules:
  0.0 429.0 jit_solution(11434108412577982844)
XLA Ops:
  1.4 0.7 broadcast_in_dim.52
  2.1 0.7 broadcast_in_dim.53
  2.8 0.7 reshape.198
  3.5 0.6 gather_fusion
  4.5 1.4 maximum_maximum_fusion.small
  5.9 35.4 %front.1 = (bf16[4,320,1024]{2,1,0:T(8,128)(2,1)}, bf16[1024,512]{1,0:T(8,128)(2,1)}, bf16[32,1024]{1,0:T(8,128)(2,1)}, bf16[1280,1024]{1,0:T(8,128)(2,1)}, bf16...) custom-call(s32[8]{0:T(128)} %copy-done.12, ...), custom_call_target="tpu_custom_call" | custom-call | tf_op jit(solution)/shard_map/front/pallas_call | solution.py:232
  41.3 0.1 bitcast_select_fusion.refs_6_
  41.5 1.6 collective-permute-start.2
  43.0 1.4 collective-permute-start.1
  44.5 0.7 collective-permute-start
  45.3 0.6 gather_fusion.1
  46.1 0.1 copy.33
  46.2 0.6 reshape.199.ktab_ref.refs_16_
  46.8 0.8 copy.34
  47.6 18.1 %attend.1 = (f32[1280,256]{1,0:T(8,128)}, bf16[1280,256]{1,0:T(8,128)(2,1)}, f32[8,8,640]{2,1,0:T(8,128)}) custom-call(s32[8]{0:T(128)} %copy-done.12, s32[16]{0:T(128)} %reshape.199.ktab_ref.refs_16_, s32[1]{0:T(128)} %copy.37.len_ref.refs_17_, bf16[1280,256]{1,0:T(8,128)(2,1)} %get-tuple-element.51.q_ref.refs_2_, bf16[2560,256]{1,0:T(8,128)(2,1)} %bitcast.36), custom_call_target="tpu_custom_call" | custom-call | tf_op jit(solution)/shard_map/attend/pallas_call | solution.py:483
  65.7 3.4 collective-permute-done.refs_3_
  69.1 0.9 copy-done.8
  70.0 0.8 copy-done.9
  70.8 105.3 %moe_layer.1 = (f32[320,1024]{1,0:T(8,128)}, bf16[320,1024]{1,0:T(8,128)(2,1)}, bf16[320,1024]{1,0:T(8,128)(2,1)}, bf16[320,1024]{1,0:T(8,128)(2,1)}, bf16[320,1...) custom-call(bf16[4,320,256]{2,1,0:T(8,128)(2,1)} %bitcast.43, ...), custom_call_target="tpu_custom_call" | custom-call | tf_op jit(solution)/shard_map/moe_layer/pallas_call | solution.py:1068
  176.1 218.6 %reduce_grads.1 = (bf16[8,1024,512]{2,1,0:T(8,128)(2,1)}, bf16[8,1024,512]{2,1,0:T(8,128)(2,1)}, bf16[8,512,1024]{2,1,0:T(8,128)(2,1)}, bf16[512,1024]{1,0:T(8,1...) custom-call(bf16[24,2,2,128,512]{4,3,2,1,0:T(8,128)(2,1)} %bitcast.3, ...), custom_call_target="tpu_custom_call" | custom-call | tf_op jit(solution)/shard_map/reduce_grads/pallas_call | solution.py:1663
  394.8 28.9 %widen.1 = (f32[8192,512]{1,0:T(8,128)}, f32[8192,512]{1,0:T(8,128)}, f32[4096,1024]{1,0:T(8,128)}, f32[512,1024]{1,0:T(8,128)}, f32[512,2048]{1,0:T(8,128)}, /*...) custom-call(bf16[8192,512]{1,0:T(8,128)(2,1)} %bitcast.33, bf16[8192,512]{1,0:T(8,128)(2,1)} %bitcast.34, ...), custom_call_target="tpu_custom_call" | custom-call | tf_op jit(solution)/shard_map/widen/pallas_call | solution.py:277
  423.7 1.7 copy.35
  425.4 2.6 fusion
  428.0 1.1 copy.38
  (43 shorter events, 0.9 us)
Async XLA Ops:
  0.6 40.7 %copy-start.7 = (bf16[1,320,1024]{2,1,0:T(8,128)(2,1)S(1)}, bf16[1,320,1024]{2,1,0:T(8,128)(2,1)}, u32[]{:S(2)}) copy-start(bf16[1,320,1024]{2,1,0:T(8,128)(2,1)} %param.16) | copy-start | bytes 1966084
  4.3 1.7 copy-start.12
  5.9 38.5 %copy-start.1 = (bf16[512,1024]{1,0:T(8,128)(2,1)S(1)}, bf16[512,1024]{1,0:T(8,128)(2,1)}, u32[]{:S(2)}) copy-start(bf16[512,1024]{1,0:T(8,128)(2,1)} %refs_2_) | copy-start | bytes 3145732
  5.9 40.8 %copy-start.11 = (s32[1,320,8]{1,2,0:T(8,128)S(1)}, s32[1,320,8]{1,2,0:T(8,128)}, u32[]{:S(2)}) copy-start(s32[1,320,8]{1,2,0:T(8,128)} %param.19) | copy-start | bytes 30724
  41.4 1.6 copy-start
  41.5 27.6 %collective-permute-start.2 = (bf16[320,1024]{1,0:T(8,128)(2,1)S(1)}, bf16[320,1024]{1,0:T(8,128)(2,1)S(1)}, u32[]{:S(2)}, u32[]{:S(2)}) collective-permute-start(bf16[320,1024]{1,0:T(8,128)(2,1)S(1)} %bitcast_select_fusion.refs_6_), channel_id=1, source_target_pairs={{0,4},{4,0},{2,6},{6,2},{1,5},{5,1},{3,7},{7,3},{8,12},{12,8},{10,... | collective-permute-start | bytes 1966088 | tf_op jit(solution)/shard_map/ppermute | solution.py:1087
  43.0 26.1 %collective-permute-start.1 = (bf16[320,1024]{1,0:T(8,128)(2,1)S(1)}, bf16[320,1024]{1,0:T(8,128)(2,1)S(1)}, u32[]{:S(2)}, u32[]{:S(2)}) collective-permute-start(bf16[320,1024]{1,0:T(8,128)(2,1)S(1)} %bitcast_select_fusion.refs_6_), channel_id=1, source_target_pairs={{0,1},{1,0},{2,3},{3,2},{4,5},{5,4},{6,7},{7,6},{8,9},{9,8},{10,11... | collective-permute-start | bytes 1966088 | tf_op jit(solution)/shard_map/ppermute | solution.py:1095
  44.5 24.6 %collective-permute-start = (bf16[256,1024]{1,0:T(8,128)(2,1)S(1)}, bf16[256,1024]{1,0:T(8,128)(2,1)S(1)}, u32[]{:S(2)}, u32[]{:S(2)}) collective-permute-start(bf16[256,1024]{1,0:T(8,128)(2,1)S(1)} %constant_dynamic-slice_fusion), channel_id=1, source_target_pairs={{0,1},{1,0},{2,3},{3,2},{4,5},{5,4},{6,7},{7,6},{8,9},{9,8},{10,11... | collective-permute-start | bytes 1572872 | tf_op jit(solution)/shard_map/ppermute | solution.py:1095
  69.1 1.7 copy-start.10
  69.1 0.9 copy-start.8
  70.0 0.8 copy-start.9
  394.8 30.6 %copy-start.3 = (f32[320,1024]{1,0:T(8,128)S(1)}, f32[320,1024]{1,0:T(8,128)}, u32[]{:S(2)}) copy-start(f32[320,1024]{1,0:T(8,128)} %get-tuple-element.58) | copy-start | bytes 3932164
  394.8 30.6 %copy-start.4 = (bf16[320,1024]{1,0:T(8,128)(2,1)S(1)}, bf16[320,1024]{1,0:T(8,128)(2,1)}, u32[]{:S(2)}) copy-start(bf16[320,1024]{1,0:T(8,128)(2,1)} %get-tuple-element.59) | copy-start | bytes 1966084
  394.8 30.6 %copy-start.5 = (bf16[320,1024]{1,0:T(8,128)(2,1)S(1)}, bf16[320,1024]{1,0:T(8,128)(2,1)}, u32[]{:S(2)}) copy-start(bf16[320,1024]{1,0:T(8,128)(2,1)} %get-tuple-element.75) | copy-start | bytes 1966084
  394.8 30.6 %copy-start.6 = (bf16[320,1024]{1,0:T(8,128)(2,1)S(1)}, bf16[320,1024]{1,0:T(8,128)(2,1)}, u32[]{:S(2)}) copy-start(bf16[320,1024]{1,0:T(8,128)(2,1)} %get-tuple-element.74) | copy-start | bytes 1966084
  425.4 2.6 copy-start.2

commit v5 on v4

--- a/solution.py
+++ b/solution.py
@@ -109,9 +109,17 @@
     return w * cos + rot * sin
 
 
+def span_at(order, j):
+    s, f = lax.axis_index("seq"), lax.axis_index("fsdp")
+    x, c = s // 2, s % 2
+    a, b, away = j % 8 // 4, j % 4 // 2, j // 8
+    q = (x + a - 2 * x * a) * 2 + c + b - 2 * c * b
+    return order[(q * 2 + f + away - 2 * f * away) * 2 + j % 2]
+
+
 def front_kernel(
-    spans, tok, w3, small, rtab, stab, tok_out, wc_out, small_all, h_out, q, kv, cos_out, sin_out,
-    tok_all, wc, h, cos, sin, s_tok, s_w, s_own, s_kv, s_end
+    order, tok, w3, norm1, norm2, router, rtab, stab, tok_out, wc_out, small_all, h_out, q, kv, cos_out, sin_out,
+    small, tok_all, wc, h, cos, sin, s_tok, s_w, s_own, s_kv, s_end
 ):
     z, s, f = lax.axis_index("dp"), lax.axis_index("seq"), lax.axis_index("fsdp")
     core = s % 2
@@ -133,12 +141,17 @@
 
     own_rows = pl.ds(pl.multiple_of(f * part, part), part)
     pieces = []
-    for first, n, to in ((0, 256, 0), (width, 128, 256), (width + width // 2, 128, 384)):
+    for first, n, to in ((width, 128, 256), (width + width // 2, 128, 384), (0, 256, 0)):
         src = w3.at[:, pl.ds(pl.multiple_of(first + s * n, 128), n)]
         pieces.append((src, wc.at[own_rows, pl.ds(to, n)]))
     local = [pltpu.make_async_copy(a, b, s_own.at[i]) for i, (a, b) in enumerate(pieces)]
     for copy in local:
         copy.start()
+    n_exp = router.shape[1]
+    row = lax.broadcasted_iota(jnp.int32, (small.shape[0] - n_exp, part), 0)
+    gains = [v[...].astype(F32).reshape(1, part) for v in (norm1, norm2)]
+    small[:n_exp, :] = jnp.transpose(router[...].astype(F32)).astype(BF)
+    small[n_exp:, :] = jnp.where(row == 0, gains[0], jnp.where(row == 1, gains[1], 0.0)).astype(BF)
     small_all[:, own_rows] = small[...]
     tok_all[0] = tok[...]
     pl.semaphore_wait(barrier, 3)
@@ -146,14 +159,14 @@
     near = remote(tok, tok_all.at[1], s_tok, 0, peer_core)
     onward = remote(tok_all.at[2], tok_all.at[3], s_tok, 2, peer_core)
     weights = [remote(a, b, s_w, i, peer_y) for i, (a, b) in enumerate(pieces)]
-    weights.append(remote(small, small_all.at[:, own_rows], s_w, 3, peer_y))
+    weights.insert(0, remote(small, small_all.at[:, own_rows], s_w, 3, peer_y))
     over.start()
     for copy in weights:
         copy.start()
     near.start()
     for copy in local:
         copy.wait()
-    for copy in weights:
+    for copy in weights[:3]:
         copy.wait_recv()
     gain = small_all[16:17, :].astype(F32)
 
@@ -161,12 +174,11 @@
         at = pl.ds(pl.multiple_of(t * rows, rows), rows)
         return remote(kv.at[0, at], kv.at[1, at], s_kv, t, peer_y)
 
-    ends = [pltpu.make_async_copy(wc, wc_out, s_end.at[0])]
-    ends[0].start()
+    ends = []
     span = rows // 2
     for k in range(8):
         at = pl.ds(k * span, span)
-        row = pl.ds(spans[k], 1)
+        row = pl.ds(span_at(order, k), 1)
         c, n = stab[0, row, :], stab[1, row, :]
         cos[at, :] = rtab[0] * c - rtab[1] * n
         sin[at, :] = rtab[1] * c + rtab[0] * n
@@ -195,15 +207,24 @@
         normed, _ = rms_parts(tok_all[t].astype(F32))
         hidden = (normed * gain).astype(BF)
         h[at, :] = hidden
-        proj = mm(hidden, wc[...])
-        c, n = cos[at, :], sin[at, :]
-        kv[0, at, :128] = rope_rows(proj[:, 256:384], c, n).astype(BF)
-        kv[0, at, 128:] = proj[:, 384:].astype(BF)
+        proj = mm(hidden, wc[:, 256:])
+        kv[0, at, :128] = rope_rows(proj[:, :128], cos[at, :], sin[at, :]).astype(BF)
+        kv[0, at, 128:] = proj[:, 128:].astype(BF)
         kv_copy(t).start()
-        for k in range(2):
-            q[at, k * 128 : (k + 1) * 128] = rope_rows(proj[:, k * 128 : (k + 1) * 128], c, n).astype(BF)
         for copy in end(t):
             copy.start()
+
+    weights[3].wait_recv()
+    ends.append(pltpu.make_async_copy(wc, wc_out, s_end.at[0]))
+    ends[-1].start()
+
+    @pl.loop(0, 4)
+    def _(t):
+        at = pl.ds(pl.multiple_of(t * rows, rows), rows)
+        proj = mm(h[at, :], wc[:, :256])
+        for k in range(2):
+            w = proj[:, k * 128 : (k + 1) * 128]
+            q[at, k * 128 : (k + 1) * 128] = rope_rows(w, cos[at, :], sin[at, :]).astype(BF)
 
     for t in range(4):
         ends.extend(end(t))
@@ -215,8 +236,9 @@
         copy.wait_send()
 
 
-def front(spans, n_spans, tok, w3, small):
+def front(order, tok, w3, norm1, norm2, router):
     rows, width = tok.shape
+    n_spans = order.shape[0]
     span, half = rows // 2, HEAD_WIDTH // 2
     freqs = np.exp(np.arange(half) * (-2.0 * math.log(ROPE_BASE) / HEAD_WIDTH)).astype(np.float32)
 
@@ -231,12 +253,12 @@
     shape = jax.ShapeDtypeStruct
     return pl.pallas_call(
         front_kernel,
-        in_specs=[pl.BlockSpec(memory_space=pltpu.SMEM), vmem, hbm, vmem, vmem, vmem],
+        in_specs=[pl.BlockSpec(memory_space=pltpu.SMEM), vmem, hbm, vmem, vmem, vmem, vmem, vmem],
         out_specs=[hbm, hbm, vmem, hbm, vmem, vmem, hbm, hbm],
         out_shape=[
             shape((4, rows, width), BF),
             shape((width, 512), BF),
-            shape((small.shape[0], width), BF),
+            shape((32, width), BF),
             shape((4 * rows, width), BF),
             shape((4 * rows, 256), BF),
             shape((2, 4 * rows, 256), BF),
@@ -244,6 +266,7 @@
             shape((4 * rows, 128), F32),
         ],
         scratch_shapes=[
+            pltpu.VMEM((32, norm1.shape[0]), BF),
             pltpu.VMEM((4, rows, width), BF), pltpu.VMEM((width, 512), BF),
             pltpu.VMEM((4 * rows, width), BF),
             pltpu.VMEM((4 * rows, 128), F32), pltpu.VMEM((4 * rows, 128), F32),
@@ -251,15 +274,20 @@
         ],
         compiler_params=params(collective_id=2, has_side_effects=True),
         name="front",
-    )(spans, tok, w3, small, rtab, stab)
-
-
-def widen_kernel(*refs):
-    n = (len(refs) - 4) // 2
-    ins, outs = refs[:n], refs[n + 1 : 2 * n + 1]
-    for a, b in zip(ins, outs):
+    )(order, tok, w3, norm1, norm2, router, rtab, stab)
+
+
+def widen_kernel(*refs, wide, parts):
+    n = wide + parts + 1
+    ins, outs = refs[:n], refs[n:]
+    for a, b in zip(ins[:wide], outs[:wide]):
         b[...] = a[...].astype(F32)
-    tiny, (one, two, router) = refs[n], refs[2 * n + 1 :]
+    if parts:
+        total = ins[wide][...].astype(F32)
+        for part in ins[wide + 1 : wide + parts]:
+            total = total + part[...].astype(F32)
+        outs[wide][...] = total.astype(BF)
+    tiny, (one, two, router) = ins[-1], outs[-3:]
 
     @pl.when(pl.program_id(0) == 0)
     def _():
@@ -268,24 +296,26 @@
         router[...] = jnp.transpose(tiny[...])[:, : router.shape[1]]
 
 
-def widen(arrays, tiny, n_experts):
+def widen(arrays, parts, tiny, n_experts):
     flat = [a.reshape(-1, a.shape[-1]) for a in arrays]
-    steps = 8
-    wide = tiny.shape[1]
-    specs = [pl.BlockSpec((a.shape[0] // steps, a.shape[1]), lambda i: (i, 0)) for a in flat]
+    steps = 4
+    cols = tiny.shape[1]
+    block = lambda a: pl.BlockSpec((a.shape[0] // steps, a.shape[1]), lambda i: (i, 0))
     shape = jax.ShapeDtypeStruct
+    smalls = [(1, cols), (1, cols), (cols, n_experts)]
+    sums = [shape(p.shape, BF) for p in parts[:1]]
     got = pl.pallas_call(
-        widen_kernel,
+        functools.partial(widen_kernel, wide=len(flat), parts=len(parts)),
         grid=(steps,),
-        in_specs=specs + [whole(tiny.shape)],
-        out_specs=specs + [whole((1, wide)), whole((1, wide)), whole((wide, n_experts))],
-        out_shape=[shape(a.shape, F32) for a in flat]
-        + [shape((1, wide), F32), shape((1, wide), F32), shape((wide, n_experts), F32)],
+        in_specs=[block(a) for a in (*flat, *parts)] + [whole(tiny.shape)],
+        out_specs=[block(a) for a in (*flat, *sums)] + [whole(v) for v in smalls],
+        out_shape=[shape(a.shape, F32) for a in flat] + sums + [shape(v, F32) for v in smalls],
         compiler_params=params(),
         name="widen",
-    )(*flat, tiny)
+    )(*flat, *parts, tiny)
     n = len(arrays)
-    return [g.reshape(a.shape) for g, a in zip(got, arrays)] + [got[n][0], got[n + 1][0], got[n + 2]]
+    wide = [g.reshape(a.shape) for g, a in zip(got, arrays)]
+    return wide, got[n : n + len(sums)], [got[-3][0], got[-2][0], got[-1]]
 
 
 def project_back_kernel(
@@ -426,20 +456,24 @@
 
 
 def attend_short_kernel(
-    qtab_ref, ktab_ref, len_ref, q_ref, kv_ref, o_ref, low_ref, lse_ref, ks, vs, *, span, kb
+    order_ref, len_ref, q_ref, kv_ref, o_ref, low_ref, lse_ref, ks, vs, *, span, kb
 ):
     step = pl.program_id(0)
     count = ks.shape[0] // span
 
     @pl.when(step == 0)
     def _():
-        sort_spans(ktab_ref, kv_ref, ks, slice(0, 128), span, count)
-        sort_spans(ktab_ref, kv_ref, vs, slice(128, 256), span, count)
+        @pl.loop(0, count)
+        def _(j):
+            to = pl.ds(pl.multiple_of(span_at(order_ref, j) * span, span), span)
+            at = pl.ds(pl.multiple_of(j * span, span), span)
+            ks[to, :] = kv_ref[at, :128]
+            vs[to, :] = kv_ref[at, 128:]
 
     q = stack_heads(q_ref[:, :128], q_ref[:, 128:])
     rows = 2 * span
     limit = len_ref[0]
-    span_id = qtab_ref[step]
+    span_id = span_at(order_ref, step)
     _, blocks = block_counts(span_id, limit, span, kb)
     qpos = span_id * span + lax.broadcasted_iota(jnp.int32, (rows, kb), 0) % span
     last = jnp.minimum(qpos, limit - 1)
@@ -477,13 +511,12 @@
         pl.when(blocks == n)(functools.partial(run, n))
 
 
-def attend(qtab, ktab, limit, q, kv, span, kb):
+def attend(body, tables, q, kv, span, kb):
     steps, keys = q.shape[0] // span, kv.shape[0]
-    body = attend_short_kernel if keys <= 4 * kb else attend_kernel
     return pl.pallas_call(
         functools.partial(body, span=span, kb=kb),
         grid_spec=pltpu.PrefetchScalarGridSpec(
-            num_scalar_prefetch=3,
+            num_scalar_prefetch=len(tables),
             grid=(steps,),
             in_specs=[pl.BlockSpec((span, 256), lambda i, *_: (i, 0)), whole(kv.shape)],
             out_specs=[
@@ -500,7 +533,7 @@
         ],
         compiler_params=params(),
         name="attend",
-    )(qtab, ktab, limit, q, kv)
+    )(*tables, q, kv)
 
 
 def attend_back_kernel(
@@ -1389,10 +1422,10 @@
                 r.dv[...] = jnp.zeros_like(r.dv)
                 inside = lax.broadcasted_iota(jnp.int32, (span, 1), 0)
                 for k in range(2 * keys // span):
-                    r.kpos[k * span : (k + 1) * span, :] = r.ktab[k] * span + inside
+                    r.kpos[k * span : (k + 1) * span, :] = span_at(r.order, k) * span + inside
                 across = lax.broadcasted_iota(jnp.int32, (8, 4 * span), 1) % span
                 for k in range(8):
-                    r.last[k] = jnp.minimum(r.qtab[k] * span + across, r.limit[0] - 1)
+                    r.last[k] = jnp.minimum(span_at(r.order, k) * span + across, r.limit[0] - 1)
 
             @pl.when(m == 0)
             def _():
@@ -1630,9 +1663,9 @@
             args[k] = (v, hbm)
             inner[k + "_in"] = pltpu.VMEM(v.shape, v.dtype)
         smem = pl.BlockSpec(memory_space=pltpu.SMEM)
-        qtab, ktab, limit = tables
+        order, limit = tables
         args.update(
-            small=(small, vmem), qtab=(qtab, smem), ktab=(ktab, smem), limit=(limit, smem),
+            small=(small, vmem), order=(order, smem), limit=(limit, smem),
             moe1=(moes[0], hbm), moe3=(moes[1], hbm),
         )
         outs.update({k: (jax.ShapeDtypeStruct(moes[0].shape, BF), hbm) for k in ("got1", "got3")})
@@ -1698,28 +1731,26 @@
     owned = w_gate.shape[0]
     count = owned // 2
 
-    table = order.reshape(groups, shards, 2)
-    relative = jnp.arange(groups, dtype=jnp.int32) ^ seq
-    table = jnp.take(table, relative, axis=0)
-    qtab = jnp.take(table, fsdp, axis=1).reshape(-1)
-    if shards == 2:
-        held = jnp.stack([fsdp, 1 - fsdp])
-    else:
-        held = jnp.arange(shards)
-    ktab = jnp.transpose(jnp.take(table, held, axis=1), (1, 0, 2)).reshape(-1)
-    qpos = (qtab[:, None] * span + jnp.arange(span, dtype=jnp.int32)[None, :]).reshape(-1)
+    own = lax.dynamic_slice_in_dim(order, (seq * shards + fsdp) * 2, 2)
+    own_pos = (own[:, None] * span + jnp.arange(span, dtype=jnp.int32)[None, :]).reshape(-1)
 
     heads = QUERY_HEADS // groups
     qw, kw = heads * HEAD_WIDTH, KEY_VALUE_HEADS // groups * HEAD_WIDTH
     w3 = query_key_value_weight
-    small = jnp.concatenate(
-        [jnp.transpose(router), norm1[None], norm2[None], jnp.zeros((14, norm1.shape[0]), BF)]
-    )
     if shards == 2:
-        tok, wcols, small, hidden_one, q, kv, cos, sin = front(qtab, order.shape[0], x, w3, small)
+        tok, wcols, small, hidden_one, q, kv, cos, sin = front(order, x, w3, norm1, norm2, router)
         tok, kv = tok.reshape(groups * rows, width), kv.reshape(-1, 256)
         w_out, cotangent, kv = lax.optimization_barrier((w_out, cotangent, kv))
     else:
+        table = order.reshape(groups, shards, 2)
+        relative = jnp.arange(groups, dtype=jnp.int32) ^ seq
+        table = jnp.take(table, relative, axis=0)
+        qtab = jnp.take(table, fsdp, axis=1).reshape(-1)
+        ktab = jnp.transpose(table, (1, 0, 2)).reshape(-1)
+        qpos = (qtab[:, None] * span + jnp.arange(span, dtype=jnp.int32)[None, :]).reshape(-1)
+        small = jnp.concatenate(
+            [jnp.transpose(router), norm1[None], norm2[None], jnp.zeros((14, norm1.shape[0]), BF)]
+        )
         half = HEAD_WIDTH // 2
         freqs = jnp.exp(jnp.arange(half, dtype=F32) * (-2.0 * math.log(ROPE_BASE) / HEAD_WIDTH))
         angles = qpos.astype(F32)[:, None] * freqs[None, :]
@@ -1738,13 +1769,17 @@
     route_rows = small[:n_experts]
 
     kb = 4 * span
-    own_valid = (qpos[:rows] < limit[0])[:, None]
+    own_valid = (own_pos < limit[0])[:, None]
     masked_cot = jnp.where(own_valid, cotangent[0], jnp.zeros_like(cotangent[0]))
     if shards == 2:
         shared = w_out.shape[0] // 2
         wo_near = flip_y(lax.dynamic_slice_in_dim(w_out, core * shared, shared, 0))
         cot_y, cot_x = flip_y(masked_cot), flip_x(masked_cot)
-    attended, low, lse = attend(qtab, ktab, limit, q, kv, span, kb)
+    if shards == 2:
+        body, tables = attend_short_kernel, (order, limit)
+    else:
+        body, tables = attend_kernel, (qtab, ktab, limit)
+    attended, low, lse = attend(body, tables, q, kv, span, kb)
     inputs = x.astype(F32)
     if shards == 2:
         out = moe_layer(
@@ -1833,7 +1868,7 @@
                 q=q, kv=kv, do=d_heads, o=attended, lse=lse,
                 tok=tok, h=hidden_one, wc=wcols, cos=cos, sin=sin, dmid=d_middle, gout=grad_out,
             ),
-            small=small, tables=(qtab, ktab, limit), moes=moes,
+            small=small, tables=(order, limit), moes=moes,
         )
         d_inputs = got.dtok
     else:
@@ -1862,13 +1897,14 @@
         tiny = tiny_rows(jnp.sum(grad_norm1, axis=0))
         tiny = lax.psum_scatter(tiny, "fsdp", scatter_dimension=0, tiled=True)[0]
         got = reduce_grads(weight_grads, tiny, slots, shards, eo=outs, cols=cols)
-    grad_gate, grad_up, grad_down, shard_out, shard_qkv, *tiny = widen(
-        [got.gate, got.up, got.down, got.out, got.qkv], got.tiny_out, n_experts
+    parts = (middle, out.moe0, got.got1, out.got2, got.got3) if shards == 2 else ()
+    wide, sums, tiny = widen(
+        [got.gate, got.up, got.down, got.out, got.qkv, d_inputs], parts, got.tiny_out, n_experts
     )
+    grad_gate, grad_up, grad_down, shard_out, shard_qkv, d_inputs = wide
     shard_out, shard_qkv = shard_out[:shard_rows], shard_qkv[:shard_rows]
     if shards == 2:
-        parts = (out.moe0, got.got1, out.got2, got.got3)
-        layer_out = (middle + sum(p.astype(F32) for p in parts)).astype(BF)
+        layer_out = sums[0]
     else:
         layer_out = (middle + give_back(moe_parts)).astype(BF)
     return (

time: 429 us -> 422 us (0.984)
    pallas_call x1, Pallas kernels: 18.1 us -> 22.9 us  [attend(): pl.pallas_call(functools.partial(body, span=span, kb=kb), grid_spec=pltpu...]
  transfers between devices with their start and end apart: 3 -> 3, of which waited for: 1 -> 1; matrix products, arithmetic and copies ran while one was open for 1% -> 0% of each run, Pallas kernels for 4% -> 5%
where the time goes in v5:
time: 422 us
  Pallas kernels  409 us (97%)
  local copies, waits for them, and re-layouts  5.79 us (1%)
    pallas_call x1, Pallas kernels, reduce_grads(): pl.pallas_call(functools.partial(reduce_kernel, names=names, slots=slots,...  217 us
    pallas_call x1, Pallas kernels, moe_layer(): pl.pallas_call(functools.partial(moe_kernel, names=names, topk=routes.sha...  106 us
    pallas_call x1, Pallas kernels, front(): pl.pallas_call(front_kernel, in_specs=[pl.BlockSpec(memory_space=pltpu.SM...  33.8 us
    pallas_call x1, Pallas kernels, widen(): pl.pallas_call(functools.partial(widen_kernel, wide=len(flat), parts=len(...  29.8 us
    pallas_call x1, Pallas kernels, attend(): pl.pallas_call(functools.partial(body, span=span, kb=kb), grid_spec=pltpu...  22.9 us
  transfers between devices with their start and end apart: 3, of which 1 were waited for; matrix products, arithmetic and copies ran while one was open for 0% of the time, Pallas kernels for 5%

profile of v5, /device:TPU:0, one launch (start us, length us, event | category | flops | bytes accessed | tf_op | source)
XLA Modules:
  0.0 421.6 jit_solution(12204963516674387752)
XLA Ops:
  0.6 0.0 copy-start.1
  0.7 0.0 copy-start.2
  1.4 0.7 dynamic-slice_multiply_fusion
  2.2 0.1 add_compare_fusion
  2.3 0.1 lt.30
  2.3 1.5 copy.25.router
  3.8 33.8 %front.1 = (bf16[4,320,1024]{2,1,0:T(8,128)(2,1)}, bf16[1024,512]{1,0:T(8,128)(2,1)}, bf16[32,1024]{1,0:T(8,128)(2,1)}, bf16[1280,1024]{1,0:T(8,128)(2,1)}, bf16...) custom-call(s32[16]{0:T(128)} %refs_15_.1, ...), custom_call_target="tpu_custom_call" | custom-call | tf_op jit(solution)/shard_map/front/pallas_call | solution.py:254
  37.6 0.0 copy-done.2
  37.6 0.1 bitcast_select_fusion.refs_6_
  37.7 0.0 copy-start
  37.7 1.0 collective-permute-start.2
  38.8 1.1 collective-permute-start.1
  39.9 1.0 collective-permute-start
  40.9 0.8 copy.26
  41.7 22.9 %attend.1 = (f32[1280,256]{1,0:T(8,128)}, bf16[1280,256]{1,0:T(8,128)(2,1)}, f32[8,8,640]{2,1,0:T(8,128)}) custom-call(s32[16]{0:T(128)} %refs_15_.1, s32[1]{0:T(128)} %copy.28.len_ref.refs_16_, bf16[1280,256]{1,0:T(8,128)(2,1)} %get-tuple-element.53.q_ref.refs_2_, bf16[2560,256]{1,0:T(8,128)(2,1)} %bitcast.25), custom_call_target="tpu_custom_call" | custom-call | tf_op jit(solution)/shard_map/attend/pallas_call | solution.py:516
  64.6 1.2 collective-permute-done.refs_3_
  65.8 0.0 collective-permute-done.2.refs_8_
  65.8 0.0 collective-permute-done.1.refs_7_
  65.8 0.9 copy-done.3
  66.7 0.8 copy-done.4
  67.5 106.1 %moe_layer.1 = (f32[320,1024]{1,0:T(8,128)}, bf16[320,1024]{1,0:T(8,128)(2,1)}, bf16[320,1024]{1,0:T(8,128)(2,1)}, bf16[320,1024]{1,0:T(8,128)(2,1)}, bf16[320,1...) custom-call(bf16[4,320,256]{2,1,0:T(8,128)(2,1)} %bitcast.31, ...), custom_call_target="tpu_custom_call" | custom-call | tf_op jit(solution)/shard_map/moe_layer/pallas_call | solution.py:1101
  173.6 216.6 %reduce_grads.1 = (bf16[8,1024,512]{2,1,0:T(8,128)(2,1)}, bf16[8,1024,512]{2,1,0:T(8,128)(2,1)}, bf16[8,512,1024]{2,1,0:T(8,128)(2,1)}, bf16[512,1024]{1,0:T(8,1...) custom-call(bf16[24,2,2,128,512]{4,3,2,1,0:T(8,128)(2,1)} %bitcast.2, ...), custom_call_target="tpu_custom_call" | custom-call | tf_op jit(solution)/shard_map/reduce_grads/pallas_call | solution.py:1696
  390.2 29.8 %widen.1 = (f32[8192,512]{1,0:T(8,128)}, f32[8192,512]{1,0:T(8,128)}, f32[4096,1024]{1,0:T(8,128)}, f32[512,1024]{1,0:T(8,128)}, f32[512,2048]{1,0:T(8,128)}, /*...) custom-call(bf16[8192,512]{1,0:T(8,128)(2,1)} %bitcast.22, ...), custom_call_target="tpu_custom_call" | custom-call | tf_op jit(solution)/shard_map/widen/pallas_call | solution.py:307
  420.0 1.7 copy.27
  (9 shorter events, 0.0 us)
Async XLA Ops:
  0.6 39.2 %copy-start.1 = (bf16[512,1024]{1,0:T(8,128)(2,1)S(1)}, bf16[512,1024]{1,0:T(8,128)(2,1)}, u32[]{:S(2)}) copy-start(bf16[512,1024]{1,0:T(8,128)(2,1)} %refs_2_) | copy-start | bytes 3145732
  0.7 36.9 %copy-start.2 = (bf16[1,320,1024]{2,1,0:T(8,128)(2,1)S(1)}, bf16[1,320,1024]{2,1,0:T(8,128)(2,1)}, u32[]{:S(2)}) copy-start(bf16[1,320,1024]{2,1,0:T(8,128)(2,1)} %param.16) | copy-start | bytes 1966084
  3.8 37.1 %copy-start.6 = (s32[1,320,8]{1,2,0:T(8,128)S(1)}, s32[1,320,8]{1,2,0:T(8,128)}, u32[]{:S(2)}) copy-start(s32[1,320,8]{1,2,0:T(8,128)} %param.19) | copy-start | bytes 30724
  37.7 1.0 copy-start
  37.7 28.0 %collective-permute-start.2 = (bf16[320,1024]{1,0:T(8,128)(2,1)S(1)}, bf16[320,1024]{1,0:T(8,128)(2,1)S(1)}, u32[]{:S(2)}, u32[]{:S(2)}) collective-permute-start(bf16[320,1024]{1,0:T(8,128)(2,1)S(1)} %bitcast_select_fusion.refs_6_), channel_id=1, source_target_pairs={{0,4},{4,0},{2,6},{6,2},{1,5},{5,1},{3,7},{7,3},{8,12},{12,8},{10,... | collective-permute-start | bytes 1966088 | tf_op jit(solution)/shard_map/ppermute | solution.py:1120
  38.8 27.0 %collective-permute-start.1 = (bf16[320,1024]{1,0:T(8,128)(2,1)S(1)}, bf16[320,1024]{1,0:T(8,128)(2,1)S(1)}, u32[]{:S(2)}, u32[]{:S(2)}) collective-permute-start(bf16[320,1024]{1,0:T(8,128)(2,1)S(1)} %bitcast_select_fusion.refs_6_), channel_id=1, source_target_pairs={{0,1},{1,0},{2,3},{3,2},{4,5},{5,4},{6,7},{7,6},{8,9},{9,8},{10,11... | collective-permute-start | bytes 1966088 | tf_op jit(solution)/shard_map/ppermute | solution.py:1128
  39.9 25.9 %collective-permute-start = (bf16[256,1024]{1,0:T(8,128)(2,1)S(1)}, bf16[256,1024]{1,0:T(8,128)(2,1)S(1)}, u32[]{:S(2)}, u32[]{:S(2)}) collective-permute-start(bf16[256,1024]{1,0:T(8,128)(2,1)S(1)} %constant_dynamic-slice_fusion), channel_id=1, source_target_pairs={{0,1},{1,0},{2,3},{3,2},{4,5},{5,4},{6,7},{7,6},{8,9},{9,8},{10,11... | collective-permute-start | bytes 1572872 | tf_op jit(solution)/shard_map/ppermute | solution.py:1128
  65.8 1.7 copy-start.5
  65.8 0.9 copy-start.3
  66.7 0.8 copy-start.4

commit v6 on v5

--- a/solution.py
+++ b/solution.py
@@ -147,10 +147,10 @@
     local = [pltpu.make_async_copy(a, b, s_own.at[i]) for i, (a, b) in enumerate(pieces)]
     for copy in local:
         copy.start()
-    n_exp = router.shape[1]
+    n_exp = router.shape[0]
     row = lax.broadcasted_iota(jnp.int32, (small.shape[0] - n_exp, part), 0)
     gains = [v[...].astype(F32).reshape(1, part) for v in (norm1, norm2)]
-    small[:n_exp, :] = jnp.transpose(router[...].astype(F32)).astype(BF)
+    small[:n_exp, :] = router[...]
     small[n_exp:, :] = jnp.where(row == 0, gains[0], jnp.where(row == 1, gains[1], 0.0)).astype(BF)
     small_all[:, own_rows] = small[...]
     tok_all[0] = tok[...]
@@ -293,7 +293,7 @@
     def _():
         one[...] = tiny[16:17, :]
         two[...] = tiny[17:18, :]
-        router[...] = jnp.transpose(tiny[...])[:, : router.shape[1]]
+        router[...] = tiny[: router.shape[0], :]
 
 
 def widen(arrays, parts, tiny, n_experts):
@@ -302,7 +302,7 @@
     cols = tiny.shape[1]
     block = lambda a: pl.BlockSpec((a.shape[0] // steps, a.shape[1]), lambda i: (i, 0))
     shape = jax.ShapeDtypeStruct
-    smalls = [(1, cols), (1, cols), (cols, n_experts)]
+    smalls = [(1, cols), (1, cols), (n_experts, cols)]
     sums = [shape(p.shape, BF) for p in parts[:1]]
     got = pl.pallas_call(
         functools.partial(widen_kernel, wide=len(flat), parts=len(parts)),
@@ -315,7 +315,7 @@
     )(*flat, *parts, tiny)
     n = len(arrays)
     wide = [g.reshape(a.shape) for g, a in zip(got, arrays)]
-    return wide, got[n : n + len(sums)], [got[-3][0], got[-2][0], got[-1]]
+    return wide, got[n : n + len(sums)], [got[-3][0], got[-2][0], jnp.transpose(got[-1])]
 
 
 def project_back_kernel(
@@ -737,10 +737,19 @@
     def block(t):
         return pl.ds(pl.multiple_of(t * rows, rows), rows)
 
-    load_cots = [
-        pltpu.make_async_copy(v, cots.at[block(i)], r.s_cot.at[i])
-        for i, v in enumerate((r.cot, r.cot_y, r.cot_x))
-    ]
+    def rows_x(i):
+        return pl.ds(pl.multiple_of(rows + 2 * i * rows, n), n)
+
+    def rows_y(i):
+        return pl.ds(pl.multiple_of(rows + n + 2 * i * rows, n), n)
+
+    load_cots = [pltpu.make_async_copy(r.cot, cots.at[block(0)], r.s_cot.at[0])]
+    for i in range(2):
+        at = pl.ds(i * n, n)
+        load_cots += [
+            pltpu.make_async_copy(r.cot_x.at[at], cots.at[rows_x(i)], r.s_cot.at[1 + i]),
+            pltpu.make_async_copy(r.cot_y.at[at], cots.at[rows_y(i)], r.s_cot.at[3 + i]),
+        ]
     for copy in load_cots:
         copy.start()
 
@@ -761,8 +770,8 @@
     for copy in heads:
         copy.start()
     diag = [
-        remote(r.cot_x.at[pl.ds(0, n)], cots.at[pl.ds(3 * rows, n)], r.s_diag, 0, peer_y),
-        remote(r.cot_y.at[pl.ds(n, n)], cots.at[pl.ds(3 * rows + n, n)], r.s_diag, 1, peer_x),
+        remote(r.cot_x.at[pl.ds(0, n)], cots.at[pl.ds(2 * rows, n)], r.s_diag, 0, peer_y),
+        remote(r.cot_x.at[pl.ds(n, n)], cots.at[pl.ds(2 * rows + n, n)], r.s_diag, 1, peer_y),
     ]
     wo_rows = pl.ds(pl.multiple_of(core * (ff // 2), ff // 2), ff // 2)
     wo_there = r.wo_there
@@ -770,8 +779,7 @@
     wo_share = remote(r.wo_near, wo_there.at[wo_rows], r.s_diag, 2, peers[1])
     wo_copy.start()
     wo_share.start()
-    for copy in diag:
-        copy.start()
+    diag[0].start()
 
     small = r.small
     table = r.table
@@ -788,10 +796,9 @@
     wo_copy.wait()
     wo_share.wait_recv()
     def share(i, j, dev):
-        at = pl.multiple_of(i * n, n)
-        return remote(
-            hx.at[pl.ds(at, n)], hx.at[pl.ds((j + 1) * rows + at, n)], r.s_h, 2 * j + i, dev
-        )
+        at = pl.ds(pl.multiple_of(i * n, n), n)
+        to = rows_x(i) if j else rows_y(i)
+        return remote(hx.at[at], hx.at[to], r.s_h, 2 * j + i, dev)
 
     @pl.loop(0, 2)
     def _(i):
@@ -823,41 +830,47 @@
         share(i, 1, peer_x).start()
 
     shares = [share(i, j, dev) for i in range(2) for j, dev in ((0, peer_y), (1, peer_x))]
-    second = remote(
-        hx.at[pl.ds(rows + n, n)], hx.at[pl.ds(3 * rows + n, n)], r.s_h, 4, peer_x
-    )
-    first = remote(hx.at[pl.ds(2 * rows, n)], hx.at[pl.ds(3 * rows, n)], r.s_h, 5, peer_y)
+    second = remote(hx.at[rows_y(1)], hx.at[pl.ds(2 * rows + n, n)], r.s_h, 4, peer_x)
+    first = remote(hx.at[rows_x(0)], hx.at[pl.ds(2 * rows, n)], r.s_h, 5, peer_y)
 
     dhs, moe, dh, dgates = r.dhs, r.moe_acc, r.dh_acc, r.dg_acc
-    few = 3 * rows // 4
-    half_rows = [(0, n), (n, n)]
+    back_x = [
+        remote(dhs.at[rows_x(i)], r.rdh.at[1, pl.ds(i * n, n)], r.s_d, i, peer_x) for i in range(2)
+    ]
     back_y = [
-        remote(dhs.at[pl.ds(rows + a, k)], r.rdh.at[0, pl.ds(a, k)], r.s_d, i, peer_y)
-        for i, (a, k) in enumerate(half_rows)
+        remote(dhs.at[rows_y(i)], r.rdh.at[0, pl.ds(i * n, n)], r.s_d, 2 + i, peer_y) for i in range(2)
     ]
-    back_x = remote(dhs.at[block(2)], r.rdh.at[1], r.s_d, 2, peer_x)
-
-    def two_hops(a, k, sem, first_dev, second_dev):
-        via = r.via.at[pl.ds(a, k)]
+
+    def two_hops(i, sem, first_dev, second_dev):
+        at = pl.ds(i * n, n)
         return (
-            remote(dhs.at[pl.ds(3 * rows + a, k)], via, r.s_d, sem, first_dev),
-            remote(via, r.rdd.at[pl.ds(a, k)], r.s_d, sem + 1, second_dev),
-        )
-
-    hop_y0, end_x0 = two_hops(0, n, 3, peer_y, peer_x)
-    hop_y1, end_x1 = two_hops(n, few - n, 5, peer_y, peer_x)
-    hop_x, end_y = two_hops(few, rows - few, 7, peer_x, peer_y)
-    moe_x = remote(r.moe2, r.got2, r.s_d, 9, peer_x)
-
-    moes = (r.moe0, r.moe1, r.moe2, r.moe3)
-
-    def moe_out(t):
-        return pltpu.make_async_copy(r.mstage.at[(0, 1, 1, 0)[t]], moes[t], r.s_m.at[t])
+            remote(dhs.at[pl.ds(2 * rows + i * n, n)], r.via.at[at], r.s_d, sem, first_dev),
+            remote(r.via.at[at], r.rdd.at[at], r.s_d, sem + 1, second_dev),
+        )
+
+    hop_y, end_x = two_hops(0, 4, peer_y, peer_x)
+    hop_x, end_y = two_hops(1, 6, peer_x, peer_y)
+    moe_x = remote(r.moe2, r.got2, r.s_d, 8, peer_x)
+
+    def moe_out(turn):
+        src = r.mstage.at[turn % 2]
+        if turn % 2 == 0:
+            return [pltpu.make_async_copy(src, (r.moe0, r.moe3)[turn // 2], r.s_m.at[turn])]
+        to = pl.ds(turn // 2 * n, n)
+        return [
+            pltpu.make_async_copy(src.at[pl.ds(0, n)], r.moe2.at[to], r.s_m.at[turn]),
+            pltpu.make_async_copy(src.at[pl.ds(n, n)], r.moe1.at[to], r.s_m.at[turn + 3]),
+        ]
+
+    def forward():
+        hop_y.wait_recv()
+        end_x.start()
+        hop_x.wait_recv()
+        end_y.start()
 
     @pl.loop(0, 4 * count)
     def _(k):
-        turn, e = k // count, k % count
-        t = 2 * turn - turn // 2 - 4 * (turn // 3)
+        t, e = k // count, k % count
 
         @pl.when(k < count)
         def _():
@@ -873,8 +886,9 @@
                 copy.wait_recv()
             second.start()
             first.start()
-            load_cots[1].wait()
-            load_cots[2].wait()
+            diag[1].start()
+            for copy in load_cots[1:]:
+                copy.wait()
 
         @pl.when(k == 2 * count)
         def _():
@@ -883,6 +897,7 @@
             for copy in diag:
                 copy.wait_recv()
 
+        pl.when(k == 4 * count - 1)(forward)
         at = block(t)
         h, c = hx[at, :width], cots[at, :]
         wg, wu, wd = r.wgs[e], r.wus[e], r.wds[e]
@@ -916,31 +931,22 @@
 
         @pl.when(e == count - 1)
         def _():
-            for i, k in enumerate((0, 2, 3, 1)):
-                @pl.when(t == k)
-                def _():
-                    if i >= 2:
-                        moe_out((0, 2)[i - 2]).wait()
-                    r.mstage[i % 2] = moe[...].astype(BF)
-                    moe_out(k).start()
-
             dhs[at, :width] = dh[...].astype(BF)
             dhs[at, width:] = dgates[...].astype(BF)
-
-            @pl.when(t == 1)
-            def _():
-                for copy in back_y:
-                    copy.start()
-
-            @pl.when(t == 2)
-            def _():
-                back_x.start()
-
-            @pl.when(t == 3)
-            def _():
-                hop_y0.start()
-                hop_x.start()
-                hop_y1.start()
+            for i in range(4):
+                @pl.when(t == i)
+                def _():
+                    if i == 2:
+                        hop_y.start()
+                        hop_x.start()
+                    elif i > 0:
+                        back_x[i // 2].start()
+                        back_y[i // 2].start()
+                    for copy in moe_out(i - 2) if i >= 2 else ():
+                        copy.wait()
+                    r.mstage[i % 2] = moe[...].astype(BF)
+                    for copy in moe_out(i):
+                        copy.start()
 
     stage = r.stage
 
@@ -995,34 +1001,27 @@
             cols = slice(k * 256, (k + 1) * 256)
             r.gout[cols, :] = mm_tn(tout[:, cols], dattn[...]).astype(BF)
 
-    def forward0():
-        hop_y0.wait_recv()
-        end_x0.start()
-
-    def forward1():
-        hop_y1.wait_recv()
-        end_x1.start()
-        hop_x.wait_recv()
-        end_y.start()
+    def send_moe():
+        for copy in moe_out(3):
+            copy.wait()
         moe_x.start()
 
     def back0():
-        for copy in (back_y[0], back_x, end_x0):
+        for copy in (back_x[0], back_y[0], end_x):
             copy.wait_recv()
         middle_back(0)
 
     def back1():
-        for copy in (back_y[1], end_x1, end_y):
+        for copy in (back_x[1], back_y[1], end_y):
             copy.wait_recv()
         middle_back(1)
 
     @pl.loop(0, 3 * count)
     def _(k):
         e, j = k // 3, k % 3
-        pl.when(k == 0)(forward0)
-        pl.when(k == 2)(forward1)
-        pl.when(k == 3 * count - 6)(back0)
-        pl.when(k == 3 * count - 1)(back1)
+        pl.when(k == 1)(send_moe)
+        pl.when(k == 3 * count - 7)(back0)
+        pl.when(k == 3 * count - 4)(back1)
 
         @pl.when(k > 0)
         def _():
@@ -1045,11 +1044,11 @@
 
     grad_copy(0, 0).wait()
     grad_copy(0, 1).wait()
-    moe_out(3).wait()
-    moe_out(1).wait()
+    for copy in moe_out(2):
+        copy.wait()
     for copy in (*returns[0], *returns[1], moe_x):
         copy.wait()
-    for copy in (*heads, *diag, wo_share, *shares, first, second, *back_y, back_x, hop_x, hop_y0, hop_y1, end_y, end_x0, end_x1):
+    for copy in (*heads, *diag, wo_share, *shares, first, second, *back_y, *back_x, hop_x, hop_y, end_y, end_x):
         copy.wait_send()
 
 
@@ -1094,8 +1093,8 @@
         via=pltpu.VMEM((rows, ext), BF), rdd=pltpu.VMEM((rows, ext), BF),
         dattn=pltpu.VMEM((rows, width), BF), dto=pltpu.VMEM((rows, width), BF),
         dsend=pltpu.VMEM((4, rows, 256), BF), stage=pltpu.VMEM((2, ff, ff), BF),
-        s_att=dma((2, 8)), s_diag=dma((2, 3)), s_h=dma((2, 6)), s_d=dma((2, 10)), s_back=dma((2, 8)),
-        s_cot=dma((3,)), s_wo=dma((1,)), s_w=dma((3, count)), s_m=dma((4,)), s_g=dma((2,)),
+        s_att=dma((2, 8)), s_diag=dma((2, 3)), s_h=dma((2, 6)), s_d=dma((2, 9)), s_back=dma((2, 8)),
+        s_cot=dma((5,)), s_wo=dma((1,)), s_w=dma((3, count)), s_m=dma((7,)), s_g=dma((2,)),
     )
     names = tuple(args) + tuple(outs) + tuple(scratch)
     got = pl.pallas_call(
@@ -1738,7 +1737,9 @@
     qw, kw = heads * HEAD_WIDTH, KEY_VALUE_HEADS // groups * HEAD_WIDTH
     w3 = query_key_value_weight
     if shards == 2:
-        tok, wcols, small, hidden_one, q, kv, cos, sin = front(order, x, w3, norm1, norm2, router)
+        tok, wcols, small, hidden_one, q, kv, cos, sin = front(
+            order, x, w3, norm1, norm2, jnp.transpose(router)
+        )
         tok, kv = tok.reshape(groups * rows, width), kv.reshape(-1, 256)
         w_out, cotangent, kv = lax.optimization_barrier((w_out, cotangent, kv))
     else:

time: 422 us -> 418 us (level)
  Pallas kernels: 409 us -> 404 us
  waiting for transfers between devices: 1.23 us -> 5.51 us
    ppermute x2, waiting for transfers between devices: 1.22 us -> 5.5 us  [flip_y(): return lax.ppermute(x, 'fsdp', [(0, 1), (1, 0)])]
    pallas_call x1, Pallas kernels: 22.9 us -> 18.6 us  [attend(): pl.pallas_call(functools.partial(body, span=span, kb=kb), grid_spec=pltpu...]
  transfers between devices with their start and end apart: 3 -> 3, of which waited for: 1 -> 1; matrix products, arithmetic and copies ran while one was open for 0% -> 0% of each run, Pallas kernels for 5% -> 4%
where the time goes in v6:
time: 418 us; the launch traced here: 417 us
  Pallas kernels  404 us (97%)
  waiting for transfers between devices  5.51 us (1%)
    pallas_call x1, Pallas kernels, reduce_grads(): pl.pallas_call(functools.partial(reduce_kernel, names=names, slots=slots,...  217 us
    pallas_call x1, Pallas kernels, moe_layer(): pl.pallas_call(functools.partial(moe_kernel, names=names, topk=routes.sha...  105 us
    pallas_call x1, Pallas kernels, front(): pl.pallas_call(front_kernel, in_specs=[pl.BlockSpec(memory_space=pltpu.SM...  33.7 us
    pallas_call x1, Pallas kernels, widen(): pl.pallas_call(functools.partial(widen_kernel, wide=len(flat), parts=len(...  29.6 us
    pallas_call x1, Pallas kernels, attend(): pl.pallas_call(functools.partial(body, span=span, kb=kb), grid_spec=pltpu...  18.6 us
  transfers between devices with their start and end apart: 3, of which 1 were waited for; matrix products, arithmetic and copies ran while one was open for 0% of the time, Pallas kernels for 4%

profile of v6, /device:TPU:0, one launch (start us, length us, event | category | flops | bytes accessed | tf_op | source)
XLA Modules:
  0.0 417.5 jit_solution(9850800007108990641)
XLA Ops:
  0.6 0.0 copy-start.1
  0.7 0.0 copy-start.2
  1.4 0.7 dynamic-slice_multiply_fusion
  2.2 0.1 add_compare_fusion
  2.3 0.1 lt.30
  2.3 33.7 %front.1 = (bf16[4,320,1024]{2,1,0:T(8,128)(2,1)}, bf16[1024,512]{1,0:T(8,128)(2,1)}, bf16[32,1024]{1,0:T(8,128)(2,1)}, bf16[1280,1024]{1,0:T(8,128)(2,1)}, bf16...) custom-call(s32[16]{0:T(128)} %refs_15_.1, ...), custom_call_target="tpu_custom_call" | custom-call | tf_op jit(solution)/shard_map/front/pallas_call | solution.py:254
  36.1 0.0 copy-done.2
  36.1 0.1 bitcast_select_fusion.refs_6_
  36.2 0.0 copy-start
  36.2 1.0 collective-permute-start.2
  37.2 0.0 copy-done
  37.2 1.1 collective-permute-start.1
  38.3 0.0 copy-done.1
  38.4 1.0 collective-permute-start
  39.4 0.8 copy.25
  40.2 18.6 %attend.1 = (f32[1280,256]{1,0:T(8,128)}, bf16[1280,256]{1,0:T(8,128)(2,1)}, f32[8,8,640]{2,1,0:T(8,128)}) custom-call(s32[16]{0:T(128)} %refs_15_.1, s32[1]{0:T(128)} %copy.26.len_ref.refs_16_, bf16[1280,256]{1,0:T(8,128)(2,1)} %get-tuple-element.53.q_ref.refs_2_, bf16[2560,256]{1,0:T(8,128)(2,1)} %bitcast.27), custom_call_target="tpu_custom_call" | custom-call | tf_op jit(solution)/shard_map/attend/pallas_call | solution.py:516
  58.8 5.5 %collective-permute-done.refs_3_ = bf16[256,1024]{1,0:T(8,128)(2,1)S(1)} collective-permute-done((bf16[256,1024]{1,0:T(8,128)(2,1)S(1)}, bf16[256,1024]{1,0:T(8,128)(2,1)S(1)}, u32[]{:S(2)}, u32[]{:S(2)}) %collective-permute-start) | collective-permute-done | bytes 524320 | tf_op jit(solution)/shard_map/ppermute | solution.py:1127
  64.3 0.0 collective-permute-done.2.refs_8_
  64.3 0.0 collective-permute-done.1.refs_7_
  64.3 0.9 copy-done.3
  65.1 0.8 copy-done.4
  66.0 104.9 %moe_layer.1 = (f32[320,1024]{1,0:T(8,128)}, bf16[320,1024]{1,0:T(8,128)(2,1)}, bf16[320,1024]{1,0:T(8,128)(2,1)}, bf16[320,1024]{1,0:T(8,128)(2,1)}, bf16[320,1...) custom-call(bf16[4,320,256]{2,1,0:T(8,128)(2,1)} %bitcast.33, ...), custom_call_target="tpu_custom_call" | custom-call | tf_op jit(solution)/shard_map/moe_layer/pallas_call | solution.py:1100
  170.9 216.8 %reduce_grads.1 = (bf16[8,1024,512]{2,1,0:T(8,128)(2,1)}, bf16[8,1024,512]{2,1,0:T(8,128)(2,1)}, bf16[8,512,1024]{2,1,0:T(8,128)(2,1)}, bf16[512,1024]{1,0:T(8,1...) custom-call(bf16[24,2,2,128,512]{4,3,2,1,0:T(8,128)(2,1)} %bitcast.2, ...), custom_call_target="tpu_custom_call" | custom-call | tf_op jit(solution)/shard_map/reduce_grads/pallas_call | solution.py:1695
  387.7 29.6 %widen.1 = (f32[8192,512]{1,0:T(8,128)}, f32[8192,512]{1,0:T(8,128)}, f32[4096,1024]{1,0:T(8,128)}, f32[512,1024]{1,0:T(8,128)}, f32[512,2048]{1,0:T(8,128)}, /*...) custom-call(bf16[8192,512]{1,0:T(8,128)(2,1)} %bitcast.24, ...), custom_call_target="tpu_custom_call" | custom-call | tf_op jit(solution)/shard_map/widen/pallas_call | solution.py:307
  (7 shorter events, 0.0 us)
Async XLA Ops:
  0.6 37.7 %copy-start.1 = (bf16[512,1024]{1,0:T(8,128)(2,1)S(1)}, bf16[512,1024]{1,0:T(8,128)(2,1)}, u32[]{:S(2)}) copy-start(bf16[512,1024]{1,0:T(8,128)(2,1)} %refs_2_) | copy-start | bytes 3145732
  0.7 35.4 %copy-start.2 = (bf16[1,320,1024]{2,1,0:T(8,128)(2,1)S(1)}, bf16[1,320,1024]{2,1,0:T(8,128)(2,1)}, u32[]{:S(2)}) copy-start(bf16[1,320,1024]{2,1,0:T(8,128)(2,1)} %param.16) | copy-start | bytes 1966084
  2.3 37.0 %copy-start.6 = (s32[1,320,8]{1,2,0:T(8,128)S(1)}, s32[1,320,8]{1,2,0:T(8,128)}, u32[]{:S(2)}) copy-start(s32[1,320,8]{1,2,0:T(8,128)} %param.19) | copy-start | bytes 30724
  36.2 1.0 copy-start
  36.2 28.0 %collective-permute-start.2 = (bf16[320,1024]{1,0:T(8,128)(2,1)S(1)}, bf16[320,1024]{1,0:T(8,128)(2,1)S(1)}, u32[]{:S(2)}, u32[]{:S(2)}) collective-permute-start(bf16[320,1024]{1,0:T(8,128)(2,1)S(1)} %bitcast_select_fusion.refs_6_), channel_id=1, source_target_pairs={{0,4},{4,0},{2,6},{6,2},{1,5},{5,1},{3,7},{7,3},{8,12},{12,8},{10,... | collective-permute-start | bytes 1966088 | tf_op jit(solution)/shard_map/ppermute | solution.py:1119
  37.2 27.0 %collective-permute-start.1 = (bf16[320,1024]{1,0:T(8,128)(2,1)S(1)}, bf16[320,1024]{1,0:T(8,128)(2,1)S(1)}, u32[]{:S(2)}, u32[]{:S(2)}) collective-permute-start(bf16[320,1024]{1,0:T(8,128)(2,1)S(1)} %bitcast_select_fusion.refs_6_), channel_id=1, source_target_pairs={{0,1},{1,0},{2,3},{3,2},{4,5},{5,4},{6,7},{7,6},{8,9},{9,8},{10,11... | collective-permute-start | bytes 1966088 | tf_op jit(solution)/shard_map/ppermute | solution.py:1127
  38.4 25.9 %collective-permute-start = (bf16[256,1024]{1,0:T(8,128)(2,1)S(1)}, bf16[256,1024]{1,0:T(8,128)(2,1)S(1)}, u32[]{:S(2)}, u32[]{:S(2)}) collective-permute-start(bf16[256,1024]{1,0:T(8,128)(2,1)S(1)} %constant_dynamic-slice_fusion), channel_id=1, source_target_pairs={{0,1},{1,0},{2,3},{3,2},{4,5},{5,4},{6,7},{7,6},{8,9},{9,8},{10,11... | collective-permute-start | bytes 1572872 | tf_op jit(solution)/shard_map/ppermute | solution.py:1127
  64.3 1.7 copy-start.5
  64.3 0.9 copy-start.3
  65.1 0.8 copy-start.4

commit v7 on v6

--- a/solution.py
+++ b/solution.py
@@ -531,7 +531,7 @@
             jax.ShapeDtypeStruct((q.shape[0], 256), BF),
             jax.ShapeDtypeStruct((steps, 8, 4 * span), F32),
         ],
-        compiler_params=params(),
+        compiler_params=pltpu.CompilerParams(vmem_limit_bytes=67043328),
         name="attend",
     )(*tables, q, kv)
 

time: 418 us -> 418 us (level)
  no operation moved by 1% of the time
where the time goes in v7:
time: 418 us; the launch traced here: 417 us
  Pallas kernels  403 us (96%)
  waiting for transfers between devices  5.91 us (1%)
    pallas_call x1, Pallas kernels, reduce_grads(): pl.pallas_call(functools.partial(reduce_kernel, names=names, slots=slots,...  217 us
    pallas_call x1, Pallas kernels, moe_layer(): pl.pallas_call(functools.partial(moe_kernel, names=names, topk=routes.sha...  105 us
    pallas_call x1, Pallas kernels, front(): pl.pallas_call(front_kernel, in_specs=[pl.BlockSpec(memory_space=pltpu.SM...  33.7 us
    pallas_call x1, Pallas kernels, widen(): pl.pallas_call(functools.partial(widen_kernel, wide=len(flat), parts=len(...  29.6 us
    pallas_call x1, Pallas kernels, attend(): pl.pallas_call(functools.partial(body, span=span, kb=kb), grid_spec=pltpu...  17.8 us
  transfers between devices with their start and end apart: 3, of which 1 were waited for; matrix products, arithmetic and copies ran while one was open for 0% of the time, Pallas kernels for 4%

profile of v7, /device:TPU:0, one launch (start us, length us, event | category | flops | bytes accessed | tf_op | source)
XLA Modules:
  0.0 417.3 jit_solution(3849574288684178018)
XLA Ops:
  0.6 0.0 copy-start
  0.7 0.0 copy-start.1
  1.4 0.7 dynamic-slice_multiply_fusion
  2.2 0.1 add_compare_fusion
  2.3 0.1 lt.30
  2.3 0.0 copy-start.2
  2.3 33.7 %front.1 = (bf16[4,320,1024]{2,1,0:T(8,128)(2,1)}, bf16[1024,512]{1,0:T(8,128)(2,1)}, bf16[32,1024]{1,0:T(8,128)(2,1)}, bf16[1280,1024]{1,0:T(8,128)(2,1)}, bf16...) custom-call(s32[16]{0:T(128)} %refs_15_.1, ...), custom_call_target="tpu_custom_call" | custom-call | tf_op jit(solution)/shard_map/front/pallas_call | solution.py:254
  36.1 0.0 copy-done.1
  36.1 1.0 bitcast_select_fusion.refs_6_
  37.1 0.9 collective-permute-start.2
  38.0 1.1 collective-permute-start.1
  39.1 0.0 copy-done
  39.1 0.8 constant_dynamic-slice_fusion
  39.9 0.9 collective-permute-start
  40.9 0.0 copy-done.2
  40.9 0.8 copy.25
  41.7 17.8 %attend.1 = (f32[1280,256]{1,0:T(8,128)}, bf16[1280,256]{1,0:T(8,128)(2,1)}, f32[8,8,640]{2,1,0:T(8,128)}) custom-call(s32[16]{0:T(128)} %refs_15_.1, s32[1]{0:T(128)} %copy.26.len_ref.refs_16_, bf16[1280,256]{1,0:T(8,128)(2,1)} %get-tuple-element.53.q_ref.refs_2_, bf16[2560,256]{1,0:T(8,128)(2,1)} %bitcast.27), custom_call_target="tpu_custom_call" | custom-call | tf_op jit(solution)/shard_map/attend/pallas_call | solution.py:516
  59.5 5.9 %collective-permute-done.refs_3_ = bf16[256,1024]{1,0:T(8,128)(2,1)} collective-permute-done((bf16[256,1024]{1,0:T(8,128)(2,1)}, bf16[256,1024]{1,0:T(8,128)(2,1)}, u32[]{:S(2)}, u32[]{:S(2)}) %collective-permute-start) | collective-permute-done | bytes 524320 | tf_op jit(solution)/shard_map/ppermute | solution.py:1127
  65.4 0.0 collective-permute-done.2.refs_8_
  65.4 0.0 collective-permute-done.1.refs_7_
  65.4 104.9 %moe_layer.1 = (f32[320,1024]{1,0:T(8,128)}, bf16[320,1024]{1,0:T(8,128)(2,1)}, bf16[320,1024]{1,0:T(8,128)(2,1)}, bf16[320,1024]{1,0:T(8,128)(2,1)}, bf16[320,1...) custom-call(bf16[4,320,256]{2,1,0:T(8,128)(2,1)} %bitcast.33, ...), custom_call_target="tpu_custom_call" | custom-call | tf_op jit(solution)/shard_map/moe_layer/pallas_call | solution.py:1100
  170.3 217.2 %reduce_grads.1 = (bf16[8,1024,512]{2,1,0:T(8,128)(2,1)}, bf16[8,1024,512]{2,1,0:T(8,128)(2,1)}, bf16[8,512,1024]{2,1,0:T(8,128)(2,1)}, bf16[512,1024]{1,0:T(8,1...) custom-call(bf16[24,2,2,128,512]{4,3,2,1,0:T(8,128)(2,1)} %bitcast.2, ...), custom_call_target="tpu_custom_call" | custom-call | tf_op jit(solution)/shard_map/reduce_grads/pallas_call | solution.py:1695
  387.5 29.6 %widen.1 = (f32[8192,512]{1,0:T(8,128)}, f32[8192,512]{1,0:T(8,128)}, f32[4096,1024]{1,0:T(8,128)}, f32[512,1024]{1,0:T(8,128)}, f32[512,2048]{1,0:T(8,128)}, /*...) custom-call(bf16[8192,512]{1,0:T(8,128)(2,1)} %bitcast.24, ...), custom_call_target="tpu_custom_call" | custom-call | tf_op jit(solution)/shard_map/widen/pallas_call | solution.py:307
Async XLA Ops:
  0.6 38.5 %copy-start = (bf16[512,1024]{1,0:T(8,128)(2,1)S(1)}, bf16[512,1024]{1,0:T(8,128)(2,1)}, u32[]{:S(2)}) copy-start(bf16[512,1024]{1,0:T(8,128)(2,1)} %refs_2_) | copy-start | bytes 3145732
  0.7 35.4 %copy-start.1 = (bf16[1,320,1024]{2,1,0:T(8,128)(2,1)S(1)}, bf16[1,320,1024]{2,1,0:T(8,128)(2,1)}, u32[]{:S(2)}) copy-start(bf16[1,320,1024]{2,1,0:T(8,128)(2,1)} %param.16) | copy-start | bytes 1966084
  2.3 38.5 %copy-start.2 = (s32[1,320,8]{1,2,0:T(8,128)S(1)}, s32[1,320,8]{1,2,0:T(8,128)}, u32[]{:S(2)}) copy-start(s32[1,320,8]{1,2,0:T(8,128)} %param.19) | copy-start | bytes 30724
  37.1 28.3 %collective-permute-start.2 = (bf16[320,1024]{1,0:T(8,128)(2,1)}, bf16[320,1024]{1,0:T(8,128)(2,1)}, u32[]{:S(2)}, u32[]{:S(2)}) collective-permute-start(bf16[320,1024]{1,0:T(8,128)(2,1)} %bitcast_select_fusion.refs_6_), channel_id=1, source_target_pairs={{0,4},{4,0},{2,6},{6,2},{1,5},{5,1},{3,7},{7,3},{8,12},{12,8},{10,... | collective-permute-start | bytes 1966088 | tf_op jit(solution)/shard_map/ppermute | solution.py:1119
  38.0 27.3 %collective-permute-start.1 = (bf16[320,1024]{1,0:T(8,128)(2,1)}, bf16[320,1024]{1,0:T(8,128)(2,1)}, u32[]{:S(2)}, u32[]{:S(2)}) collective-permute-start(bf16[320,1024]{1,0:T(8,128)(2,1)} %bitcast_select_fusion.refs_6_), channel_id=1, source_target_pairs={{0,1},{1,0},{2,3},{3,2},{4,5},{5,4},{6,7},{7,6},{8,9},{9,8},{10,11... | collective-permute-start | bytes 1966088 | tf_op jit(solution)/shard_map/ppermute | solution.py:1127
  39.9 25.4 %collective-permute-start = (bf16[256,1024]{1,0:T(8,128)(2,1)}, bf16[256,1024]{1,0:T(8,128)(2,1)}, u32[]{:S(2)}, u32[]{:S(2)}) collective-permute-start(bf16[256,1024]{1,0:T(8,128)(2,1)} %constant_dynamic-slice_fusion), channel_id=1, source_target_pairs={{0,1},{1,0},{2,3},{3,2},{4,5},{5,4},{6,7},{7,6},{8,9},{9,8},{10,11... | collective-permute-start | bytes 1572872 | tf_op jit(solution)/shard_map/ppermute | solution.py:1127
